TPU v7x, 256 devices: a whole 4x4x8 slice. The times are simulated.
256 devices in a mesh: inst: 8 (over y, x_lo), ax: 16 (over z, core), circ: 2 (over x_hi).
Axes of the slice: x: 4 (x_hi: 2, x_lo: 2; x = x_hi * 2 + x_lo), y: 4, z: 8, core: 2. Of those that a mesh axis runs over, the one named last changes fastest.
Arguments:
- flow_state: float32 [8, 7, 128, 128, 128], P('inst', None, 'ax', 'circ'), may hold values from -2 to 40, as said below
- thinc_flags: int32 [8, 128, 128], P('inst', 'ax', 'circ'), may hold values 0 or 1
Outputs:
- new_state: float32 [8, 7, 128, 128, 128], P('inst', None, 'ax', 'circ')
Inputs may be any that keep to these rules, and one draw needn't show every extreme that they name: `flow_state`: every cell holds a two-phase state with positive partial densities and positive pressure, whose seventh field, the volume fraction, lies between 0.02 and 0.98.
All inputs are finite; a program needn't handle non-finite values. No bound on the sum of `thinc_flags` on one device may be relied on, other than what follows from the above.
Results may differ from a plain program's by a relative error of at most 0.0003.
Values sent between devices are 32-bit elements; how exact they have to be, the bound alone decides.
No kernel may reach another device: no remote copies, remote signals or barrier semaphores. Data moves between devices by JAX's collectives and lax.ppermute only.
A program may use at most 64 MiB of HBM per device.

v0:
```python
import functools
import math

import jax
import jax.numpy as jnp
from jax import lax
from jax.experimental import pallas as pl
from jax.experimental.pallas import tpu as pltpu
from jax.sharding import PartitionSpec as P


G_LIQ = 4.4
P_LIQ = 6.0
G_GAS = 1.4
BETA = 1.6
EPSA = 0.1
ALPHA = 4.0
DIAG0 = 0.016
OMEGA = 1.0
NU_T = 0.25

FIELDS = 7
ORDER = (5, 4, 3, 7, 2, 6, 1)
EDGES = 2 * FIELDS + 3
COEFS = 5
TILE = 8


VMEM = pl.BlockSpec(memory_space=pltpu.VMEM)


def spectral_weights(count):
    table = []
    for k in range(count):
        if k == 0:
            first, second = 0.0, -(count * count + 2) / 12.0
        else:
            sign = 1.0 if k % 2 == 0 else -1.0
            angle = math.pi * k / count
            first = 0.5 * sign * math.cos(angle) / math.sin(angle)
            second = -sign / (2.0 * math.sin(angle) ** 2)
        table.append(OMEGA * first - NU_T * OMEGA * OMEGA * second)
    return table


def core_index():
    return lax.rem(lax.axis_index("ax"), 2)


def call(kernel, outs, *operands, flops=0, scratch=()):
    outs = [jax.ShapeDtypeStruct(shape, jnp.float32) for shape in outs]
    total = sum(x.size * 4 for x in operands) + sum(x.size * 4 for x in outs)
    run = pl.pallas_call(
        kernel,
        out_shape=outs,
        in_specs=[VMEM] * len(operands),
        out_specs=[VMEM] * len(outs),
        scratch_shapes=[pltpu.VMEM(x, jnp.float32) for x in scratch],
        compiler_params=pltpu.CompilerParams(
            vmem_limit_bytes=total + sum(math.prod(x) * 4 for x in scratch) + (2 << 20)
        ),
        cost_estimate=pl.CostEstimate(flops=flops, bytes_accessed=total, transcendentals=0),
    )
    return list(run(*operands))


def slots(count):
    steps = [(dy, dx) for dy in range(count // 2) for dx in range(2)]
    return steps


def route(dy, dx, count):
    ring = count // 2
    return [(i, 2 * ((i // 2 + dy) % ring) + ((i % 2) ^ dx)) for i in range(count)]


def pick_kernel(count, state_ref, flag_ref, *refs):
    outs = refs[:count]
    edge_ref, held_ref, sems = refs[count:]
    fields, _, rows = state_ref.shape[1:4]
    index = lax.axis_index("inst")
    ring = count // 2
    places = [
        2 * lax.rem(index // 2 + dy, ring) + lax.rem(lax.rem(index, 2) + dx, 2)
        for dy, dx in slots(count)
    ]
    copies = [
        pltpu.make_async_copy(state_ref.at[0, :, place], out, sems.at[k])
        for k, (place, out) in enumerate(zip(places, outs))
    ]
    for copy in copies:
        copy.start()
    flag_copy = pltpu.make_async_copy(flag_ref, held_ref, sems.at[count])
    flag_copy.start()
    flag_copy.wait()
    flags = (held_ref[0] > 0).astype(jnp.float32)
    edge_ref[EDGES - 1] = jnp.broadcast_to(flags[:, 0:1], edge_ref.shape[1:])
    for copy, place, out in zip(copies, places, outs):
        copy.wait()
        row = pl.ds(place, 1)
        for f in range(fields):
            edge_ref[f, row] = out[f, 0:1]
            edge_ref[fields + f, row] = out[f, rows - 1 : rows]
        edge_ref[2 * fields, row] = out[fields - 1, 1:2]
        edge_ref[2 * fields + 1, row] = out[fields - 1, rows - 2 : rows - 1]


def pick(state, flags, count):
    _, fields, planes, rows, lanes = state.shape
    shapes = [(fields, rows, lanes)] * count + [(EDGES, planes, lanes)]
    return pl.pallas_call(
        functools.partial(pick_kernel, count),
        out_shape=[jax.ShapeDtypeStruct(x, jnp.float32) for x in shapes],
        in_specs=[pl.BlockSpec(memory_space=pltpu.HBM)] * 2,
        out_specs=[VMEM] * len(shapes),
        scratch_shapes=[
            pltpu.VMEM(flags.shape, flags.dtype),
            pltpu.SemaphoreType.DMA((count + 1,)),
        ],
        compiler_params=pltpu.CompilerParams(vmem_limit_bytes=state.size * 4 + (3 << 20)),
        cost_estimate=pl.CostEstimate(flops=0, bytes_accessed=state.size * 8, transcendentals=0),
    )(*(pltpu.with_memory_space_constraint(x, pltpu.HBM) for x in (state, flags)))


def mixing(count, parity):
    weights = spectral_weights(count)
    table = []
    for shift in (0, 1 - 2 * parity, 2 * parity - 1):
        g = [weights[(2 * a + shift) % count] for a in range(4)]
        table += [0.5 * (g[0] + g[2]), 0.5 * (g[1] + g[3])]
        table += [0.5 * (g[0] - g[2]), 0.5 * (g[1] - g[3])]
    return table


def spectral_kernel(*refs):
    count = len(refs) // 2
    ins, outs = refs[:count], refs[count:]
    fields, rows, _ = ins[0].shape
    tiles = rows // TILE
    first = lax.rem(lax.axis_index("inst"), 2) == 0
    mix = [
        jnp.where(first, jnp.float32(a), jnp.float32(b))
        for a, b in zip(mixing(count, 0), mixing(count, 1))
    ]

    def step(index, _):
        f = index // tiles
        span = pl.ds(pl.multiple_of((index % tiles) * TILE, TILE), TILE)
        parts = []
        for dx in range(2):
            u = [ins[2 * dy + dx][f, span] for dy in range(4)]
            parts.append((u[0] + u[2], u[1] + u[3], u[0] - u[2], u[1] - u[3]))
        for ex in range(2):
            even, odd, even_next, odd_next = 0.0, 0.0, 0.0, 0.0
            for dx in range(2):
                kind = 0 if ex == dx else (1 if ex else 2)
                e0, e1, o0, o1 = mix[4 * kind : 4 * kind + 4]
                s0, s1, d0, d1 = parts[dx]
                even = even + (e0 * s0 + e1 * s1)
                odd = odd + (o0 * d0 + o1 * d1)
                even_next = even_next + (e1 * s0 + e0 * s1)
                odd_next = odd_next + (o1 * d0 - o0 * d1)
            outs[ex][f, span] = even + odd
            outs[4 + ex][f, span] = even - odd
            outs[2 + ex][f, span] = even_next + odd_next
            outs[6 + ex][f, span] = even_next - odd_next
        return 0

    lax.fori_loop(0, fields * tiles, step, 0)


def primitives(cells):
    density = cells[0] + cells[1]
    inverse = 1.0 / density
    vel_ax = cells[2] * inverse
    vel_circ = cells[3] * inverse
    vel_rad = cells[4] * inverse
    fraction = cells[6]
    gamma_term = fraction / (G_LIQ - 1.0) + (1.0 - fraction) / (G_GAS - 1.0)
    stiff_term = fraction * (G_LIQ * P_LIQ / (G_LIQ - 1.0))
    kinetic = 0.5 * density * (vel_ax * vel_ax + vel_circ * vel_circ + vel_rad * vel_rad)
    gamma_inv = 1.0 / gamma_term
    pressure = (cells[5] - kinetic - stiff_term) * gamma_inv
    sound_speed = jnp.sqrt(((1.0 + gamma_inv) * pressure + stiff_term * gamma_inv) * inverse)
    return vel_ax, vel_circ, pressure, sound_speed


def sharpen(lower_val, centre, upper_val, offset):
    average = 0.5 * (lower_val + upper_val)
    difference = upper_val - lower_val
    steepness = 2.0 * (centre - average) / (jnp.abs(difference) + EPSA)
    return average + 0.5 * difference * jnp.tanh(BETA * (steepness + offset))


def flux_kernel(
    state_ref, halo_ref, flag_ref, res_ref, coup_ref, inv_ref, v_ref, w_ref, keep_ref, send_ref
):
    planes = state_ref.shape[2]
    rows = state_ref.shape[3]
    last = planes - 1

    def plane(i, _):
        row = pl.ds(i, 1)
        quad = (TILE // 2, state_ref.shape[4])
        cells = []
        for f in range(FIELDS):
            upper, lower = halo_ref[f, row], halo_ref[FIELDS + f, row]
            if f < FIELDS - 1:
                edge = [jnp.broadcast_to(upper, quad), jnp.broadcast_to(lower, quad)]
            else:
                next_upper = halo_ref[2 * FIELDS, row]
                next_lower = halo_ref[2 * FIELDS + 1, row]
                edge = [upper] + [next_upper] * 3 + [next_lower] * 3 + [lower]
            cells.append(jnp.concatenate([state_ref[0, f, i]] + edge, axis=0))
        edge = jnp.broadcast_to(halo_ref[EDGES - 1, row], (TILE, state_ref.shape[4]))
        flags = jnp.concatenate([flag_ref[i], edge], axis=0)
        total = rows + TILE

        def below(x, by=1):
            return pltpu.roll(x, by, 0)

        def above(x):
            return pltpu.roll(x, total - 1, 0)

        vel_ax, vel_circ, pressure, sound = primitives(cells)
        coup_ref[i] = -ALPHA * (jnp.abs(vel_ax) + sound)[:rows]
        wave = jnp.abs(vel_circ) + sound
        half_speed = 0.5 * jnp.maximum(below(wave), wave)
        fraction = cells[6]
        back1 = below(fraction)
        sharp_left = sharpen(below(fraction, 2), back1, fraction, 1.0)
        sharp_right = sharpen(back1, fraction, above(fraction), -1.0)
        flagged = flags > 0.5
        frac_left = jnp.where(flagged, sharp_left, back1)
        frac_right = jnp.where(flagged, sharp_right, fraction)
        for f in range(FIELDS):
            if f < 6:
                flux = cells[f] * vel_circ
                if f == 3:
                    flux = flux + pressure
                elif f == 5:
                    flux = flux + pressure * vel_circ
                mean = 0.5 * (below(flux) + flux)
                jump = cells[f] - below(cells[f])
            else:
                mean = 0.5 * (frac_left * below(vel_circ) + frac_right * vel_circ)
                jump = frac_right - frac_left
            face = mean - half_speed * jump
            res_ref[i, f] = (above(face) - face)[:rows]
        return 0

    lax.fori_loop(0, planes, plane, 0)

    core = core_index()
    tiles = rows // TILE // 2
    for target_ref, side in ((keep_ref, core), (send_ref, 1 - core)):

        def factor(t, _, target_ref=target_ref, side=side):
            span = pl.ds(pl.multiple_of((side * tiles + t) * TILE, TILE), TILE)
            place = pl.ds(pl.multiple_of(t * TILE, TILE), TILE)
            coup = [coup_ref[i, span] for i in range(planes)]
            inv, ratio, v = [], [], []
            for i in range(last):
                pivot = DIAG0 - 2.0 * coup[i]
                if i:
                    pivot = pivot - coup[i] * ratio[-1]
                inv.append(1.0 / pivot)
                ratio.append(coup[i] * inv[-1])
                v.append(inv[-1] if i == 0 else -(ratio[-1] * v[-1]))
                inv_ref[i, span] = inv[-1]
            v_next, w_next = v[-1], inv[-1]
            v_last, w_last = v_next * coup[0], w_next * coup[last - 1]
            for i in range(last - 1, -1, -1):
                if i < last - 1:
                    v_next = v[i] - ratio[i] * v_next
                    w_next = -(ratio[i] * w_next)
                v_first, w_first = v_next * coup[0], w_next * coup[last - 1]
                v_ref[i, span] = v_first
                w_ref[i, span] = w_first
            sep = coup[last]
            target_ref[0, place] = -(sep * v_last)
            target_ref[1, place] = DIAG0 - 2.0 * sep - sep * w_last
            target_ref[2, place] = sep
            target_ref[3, place] = v_first
            target_ref[4, place] = w_first
            return 0

        lax.fori_loop(0, tiles, factor, 0)


def pair_kernel(keep_ref, got_ref, pair_ref, raw_ref, ends_ref):
    lower_core = core_index() == 0
    lower_a, diag_a, sep_a, v_a, w_a = (
        jnp.where(lower_core, keep_ref[k], got_ref[k]) for k in range(COEFS)
    )
    lower_b, diag_b, sep_b, v_b, w_b = (
        jnp.where(lower_core, got_ref[k], keep_ref[k]) for k in range(COEFS)
    )
    inv = 1.0 / (diag_a - sep_a * v_b)
    v = inv * lower_a
    w = -(inv * sep_a * w_b)
    for k, x in enumerate((inv, sep_a, w_a, lower_b, v, w)):
        pair_ref[k] = x
    raw_ref[0] = diag_b - lower_b * w
    raw_ref[1] = -(lower_b * v)
    raw_ref[2] = sep_b
    ends_ref[0] = v_a - w_a * v
    ends_ref[1] = -(w_a * w)


def link_kernel(raw_ref, ends_ref, link_ref, edge_ref):
    sep = raw_ref[2]
    scale = 1.0 / (raw_ref[0] - sep * ends_ref[0])
    link_ref[0] = scale
    link_ref[1] = raw_ref[1] * scale
    link_ref[2] = -(sep * ends_ref[1]) * scale
    edge_ref[0] = sep * scale


def join_kernel(link_ref, edge_ref, out_ref):
    for k in range(3):
        out_ref[k] = link_ref[k]
    out_ref[3] = edge_ref[0]


def half_of(mine):
    core = core_index()
    return core if mine else 1 - core


def sweep_kernel(mine, res_ref, coup_ref, inv_ref, *refs):
    count = len(refs) - 3
    specs = refs[:count]
    y_ref, target_ref, right_ref = refs[count:]
    planes, fields, rows, _ = res_ref.shape
    last = planes - 1
    tiles = rows // TILE // 2
    side = half_of(mine)
    index = lax.axis_index("inst")
    ring = count // 2
    places = [
        2 * lax.rem(index // 2 + ring - dy, ring) + lax.rem(lax.rem(index, 2) + dx, 2)
        for dy, dx in slots(count)
    ]

    def step(t, _):
        span = pl.ds(pl.multiple_of((side * tiles + t) * TILE, TILE), TILE)
        place = pl.ds(pl.multiple_of(t * TILE, TILE), TILE)
        for f in range(fields):
            for i, spec_ref in zip(places, specs):
                right_ref[f, i] = -(res_ref[i, f, span] + spec_ref[f, span])
        coup = [coup_ref[i, span] for i in range(planes)]
        inv = [inv_ref[i, span] for i in range(last)]
        ratio = [coup[i] * inv[i] for i in range(last)]
        for f in range(fields):
            value = []
            for i in range(last):
                right = right_ref[f, i]
                if i:
                    right = right - coup[i] * value[-1]
                value.append(right * inv[i])
            y = value[-1]
            y_last = y
            y_ref[last - 1, f, place] = y
            for i in range(last - 2, -1, -1):
                y = value[i] - ratio[i] * y
                y_ref[i, f, place] = y
            target_ref[f, place] = y
            target_ref[fields + f, place] = right_ref[f, last] - coup[last] * y_last
        return 0

    lax.fori_loop(0, tiles, step, 0)


def merge_kernel(keep_ref, got_ref, pair_ref, link_ref, inner_ref, out_ref):
    fields = inner_ref.shape[0]
    rows = inner_ref.shape[1]
    lower_core = core_index() == 0

    def step(t, _):
        span = pl.ds(pl.multiple_of(t * TILE, TILE), TILE)
        inv, sep_a, first_a, lower_b = (pair_ref[k, span] for k in range(4))
        scale, lower, upper, edge = (link_ref[k, span] for k in range(4))
        for f in range(fields):
            keep_y, got_y = keep_ref[f, span], got_ref[f, span]
            keep_own, got_own = keep_ref[fields + f, span], got_ref[fields + f, span]
            y_a = jnp.where(lower_core, keep_y, got_y)
            y_b = jnp.where(lower_core, got_y, keep_y)
            own_a = jnp.where(lower_core, keep_own, got_own)
            own_b = jnp.where(lower_core, got_own, keep_own)
            inner = inv * (own_a - sep_a * y_b)
            inner_ref[f, span] = inner
            for k, x in (
                (f, scale * (own_b - lower_b * inner)),
                (fields + f, edge * (y_a - first_a * inner)),
            ):
                out_ref[2 * t, k] = x[0:4]
                out_ref[2 * t + 1, k] = x[4:8]
        for k, x in ((2 * fields, lower), (2 * fields + 1, upper)):
            out_ref[2 * t, k] = x[0:4]
            out_ref[2 * t + 1, k] = x[4:8]
        return 0

    lax.fori_loop(0, rows // TILE, step, 0)


def reduced_kernel(rhs_ref, out_ref):
    count = rhs_ref.shape[0]
    fields = out_ref.shape[1] // 2
    ratio = []
    values = []
    for p in range(count):
        lower, upper = rhs_ref[p, 2 * fields], rhs_ref[p, 2 * fields + 1]
        more = p + 1 < count
        inv = 1.0 / (1.0 - lower * ratio[-1]) if p else jnp.ones_like(lower)
        ratio.append(upper * inv)
        row = []
        for f in range(fields):
            right = rhs_ref[p, f]
            if more:
                right = right - rhs_ref[p + 1, fields + f]
            if p:
                right = right - lower * values[-1][f]
            row.append(right * inv)
        values.append(row)
    solved = values[-1]
    for p in range(count - 1, -1, -1):
        if p < count - 1:
            solved = [values[p][f] - ratio[p] * solved[f] for f in range(fields)]
        for f in range(fields):
            out_ref[p, fields + f] = solved[f]
            if p < count - 1:
                out_ref[p + 1, f] = solved[f]
    for f in range(fields):
        out_ref[0, f] = jnp.zeros_like(solved[f])


def expand_kernel(solved_ref, inner_ref, pair_ref, keep_ref, send_ref):
    fields, rows, _ = inner_ref.shape
    lower_core = core_index() == 0

    def step(t, _):
        span = pl.ds(pl.multiple_of(t * TILE, TILE), TILE)
        v, w = pair_ref[4, span], pair_ref[5, span]
        for f in range(fields):
            prev = jnp.concatenate([solved_ref[2 * t, f], solved_ref[2 * t + 1, f]], axis=0)
            own = jnp.concatenate(
                [solved_ref[2 * t, fields + f], solved_ref[2 * t + 1, fields + f]], axis=0
            )
            inner = inner_ref[f, span] - v * prev - w * own
            keep_ref[f, span] = jnp.where(lower_core, prev, inner)
            keep_ref[fields + f, span] = jnp.where(lower_core, inner, own)
            send_ref[f, span] = jnp.where(lower_core, inner, prev)
            send_ref[fields + f, span] = jnp.where(lower_core, own, inner)
        return 0

    lax.fori_loop(0, rows // TILE, step, 0)


def finish_kernel(mine, state_ref, v_ref, w_ref, y_ref, ends_ref, *refs):
    out_ref, block_ref, sems = refs[-3:]
    fields, planes, rows = state_ref.shape[1:4]
    last = planes - 1
    tiles = rows // TILE // 2
    side = half_of(mine)
    copies = []
    for t in range(tiles):
        span = pl.ds(pl.multiple_of((side * tiles + t) * TILE, TILE), TILE)
        place = pl.ds(t * TILE, TILE)

        def field(f, _, span=span, place=place, t=t):
            prev, own = ends_ref[f, place], ends_ref[fields + f, place]
            for i in range(last):
                delta = y_ref[i, f, place] - v_ref[i, span] * prev - w_ref[i, span] * own
                block_ref[t, f, i] = state_ref[0, f, i, span] + delta
            block_ref[t, f, last] = state_ref[0, f, last, span] + own
            return 0

        lax.fori_loop(0, fields, field, 0)
        copy = pltpu.make_async_copy(
            block_ref.at[t], out_ref.at[0, :, :, span], sems.at[t]
        )
        copy.start()
        copies.append(copy)
    for copy in copies:
        copy.wait()


def finish(mine, state, v, w, y, ends, partial=None):
    fields, planes, rows, lanes = state.shape[1:]
    tiles = rows // TILE // 2
    hbm = pl.BlockSpec(memory_space=pltpu.HBM)
    operands = [state, v, w, y, ends]
    specs = [VMEM] * len(operands)
    aliases = {}
    if partial is not None:
        aliases = {len(operands): 0}
        operands.append(partial)
        specs.append(hbm)
    return pl.pallas_call(
        functools.partial(finish_kernel, mine),
        out_shape=jax.ShapeDtypeStruct(state.shape, jnp.float32),
        in_specs=specs,
        out_specs=hbm,
        scratch_shapes=[
            pltpu.VMEM((tiles, fields, planes, TILE, lanes), jnp.float32),
            pltpu.SemaphoreType.DMA((tiles,)),
        ],
        input_output_aliases=aliases,
        compiler_params=pltpu.CompilerParams(vmem_limit_bytes=state.size * 12),
        cost_estimate=pl.CostEstimate(
            flops=state.size * 2, bytes_accessed=state.size * 6, transcendentals=0
        ),
    )(*operands)


def flux_parts(state, halo, flag_cells):
    fields, planes, rows, lanes = state.shape[1:]
    grid = (rows, lanes)
    return call(
        flux_kernel,
        [
            (planes, fields) + grid,
            (planes,) + grid,
            (planes - 1,) + grid,
            (planes - 1,) + grid,
            (planes - 1,) + grid,
            (COEFS, rows // 2, lanes),
            (COEFS, rows // 2, lanes),
        ],
        state,
        halo,
        flag_cells,
        flops=state.size * 60,
    )


def exchange(x, axis, groups=None):
    return lax.all_to_all(x, axis, 0, 0, tiled=True, axis_index_groups=groups)


def body(flow_state, thinc_flags):
    own = flow_state[0]
    planes, rows, lanes = own.shape[1:]
    instances = lax.axis_size("inst")
    ax_count = lax.axis_size("ax")
    circ_count = lax.axis_size("circ")
    chips = ax_count // 2
    half = rows // 2
    piece = half // chips

    swap = [(i, i ^ 1) for i in range(ax_count)]
    groups = [list(range(c, ax_count, 2)) for c in range(2)]

    def partner(x):
        return lax.ppermute(x, "ax", swap)

    def neighbour(x, by):
        moves = [(i, i + 2 * by) for i in range(ax_count) if 0 <= i + 2 * by < ax_count]
        return lax.ppermute(x, "ax", moves)

    steps = slots(instances)
    blocks = list(pick(flow_state, thinc_flags, instances))
    edges = blocks.pop()
    halo = lax.ppermute(
        edges, "circ", [(i, (i + 1) % circ_count) for i in range(circ_count)]
    )
    order = ORDER
    for k in order:
        blocks[k] = lax.ppermute(blocks[k], "inst", route(*steps[k], instances))
    flags = (thinc_flags[0] > 0).astype(jnp.float32)
    flag_cells = jnp.broadcast_to(flags[:, :, None], (planes, rows, lanes))

    res, coup, inv, v, w, keep, send = flux_parts(flow_state, halo, flag_cells)

    thin = (half, lanes)
    pair, raw, ends = call(
        pair_kernel, [(6,) + thin, (3,) + thin, (2,) + thin], keep, partner(send)
    )
    blocks, res, ends = lax.optimization_barrier((blocks, res, ends))
    specs = call(spectral_kernel, [blocks[0].shape] * instances, *blocks, flops=own.size * 9)
    for k in order:
        specs[k] = lax.ppermute(specs[k], "inst", route(*steps[k], instances))
    ends = neighbour(ends, -1)
    link, edge = call(link_kernel, [(3,) + thin, (1,) + thin], raw, ends)
    edge = neighbour(edge, 1)
    (link,) = call(join_kernel, [(4,) + thin], link, edge)
    shapes = [(planes - 1, FIELDS, half, lanes), (2 * FIELDS, half, lanes)]
    parts = []
    for mine in (False, True):
        parts.append(
            call(
                functools.partial(sweep_kernel, mine),
                shapes,
                res,
                coup,
                inv,
                *specs,
                flops=own.size * 4,
                scratch=[(FIELDS, planes, TILE, lanes)],
            )
        )
    (y_other, send), (y_mine, keep) = parts
    inner, rhs = call(
        merge_kernel,
        [(FIELDS, half, lanes), (chips, 2 * FIELDS + 2, piece, lanes)],
        keep,
        partner(send),
        pair,
        link,
        flops=send.size * 4,
    )
    rhs = exchange(rhs, "ax", groups)
    (solved,) = call(
        reduced_kernel, [(chips, 2 * FIELDS, piece, lanes)], rhs, flops=rhs.size * 8
    )
    solved = exchange(solved, "ax", groups)
    keep, send = call(
        expand_kernel,
        [(2 * FIELDS, half, lanes)] * 2,
        solved,
        inner,
        pair,
        flops=send.size * 4,
    )
    got = partner(send)
    out = finish(True, flow_state, v, w, y_mine, keep)
    return finish(False, flow_state, v, w, y_other, got, out)


def solution(mesh):
    return jax.shard_map(
        body,
        mesh=mesh,
        in_specs=(P("inst", None, "ax", "circ", None), P("inst", "ax", "circ")),
        out_specs=P("inst", None, "ax", "circ", None),
        check_vma=False,
    )
```

profile of v0, /device:TPU:1, one launch (start us, length us, event | category | flops | bytes accessed | tf_op | source)
XLA Modules:
  0.0 115.1 jit_solution(13647595674289141285)
XLA Ops:
  0.0 1.8 %shard_map.28 = (f32[7,64,128]{2,1,0:T(8,128)S(1)}, f32[7,64,128]{2,1,0:T(8,128)S(1)}, f32[7,64,128]{2,1,0:T(8,128)S(1)}, f32[7,64,128]{2,1,0:T(8,128)S(1)}, f32...) custom-call(f32[1,7,8,64,128]{4,3,2,1,0:T(8,128)} %state_ref.7, ...), custom_call_target="tpu_custom_call" | custom-call | bytes 3670016 | tf_op jit(solution)/shard_map/pallas_call | solution.py:111
  1.8 3.6 %collective-permute-start = (f32[17,8,128]{2,1,0:T(8,128)S(1)}, f32[17,8,128]{2,1,0:T(8,128)S(1)}, u32[]{:S(2)}, u32[]{:S(2)}) collective-permute-start(f32[17,8,128]{2,1,0:T(8,128)S(1)} %get-tuple-element.52), channel_id=1, source_target_pairs={{0,1},{1,0},{2,3},{3,2},{4,5},{5,4},{6,7},{7,6},{8,9},{9,8},{10,11... | collective-permute-start | bytes 208904 | tf_op jit(solution)/shard_map/ppermute | solution.py:565
  5.4 0.3 collective-permute-start.1
  5.8 1.3 %collective-permute-start.2 = (f32[7,64,128]{2,1,0:T(8,128)S(1)}, f32[7,64,128]{2,1,0:T(8,128)S(1)}, u32[]{:S(2)}, u32[]{:S(2)}) collective-permute-start(f32[7,64,128]{2,1,0:T(8,128)S(1)} %get-tuple-element.57), channel_id=1, source_target_pairs={{0,64},{32,96},{64,128},{96,160},{128,192},{160,224},{192,0},{224,... | collective-permute-start | bytes 688136 | tf_op jit(solution)/shard_map/ppermute | solution.py:570
  7.1 0.1 collective-permute-done.halo_ref
  7.1 0.1 broadcast_in_dim.2.flag_ref
  7.3 2.5 %shard_map.29 = (f32[8,7,64,128]{3,2,1,0:T(8,128)S(1)}, f32[8,64,128]{2,1,0:T(8,128)S(1)}, f32[7,64,128]{2,1,0:T(8,128)S(1)}, f32[7,64,128]{2,1,0:T(8,128)S(1)},...) custom-call(f32[1,7,8,64,128]{4,3,2,1,0:T(8,128)S(1)} %copy-done, ...), custom_call_target="tpu_custom_call" | custom-call | flops 27525120 | bytes 5115904 | tf_op jit(solution)/shard_map/pallas_call | solution.py:64
  9.8 4.6 %collective-permute-start.8 = (f32[5,32,128]{2,1,0:T(8,128)S(1)}, f32[5,32,128]{2,1,0:T(8,128)S(1)}, u32[]{:S(2)}, u32[]{:S(2)}) collective-permute-start(f32[5,32,128]{2,1,0:T(8,128)S(1)} %get-tuple-element.65), channel_id=1, source_target_pairs={{0,2},{2,0},{4,6},{6,4},{8,10},{10,8},{12,14},{14,12},{16,18},{18,... | collective-permute-start | bytes 245768 | tf_op jit(solution)/shard_map/ppermute | solution.py:556
  14.3 0.5 collective-permute-start.3
  14.9 2.6 %collective-permute-start.4 = (f32[7,64,128]{2,1,0:T(8,128)S(1)}, f32[7,64,128]{2,1,0:T(8,128)S(1)}, u32[]{:S(2)}, u32[]{:S(2)}) collective-permute-start(f32[7,64,128]{2,1,0:T(8,128)S(1)} %get-tuple-element.59), channel_id=1, source_target_pairs={{0,128},{32,160},{64,192},{96,224},{128,0},{160,32},{192,64},{224,... | collective-permute-start | bytes 688136 | tf_op jit(solution)/shard_map/ppermute | solution.py:570
  17.5 0.0 collective-permute-done.8.got_ref
  17.5 0.0 collective-permute-start.5
  17.5 0.0 collective-permute-done.1.refs_1_
  17.5 3.4 %collective-permute-start.6 = (f32[7,64,128]{2,1,0:T(8,128)S(1)}, f32[7,64,128]{2,1,0:T(8,128)S(1)}, u32[]{:S(2)}, u32[]{:S(2)}) collective-permute-start(f32[7,64,128]{2,1,0:T(8,128)S(1)} %get-tuple-element.61), channel_id=1, source_target_pairs={{0,192},{32,224},{64,0},{96,32},{128,64},{160,96},{192,128},{224,1... | collective-permute-start | bytes 688136 | tf_op jit(solution)/shard_map/ppermute | solution.py:570
  20.9 0.0 collective-permute-done.2.refs_2_
  20.9 0.7 collective-permute-start.7
  21.7 2.2 %collective-permute-done.3.refs_3_ = f32[7,64,128]{2,1,0:T(8,128)S(1)} collective-permute-done((f32[7,64,128]{2,1,0:T(8,128)S(1)}, f32[7,64,128]{2,1,0:T(8,128)S(1)}, u32[]{:S(2)}, u32[]{:S(2)}) %collective-permute-start.3) | collective-permute-done | bytes 229408 | tf_op jit(solution)/shard_map/ppermute | solution.py:570
  23.9 9.9 %collective-permute-done.4.refs_4_ = f32[7,64,128]{2,1,0:T(8,128)S(1)} collective-permute-done((f32[7,64,128]{2,1,0:T(8,128)S(1)}, f32[7,64,128]{2,1,0:T(8,128)S(1)}, u32[]{:S(2)}, u32[]{:S(2)}) %collective-permute-start.4) | collective-permute-done | bytes 229408 | tf_op jit(solution)/shard_map/ppermute | solution.py:570
  33.8 0.0 collective-permute-done.5.refs_5_
  33.8 3.2 %collective-permute-done.6.refs_6_ = f32[7,64,128]{2,1,0:T(8,128)S(1)} collective-permute-done((f32[7,64,128]{2,1,0:T(8,128)S(1)}, f32[7,64,128]{2,1,0:T(8,128)S(1)}, u32[]{:S(2)}, u32[]{:S(2)}) %collective-permute-start.6) | collective-permute-done | bytes 229408 | tf_op jit(solution)/shard_map/ppermute | solution.py:570
  36.9 0.0 collective-permute-done.7.refs_7_
  36.9 1.3 %shard_map.31 = (f32[7,64,128]{2,1,0:T(8,128)S(1)}, f32[7,64,128]{2,1,0:T(8,128)S(1)}, f32[7,64,128]{2,1,0:T(8,128)S(1)}, f32[7,64,128]{2,1,0:T(8,128)S(1)}, f32...) custom-call(f32[7,64,128]{2,1,0:T(8,128)S(1)} %get-tuple-element.70.r, ...), custom_call_target="tpu_custom_call" | custom-call | flops 4128768 | bytes 3670016 | tf_op jit(solution)/shard_map/pallas_call | solution.py:64
  38.2 2.0 %collective-permute-start.9 = (f32[7,64,128]{2,1,0:T(8,128)S(1)}, f32[7,64,128]{2,1,0:T(8,128)S(1)}, u32[]{:S(2)}, u32[]{:S(2)}) collective-permute-start(f32[7,64,128]{2,1,0:T(8,128)S(1)} %get-tuple-element.79), channel_id=1, source_target_pairs={{0,32},{32,0},{64,96},{96,64},{128,160},{160,128},{192,224},{224,1... | collective-permute-start | bytes 688136 | tf_op jit(solution)/shard_map/ppermute | solution.py:583
  40.3 1.1 collective-permute-start.10
  41.4 1.1 collective-permute-start.11
  42.5 2.0 %collective-permute-start.12 = (f32[7,64,128]{2,1,0:T(8,128)S(1)}, f32[7,64,128]{2,1,0:T(8,128)S(1)}, u32[]{:S(2)}, u32[]{:S(2)}) collective-permute-start(f32[7,64,128]{2,1,0:T(8,128)S(1)} %get-tuple-element.82), channel_id=1, source_target_pairs={{0,128},{32,160},{64,192},{96,224},{128,0},{160,32},{192,64},{224,... | collective-permute-start | bytes 688136 | tf_op jit(solution)/shard_map/ppermute | solution.py:583
  44.6 0.9 collective-permute-start.13
  45.5 0.0 collective-permute-done.9.refs_1_
  45.5 3.4 %collective-permute-start.14 = (f32[7,64,128]{2,1,0:T(8,128)S(1)}, f32[7,64,128]{2,1,0:T(8,128)S(1)}, u32[]{:S(2)}, u32[]{:S(2)}) collective-permute-start(f32[7,64,128]{2,1,0:T(8,128)S(1)} %get-tuple-element.84), channel_id=1, source_target_pairs={{0,192},{32,224},{64,0},{96,32},{128,64},{160,96},{192,128},{224,1... | collective-permute-start | bytes 688136 | tf_op jit(solution)/shard_map/ppermute | solution.py:583
  48.9 0.0 collective-permute-done.10.refs_2_
  48.9 8.8 %collective-permute-start.15 = (f32[7,64,128]{2,1,0:T(8,128)S(1)}, f32[7,64,128]{2,1,0:T(8,128)S(1)}, u32[]{:S(2)}, u32[]{:S(2)}) collective-permute-start(f32[7,64,128]{2,1,0:T(8,128)S(1)} %get-tuple-element.85), channel_id=1, source_target_pairs={{0,224},{32,192},{64,32},{96,0},{128,96},{160,64},{192,160},{224,1... | collective-permute-start | bytes 688136 | tf_op jit(solution)/shard_map/ppermute | solution.py:583
  57.7 6.6 %collective-permute-done.12.refs_4_ = f32[7,64,128]{2,1,0:T(8,128)S(1)} collective-permute-done((f32[7,64,128]{2,1,0:T(8,128)S(1)}, f32[7,64,128]{2,1,0:T(8,128)S(1)}, u32[]{:S(2)}, u32[]{:S(2)}) %collective-permute-start.12) | collective-permute-done | bytes 229408 | tf_op jit(solution)/shard_map/ppermute | solution.py:583
  64.3 0.5 shard_map.32
  64.8 2.8 %collective-permute-start.16 = (f32[14,32,128]{2,1,0:T(8,128)S(1)}, f32[14,32,128]{2,1,0:T(8,128)S(1)}, u32[]{:S(2)}, u32[]{:S(2)}) collective-permute-start(f32[14,32,128]{2,1,0:T(8,128)S(1)} %get-tuple-element.88), channel_id=1, source_target_pairs={{0,2},{2,0},{4,6},{6,4},{8,10},{10,8},{12,14},{14,12},{16,18},{18,... | collective-permute-start | bytes 688136 | tf_op jit(solution)/shard_map/ppermute | solution.py:556
  67.6 1.3 %collective-permute-start.17 = (f32[2,32,128]{2,1,0:T(8,128)S(1)}, f32[2,32,128]{2,1,0:T(8,128)S(1)}, u32[]{:S(2)}, u32[]{:S(2)}) collective-permute-start(f32[2,32,128]{2,1,0:T(8,128)S(1)} %get-tuple-element.91), channel_id=1, source_target_pairs={{4,0},{6,2},{8,4},{10,6},{12,8},{14,10},{16,12},{18,14},{20,16},{2... | collective-permute-start | bytes 98312 | tf_op jit(solution)/shard_map/ppermute | solution.py:560
  68.9 3.9 %collective-permute-done.17.ends_ref = f32[2,32,128]{2,1,0:T(8,128)S(1)} collective-permute-done((f32[2,32,128]{2,1,0:T(8,128)S(1)}, f32[2,32,128]{2,1,0:T(8,128)S(1)}, u32[]{:S(2)}, u32[]{:S(2)}) %collective-permute-start.17) | collective-permute-done | bytes 32800 | tf_op jit(solution)/shard_map/ppermute | solution.py:560
  72.8 3.5 %collective-permute-start.18 = (f32[1,32,128]{2,1,0:T(8,128)S(1)}, f32[1,32,128]{2,1,0:T(8,128)S(1)}, u32[]{:S(2)}, u32[]{:S(2)}) collective-permute-start(f32[1,32,128]{2,1,0:T(8,128)S(1)} %get-tuple-element.93), channel_id=1, source_target_pairs={{0,4},{2,6},{4,8},{6,10},{8,12},{10,14},{12,16},{14,18},{16,20},{1... | collective-permute-start | bytes 49160 | tf_op jit(solution)/shard_map/ppermute | solution.py:560
  76.4 0.9 collective-permute-done.18.edge_ref
  77.2 0.5 shard_map.33
  77.8 0.1 shard_map.36
  77.9 18.2 %all_to_all.10.rhs_ref = f32[8,16,4,128]{3,2,1,0:T(4,128)S(1)} all-to-all(f32[8,16,4,128]{3,2,1,0:T(4,128)S(1)} %get-tuple-element.94), channel_id=1, replica_groups={{0,4,8,12,16,20,24,28},{2,6,10,14,18,22,26,30},{1,5,9,13,17,21,25,29},{..., dimensions={0} | all-to-all | bytes 524288 | tf_op jit(solution)/shard_map/all_to_all | solution.py:539
  96.0 0.1 shard_map.37
  96.1 11.4 %all_to_all.11.solved_ref = f32[8,14,4,128]{3,2,1,0:T(4,128)S(1)} all-to-all(f32[8,14,4,128]{3,2,1,0:T(4,128)S(1)} %shard_map.37), channel_id=1, replica_groups={{0,4,8,12,16,20,24,28},{2,6,10,14,18,22,26,30},{1,5,9,13,17,21,25,29},{..., dimensions={0} | all-to-all | bytes 458752 | tf_op jit(solution)/shard_map/all_to_all | solution.py:539
  107.5 0.1 shard_map.38
  107.6 4.9 %collective-permute-start.19 = (f32[14,32,128]{2,1,0:T(8,128)S(1)}, f32[14,32,128]{2,1,0:T(8,128)S(1)}, u32[]{:S(2)}, u32[]{:S(2)}) collective-permute-start(f32[14,32,128]{2,1,0:T(8,128)S(1)} %get-tuple-element.96), channel_id=1, source_target_pairs={{0,2},{2,0},{4,6},{6,4},{8,10},{10,8},{12,14},{14,12},{16,18},{18,... | collective-permute-start | bytes 688136 | tf_op jit(solution)/shard_map/ppermute | solution.py:556
  112.5 1.3 %shard_map.39.refs_0_ = f32[1,7,8,64,128]{4,3,2,1,0:T(8,128)} custom-call(f32[1,7,8,64,128]{4,3,2,1,0:T(8,128)S(1)} %copy-done, f32[7,64,128]{2,1,0:T(8,128)S(1)} %get-tuple-element.53.v_ref, f32[7,64,128]{2,1,0:T(8,128)S(1)} %get-tuple-element.54.w_ref, f32[7,7,32,128]{3,2,1,0:T(8,128)S(1)} %get-tuple-element.97.y_ref, ...), custom_call_target="tpu_custom_call" | custom-call | flops 917504 | bytes 2752512 | tf_op jit(solution)/shard_map/pallas_call | solution.py:500
  113.8 0.0 collective-permute-done.19.ends_ref
  113.8 1.3 %shard_map.40 = f32[1,7,8,64,128]{4,3,2,1,0:T(8,128)} custom-call(f32[1,7,8,64,128]{4,3,2,1,0:T(8,128)S(1)} %copy-done, f32[7,64,128]{2,1,0:T(8,128)S(1)} %get-tuple-element.53.v_ref, f32[7,64,128]{2,1,0:T(8,128)S(1)} %get-tuple-element.54.w_ref, f32[7,7,32,128]{3,2,1,0:T(8,128)S(1)} %get-tuple-element.86.y_ref, ...), custom_call_target="tpu_custom_call", output_to_operand_aliasing={{}: (5, {})} | custom-call | flops 917504 | bytes 2752512 | tf_op jit(solution)/shard_map/pallas_call | solution.py:500
  (13 shorter events, 0.1 us)
Async XLA Ops:
  0.0 7.3 %copy-start = (f32[1,7,8,64,128]{4,3,2,1,0:T(8,128)S(1)}, f32[1,7,8,64,128]{4,3,2,1,0:T(8,128)}, u32[]{:S(2)}) copy-start(f32[1,7,8,64,128]{4,3,2,1,0:T(8,128)} %state_ref.7) | copy-start | bytes 5505028
  0.0 7.0 %copy-start.1 = (s32[1,8,64]{2,1,0:T(8,128)S(1)}, s32[1,8,64]{2,1,0:T(8,128)}, u32[]{:S(2)}) copy-start(s32[1,8,64]{2,1,0:T(8,128)} %flag_ref.1) | copy-start | bytes 6148
  1.8 5.3 %collective-permute-start = (f32[17,8,128]{2,1,0:T(8,128)S(1)}, f32[17,8,128]{2,1,0:T(8,128)S(1)}, u32[]{:S(2)}, u32[]{:S(2)}) collective-permute-start(f32[17,8,128]{2,1,0:T(8,128)S(1)} %get-tuple-element.52), channel_id=1, source_target_pairs={{0,1},{1,0},{2,3},{3,2},{4,5},{5,4},{6,7},{7,6},{8,9},{9,8},{10,11... | collective-permute-start | bytes 208904 | tf_op jit(solution)/shard_map/ppermute | solution.py:565
  5.4 12.1 %collective-permute-start.1 = (f32[7,64,128]{2,1,0:T(8,128)S(1)}, f32[7,64,128]{2,1,0:T(8,128)S(1)}, u32[]{:S(2)}, u32[]{:S(2)}) collective-permute-start(f32[7,64,128]{2,1,0:T(8,128)S(1)} %get-tuple-element.56), channel_id=1, source_target_pairs={{0,32},{32,0},{64,96},{96,64},{128,160},{160,128},{192,224},{224,1... | collective-permute-start | bytes 688136 | tf_op jit(solution)/shard_map/ppermute | solution.py:570
  5.8 15.2 %collective-permute-start.2 = (f32[7,64,128]{2,1,0:T(8,128)S(1)}, f32[7,64,128]{2,1,0:T(8,128)S(1)}, u32[]{:S(2)}, u32[]{:S(2)}) collective-permute-start(f32[7,64,128]{2,1,0:T(8,128)S(1)} %get-tuple-element.57), channel_id=1, source_target_pairs={{0,64},{32,96},{64,128},{96,160},{128,192},{160,224},{192,0},{224,... | collective-permute-start | bytes 688136 | tf_op jit(solution)/shard_map/ppermute | solution.py:570
  9.8 7.7 %collective-permute-start.8 = (f32[5,32,128]{2,1,0:T(8,128)S(1)}, f32[5,32,128]{2,1,0:T(8,128)S(1)}, u32[]{:S(2)}, u32[]{:S(2)}) collective-permute-start(f32[5,32,128]{2,1,0:T(8,128)S(1)} %get-tuple-element.65), channel_id=1, source_target_pairs={{0,2},{2,0},{4,6},{6,4},{8,10},{10,8},{12,14},{14,12},{16,18},{18,... | collective-permute-start | bytes 245768 | tf_op jit(solution)/shard_map/ppermute | solution.py:556
  14.3 9.5 %collective-permute-start.3 = (f32[7,64,128]{2,1,0:T(8,128)S(1)}, f32[7,64,128]{2,1,0:T(8,128)S(1)}, u32[]{:S(2)}, u32[]{:S(2)}) collective-permute-start(f32[7,64,128]{2,1,0:T(8,128)S(1)} %get-tuple-element.58), channel_id=1, source_target_pairs={{0,96},{32,64},{64,160},{96,128},{128,224},{160,192},{192,32},{224... | collective-permute-start | bytes 688136 | tf_op jit(solution)/shard_map/ppermute | solution.py:570
  14.9 18.9 %collective-permute-start.4 = (f32[7,64,128]{2,1,0:T(8,128)S(1)}, f32[7,64,128]{2,1,0:T(8,128)S(1)}, u32[]{:S(2)}, u32[]{:S(2)}) collective-permute-start(f32[7,64,128]{2,1,0:T(8,128)S(1)} %get-tuple-element.59), channel_id=1, source_target_pairs={{0,128},{32,160},{64,192},{96,224},{128,0},{160,32},{192,64},{224,... | collective-permute-start | bytes 688136 | tf_op jit(solution)/shard_map/ppermute | solution.py:570
  17.5 16.3 %collective-permute-start.5 = (f32[7,64,128]{2,1,0:T(8,128)S(1)}, f32[7,64,128]{2,1,0:T(8,128)S(1)}, u32[]{:S(2)}, u32[]{:S(2)}) collective-permute-start(f32[7,64,128]{2,1,0:T(8,128)S(1)} %get-tuple-element.60), channel_id=1, source_target_pairs={{0,160},{32,128},{64,224},{96,192},{128,32},{160,0},{192,96},{224,... | collective-permute-start | bytes 688136 | tf_op jit(solution)/shard_map/ppermute | solution.py:570
  17.5 19.4 %collective-permute-start.6 = (f32[7,64,128]{2,1,0:T(8,128)S(1)}, f32[7,64,128]{2,1,0:T(8,128)S(1)}, u32[]{:S(2)}, u32[]{:S(2)}) collective-permute-start(f32[7,64,128]{2,1,0:T(8,128)S(1)} %get-tuple-element.61), channel_id=1, source_target_pairs={{0,192},{32,224},{64,0},{96,32},{128,64},{160,96},{192,128},{224,1... | collective-permute-start | bytes 688136 | tf_op jit(solution)/shard_map/ppermute | solution.py:570
  20.9 16.0 %collective-permute-start.7 = (f32[7,64,128]{2,1,0:T(8,128)S(1)}, f32[7,64,128]{2,1,0:T(8,128)S(1)}, u32[]{:S(2)}, u32[]{:S(2)}) collective-permute-start(f32[7,64,128]{2,1,0:T(8,128)S(1)} %get-tuple-element.62), channel_id=1, source_target_pairs={{0,224},{32,192},{64,32},{96,0},{128,96},{160,64},{192,160},{224,1... | collective-permute-start | bytes 688136 | tf_op jit(solution)/shard_map/ppermute | solution.py:570
  38.2 7.2 %collective-permute-start.9 = (f32[7,64,128]{2,1,0:T(8,128)S(1)}, f32[7,64,128]{2,1,0:T(8,128)S(1)}, u32[]{:S(2)}, u32[]{:S(2)}) collective-permute-start(f32[7,64,128]{2,1,0:T(8,128)S(1)} %get-tuple-element.79), channel_id=1, source_target_pairs={{0,32},{32,0},{64,96},{96,64},{128,160},{160,128},{192,224},{224,1... | collective-permute-start | bytes 688136 | tf_op jit(solution)/shard_map/ppermute | solution.py:583
  40.3 8.6 %collective-permute-start.10 = (f32[7,64,128]{2,1,0:T(8,128)S(1)}, f32[7,64,128]{2,1,0:T(8,128)S(1)}, u32[]{:S(2)}, u32[]{:S(2)}) collective-permute-start(f32[7,64,128]{2,1,0:T(8,128)S(1)} %get-tuple-element.80), channel_id=1, source_target_pairs={{0,64},{32,96},{64,128},{96,160},{128,192},{160,224},{192,0},{224,... | collective-permute-start | bytes 688136 | tf_op jit(solution)/shard_map/ppermute | solution.py:583
  41.4 16.3 %collective-permute-start.11 = (f32[7,64,128]{2,1,0:T(8,128)S(1)}, f32[7,64,128]{2,1,0:T(8,128)S(1)}, u32[]{:S(2)}, u32[]{:S(2)}) collective-permute-start(f32[7,64,128]{2,1,0:T(8,128)S(1)} %get-tuple-element.81), channel_id=1, source_target_pairs={{0,96},{32,64},{64,160},{96,128},{128,224},{160,192},{192,32},{224... | collective-permute-start | bytes 688136 | tf_op jit(solution)/shard_map/ppermute | solution.py:583
  42.5 21.7 %collective-permute-start.12 = (f32[7,64,128]{2,1,0:T(8,128)S(1)}, f32[7,64,128]{2,1,0:T(8,128)S(1)}, u32[]{:S(2)}, u32[]{:S(2)}) collective-permute-start(f32[7,64,128]{2,1,0:T(8,128)S(1)} %get-tuple-element.82), channel_id=1, source_target_pairs={{0,128},{32,160},{64,192},{96,224},{128,0},{160,32},{192,64},{224,... | collective-permute-start | bytes 688136 | tf_op jit(solution)/shard_map/ppermute | solution.py:583
  44.6 19.7 %collective-permute-start.13 = (f32[7,64,128]{2,1,0:T(8,128)S(1)}, f32[7,64,128]{2,1,0:T(8,128)S(1)}, u32[]{:S(2)}, u32[]{:S(2)}) collective-permute-start(f32[7,64,128]{2,1,0:T(8,128)S(1)} %get-tuple-element.83), channel_id=1, source_target_pairs={{0,160},{32,128},{64,224},{96,192},{128,32},{160,0},{192,96},{224,... | collective-permute-start | bytes 688136 | tf_op jit(solution)/shard_map/ppermute | solution.py:583
  45.5 18.8 %collective-permute-start.14 = (f32[7,64,128]{2,1,0:T(8,128)S(1)}, f32[7,64,128]{2,1,0:T(8,128)S(1)}, u32[]{:S(2)}, u32[]{:S(2)}) collective-permute-start(f32[7,64,128]{2,1,0:T(8,128)S(1)} %get-tuple-element.84), channel_id=1, source_target_pairs={{0,192},{32,224},{64,0},{96,32},{128,64},{160,96},{192,128},{224,1... | collective-permute-start | bytes 688136 | tf_op jit(solution)/shard_map/ppermute | solution.py:583
  48.9 15.4 %collective-permute-start.15 = (f32[7,64,128]{2,1,0:T(8,128)S(1)}, f32[7,64,128]{2,1,0:T(8,128)S(1)}, u32[]{:S(2)}, u32[]{:S(2)}) collective-permute-start(f32[7,64,128]{2,1,0:T(8,128)S(1)} %get-tuple-element.85), channel_id=1, source_target_pairs={{0,224},{32,192},{64,32},{96,0},{128,96},{160,64},{192,160},{224,1... | collective-permute-start | bytes 688136 | tf_op jit(solution)/shard_map/ppermute | solution.py:583
  64.8 12.9 %collective-permute-start.16 = (f32[14,32,128]{2,1,0:T(8,128)S(1)}, f32[14,32,128]{2,1,0:T(8,128)S(1)}, u32[]{:S(2)}, u32[]{:S(2)}) collective-permute-start(f32[14,32,128]{2,1,0:T(8,128)S(1)} %get-tuple-element.88), channel_id=1, source_target_pairs={{0,2},{2,0},{4,6},{6,4},{8,10},{10,8},{12,14},{14,12},{16,18},{18,... | collective-permute-start | bytes 688136 | tf_op jit(solution)/shard_map/ppermute | solution.py:556
  67.6 5.2 %collective-permute-start.17 = (f32[2,32,128]{2,1,0:T(8,128)S(1)}, f32[2,32,128]{2,1,0:T(8,128)S(1)}, u32[]{:S(2)}, u32[]{:S(2)}) collective-permute-start(f32[2,32,128]{2,1,0:T(8,128)S(1)} %get-tuple-element.91), channel_id=1, source_target_pairs={{4,0},{6,2},{8,4},{10,6},{12,8},{14,10},{16,12},{18,14},{20,16},{2... | collective-permute-start | bytes 98312 | tf_op jit(solution)/shard_map/ppermute | solution.py:560
  72.8 4.4 %collective-permute-start.18 = (f32[1,32,128]{2,1,0:T(8,128)S(1)}, f32[1,32,128]{2,1,0:T(8,128)S(1)}, u32[]{:S(2)}, u32[]{:S(2)}) collective-permute-start(f32[1,32,128]{2,1,0:T(8,128)S(1)} %get-tuple-element.93), channel_id=1, source_target_pairs={{0,4},{2,6},{4,8},{6,10},{8,12},{10,14},{12,16},{14,18},{16,20},{1... | collective-permute-start | bytes 49160 | tf_op jit(solution)/shard_map/ppermute | solution.py:560
  107.6 6.2 %collective-permute-start.19 = (f32[14,32,128]{2,1,0:T(8,128)S(1)}, f32[14,32,128]{2,1,0:T(8,128)S(1)}, u32[]{:S(2)}, u32[]{:S(2)}) collective-permute-start(f32[14,32,128]{2,1,0:T(8,128)S(1)} %get-tuple-element.96), channel_id=1, source_target_pairs={{0,2},{2,0},{4,6},{6,4},{8,10},{10,8},{12,14},{14,12},{16,18},{18,... | collective-permute-start | bytes 688136 | tf_op jit(solution)/shard_map/ppermute | solution.py:556
where the time goes:
time: 115 us
  starting transfers between devices  49.1 us (43%)
  blocking collectives  29.5 us (26%)
  waiting for transfers between devices  26.7 us (23%)
  Pallas kernels  9.43 us (8%)
    all_to_all x2, blocking collectives, exchange(): return lax.all_to_all(x, axis, 0, 0, tiled=True, axis_index_groups=groups)  29.5 us
    ppermute x7, starting transfers between devices, body(): specs[k] = lax.ppermute(specs[k], 'inst', route(*steps[k], instances))  19.4 us
    ppermute x7, waiting for transfers between devices, body(): blocks[k] = lax.ppermute(blocks[k], 'inst', route(*steps[k], instances))  15.3 us
    ppermute x3, starting transfers between devices, partner(): return lax.ppermute(x, 'ax', swap)  12.3 us
    ppermute x7, starting transfers between devices, body(): blocks[k] = lax.ppermute(blocks[k], 'inst', route(*steps[k], instances))  8.9 us
    ppermute x7, waiting for transfers between devices, body(): specs[k] = lax.ppermute(specs[k], 'inst', route(*steps[k], instances))  6.57 us
    pallas_call x10, Pallas kernels, call(): return list(run(*operands))  5.12 us
    ppermute x2, starting transfers between devices, neighbour(): return lax.ppermute(x, 'ax', moves)  4.82 us
  transfers between devices with their start and end apart: 20, of which 7 were waited for; matrix products, arithmetic and copies ran while one was open for 0% of the time, Pallas kernels for 4%

commit v1 on v0

--- a/solution.py
+++ b/solution.py
@@ -20,7 +20,7 @@
 NU_T = 0.25
 
 FIELDS = 7
-ORDER = (5, 4, 3, 7, 2, 6, 1)
+ORDER = (4, 5, 3, 7, 1, 2, 6)
 EDGES = 2 * FIELDS + 3
 COEFS = 5
 TILE = 8
@@ -166,7 +166,7 @@
             outs[6 + ex][f, span] = even_next - odd_next
         return 0
 
-    lax.fori_loop(0, fields * tiles, step, 0)
+    lax.fori_loop(0, fields * tiles, step, 0, unroll=4)
 
 
 def primitives(cells):
@@ -463,23 +463,22 @@
     last = planes - 1
     tiles = rows // TILE // 2
     side = half_of(mine)
+    lines = pl.ds(pl.multiple_of(side * (rows // 2), rows // 2), rows // 2)
     copies = []
-    for t in range(tiles):
-        span = pl.ds(pl.multiple_of((side * tiles + t) * TILE, TILE), TILE)
-        place = pl.ds(t * TILE, TILE)
-
-        def field(f, _, span=span, place=place, t=t):
+    for f in range(fields):
+
+        def tile(t, _, f=f):
+            span = pl.ds(pl.multiple_of((side * tiles + t) * TILE, TILE), TILE)
+            place = pl.ds(pl.multiple_of(t * TILE, TILE), TILE)
             prev, own = ends_ref[f, place], ends_ref[fields + f, place]
             for i in range(last):
                 delta = y_ref[i, f, place] - v_ref[i, span] * prev - w_ref[i, span] * own
-                block_ref[t, f, i] = state_ref[0, f, i, span] + delta
-            block_ref[t, f, last] = state_ref[0, f, last, span] + own
+                block_ref[f, i, place] = state_ref[0, f, i, span] + delta
+            block_ref[f, last, place] = state_ref[0, f, last, span] + own
             return 0
 
-        lax.fori_loop(0, fields, field, 0)
-        copy = pltpu.make_async_copy(
-            block_ref.at[t], out_ref.at[0, :, :, span], sems.at[t]
-        )
+        lax.fori_loop(0, tiles, tile, 0)
+        copy = pltpu.make_async_copy(block_ref.at[f], out_ref.at[0, f, :, lines], sems.at[f])
         copy.start()
         copies.append(copy)
     for copy in copies:
@@ -488,7 +487,6 @@
 
 def finish(mine, state, v, w, y, ends, partial=None):
     fields, planes, rows, lanes = state.shape[1:]
-    tiles = rows // TILE // 2
     hbm = pl.BlockSpec(memory_space=pltpu.HBM)
     operands = [state, v, w, y, ends]
     specs = [VMEM] * len(operands)
@@ -503,8 +501,8 @@
         in_specs=specs,
         out_specs=hbm,
         scratch_shapes=[
-            pltpu.VMEM((tiles, fields, planes, TILE, lanes), jnp.float32),
-            pltpu.SemaphoreType.DMA((tiles,)),
+            pltpu.VMEM((fields, planes, rows // 2, lanes), jnp.float32),
+            pltpu.SemaphoreType.DMA((fields,)),
         ],
         input_output_aliases=aliases,
         compiler_params=pltpu.CompilerParams(vmem_limit_bytes=state.size * 12),

time: 115 us -> 115 us (level)
  no operation moved by 1% of the time
where the time goes in v1:
time: 115 us
  starting transfers between devices  49.1 us (43%)
  blocking collectives  29.5 us (26%)
  waiting for transfers between devices  26.7 us (23%)
  Pallas kernels  9 us (8%)
    all_to_all x2, blocking collectives, exchange(): return lax.all_to_all(x, axis, 0, 0, tiled=True, axis_index_groups=groups)  29.5 us
    ppermute x7, starting transfers between devices, body(): specs[k] = lax.ppermute(specs[k], 'inst', route(*steps[k], instances))  19.4 us
    ppermute x7, waiting for transfers between devices, body(): blocks[k] = lax.ppermute(blocks[k], 'inst', route(*steps[k], instances))  15.3 us
    ppermute x3, starting transfers between devices, partner(): return lax.ppermute(x, 'ax', swap)  12.3 us
    ppermute x7, starting transfers between devices, body(): blocks[k] = lax.ppermute(blocks[k], 'inst', route(*steps[k], instances))  8.9 us
    ppermute x7, waiting for transfers between devices, body(): specs[k] = lax.ppermute(specs[k], 'inst', route(*steps[k], instances))  6.57 us
    ppermute x2, starting transfers between devices, neighbour(): return lax.ppermute(x, 'ax', moves)  4.82 us
    ppermute x2, waiting for transfers between devices, neighbour(): return lax.ppermute(x, 'ax', moves)  4.74 us
  transfers between devices with their start and end apart: 20, of which 7 were waited for; matrix products, arithmetic and copies ran while one was open for 0% of the time, Pallas kernels for 4%

profile of v1, /device:TPU:1, one launch (start us, length us, event | category | flops | bytes accessed | tf_op | source)
XLA Modules:
  0.0 114.6 jit_solution(3130914128311753608)
XLA Ops:
  0.0 1.8 %shard_map.28 = (f32[7,64,128]{2,1,0:T(8,128)S(1)}, f32[7,64,128]{2,1,0:T(8,128)S(1)}, f32[7,64,128]{2,1,0:T(8,128)S(1)}, f32[7,64,128]{2,1,0:T(8,128)S(1)}, f32...) custom-call(f32[1,7,8,64,128]{4,3,2,1,0:T(8,128)} %state_ref.7, ...), custom_call_target="tpu_custom_call" | custom-call | bytes 3670016 | tf_op jit(solution)/shard_map/pallas_call | solution.py:111
  1.8 3.6 %collective-permute-start = (f32[17,8,128]{2,1,0:T(8,128)S(1)}, f32[17,8,128]{2,1,0:T(8,128)S(1)}, u32[]{:S(2)}, u32[]{:S(2)}) collective-permute-start(f32[17,8,128]{2,1,0:T(8,128)S(1)} %get-tuple-element.52), channel_id=1, source_target_pairs={{0,1},{1,0},{2,3},{3,2},{4,5},{5,4},{6,7},{7,6},{8,9},{9,8},{10,11... | collective-permute-start | bytes 208904 | tf_op jit(solution)/shard_map/ppermute | solution.py:563
  5.4 0.3 collective-permute-start.1
  5.8 1.3 %collective-permute-start.2 = (f32[7,64,128]{2,1,0:T(8,128)S(1)}, f32[7,64,128]{2,1,0:T(8,128)S(1)}, u32[]{:S(2)}, u32[]{:S(2)}) collective-permute-start(f32[7,64,128]{2,1,0:T(8,128)S(1)} %get-tuple-element.57), channel_id=1, source_target_pairs={{0,64},{32,96},{64,128},{96,160},{128,192},{160,224},{192,0},{224,... | collective-permute-start | bytes 688136 | tf_op jit(solution)/shard_map/ppermute | solution.py:568
  7.1 0.1 collective-permute-done.halo_ref
  7.1 0.1 broadcast_in_dim.2.flag_ref
  7.3 2.5 %shard_map.29 = (f32[8,7,64,128]{3,2,1,0:T(8,128)S(1)}, f32[8,64,128]{2,1,0:T(8,128)S(1)}, f32[7,64,128]{2,1,0:T(8,128)S(1)}, f32[7,64,128]{2,1,0:T(8,128)S(1)},...) custom-call(f32[1,7,8,64,128]{4,3,2,1,0:T(8,128)S(1)} %copy-done, ...), custom_call_target="tpu_custom_call" | custom-call | flops 27525120 | bytes 5115904 | tf_op jit(solution)/shard_map/pallas_call | solution.py:64
  9.8 4.6 %collective-permute-start.8 = (f32[5,32,128]{2,1,0:T(8,128)S(1)}, f32[5,32,128]{2,1,0:T(8,128)S(1)}, u32[]{:S(2)}, u32[]{:S(2)}) collective-permute-start(f32[5,32,128]{2,1,0:T(8,128)S(1)} %get-tuple-element.65), channel_id=1, source_target_pairs={{0,2},{2,0},{4,6},{6,4},{8,10},{10,8},{12,14},{14,12},{16,18},{18,... | collective-permute-start | bytes 245768 | tf_op jit(solution)/shard_map/ppermute | solution.py:554
  14.3 0.5 collective-permute-start.3
  14.9 2.6 %collective-permute-start.4 = (f32[7,64,128]{2,1,0:T(8,128)S(1)}, f32[7,64,128]{2,1,0:T(8,128)S(1)}, u32[]{:S(2)}, u32[]{:S(2)}) collective-permute-start(f32[7,64,128]{2,1,0:T(8,128)S(1)} %get-tuple-element.59), channel_id=1, source_target_pairs={{0,128},{32,160},{64,192},{96,224},{128,0},{160,32},{192,64},{224,... | collective-permute-start | bytes 688136 | tf_op jit(solution)/shard_map/ppermute | solution.py:568
  17.5 0.0 collective-permute-done.8.got_ref
  17.5 0.0 collective-permute-start.5
  17.5 0.0 collective-permute-done.1.refs_1_
  17.5 3.4 %collective-permute-start.6 = (f32[7,64,128]{2,1,0:T(8,128)S(1)}, f32[7,64,128]{2,1,0:T(8,128)S(1)}, u32[]{:S(2)}, u32[]{:S(2)}) collective-permute-start(f32[7,64,128]{2,1,0:T(8,128)S(1)} %get-tuple-element.61), channel_id=1, source_target_pairs={{0,192},{32,224},{64,0},{96,32},{128,64},{160,96},{192,128},{224,1... | collective-permute-start | bytes 688136 | tf_op jit(solution)/shard_map/ppermute | solution.py:568
  20.9 0.0 collective-permute-done.2.refs_2_
  20.9 0.7 collective-permute-start.7
  21.7 2.2 %collective-permute-done.3.refs_3_ = f32[7,64,128]{2,1,0:T(8,128)S(1)} collective-permute-done((f32[7,64,128]{2,1,0:T(8,128)S(1)}, f32[7,64,128]{2,1,0:T(8,128)S(1)}, u32[]{:S(2)}, u32[]{:S(2)}) %collective-permute-start.3) | collective-permute-done | bytes 229408 | tf_op jit(solution)/shard_map/ppermute | solution.py:568
  23.9 9.9 %collective-permute-done.4.refs_4_ = f32[7,64,128]{2,1,0:T(8,128)S(1)} collective-permute-done((f32[7,64,128]{2,1,0:T(8,128)S(1)}, f32[7,64,128]{2,1,0:T(8,128)S(1)}, u32[]{:S(2)}, u32[]{:S(2)}) %collective-permute-start.4) | collective-permute-done | bytes 229408 | tf_op jit(solution)/shard_map/ppermute | solution.py:568
  33.8 0.0 collective-permute-done.5.refs_5_
  33.8 3.2 %collective-permute-done.6.refs_6_ = f32[7,64,128]{2,1,0:T(8,128)S(1)} collective-permute-done((f32[7,64,128]{2,1,0:T(8,128)S(1)}, f32[7,64,128]{2,1,0:T(8,128)S(1)}, u32[]{:S(2)}, u32[]{:S(2)}) %collective-permute-start.6) | collective-permute-done | bytes 229408 | tf_op jit(solution)/shard_map/ppermute | solution.py:568
  36.9 0.0 collective-permute-done.7.refs_7_
  36.9 0.8 shard_map.31
  37.8 2.0 %collective-permute-start.9 = (f32[7,64,128]{2,1,0:T(8,128)S(1)}, f32[7,64,128]{2,1,0:T(8,128)S(1)}, u32[]{:S(2)}, u32[]{:S(2)}) collective-permute-start(f32[7,64,128]{2,1,0:T(8,128)S(1)} %get-tuple-element.79), channel_id=1, source_target_pairs={{0,32},{32,0},{64,96},{96,64},{128,160},{160,128},{192,224},{224,1... | collective-permute-start | bytes 688136 | tf_op jit(solution)/shard_map/ppermute | solution.py:581
  39.8 1.1 collective-permute-start.10
  41.0 1.1 collective-permute-start.11
  42.0 2.0 %collective-permute-start.12 = (f32[7,64,128]{2,1,0:T(8,128)S(1)}, f32[7,64,128]{2,1,0:T(8,128)S(1)}, u32[]{:S(2)}, u32[]{:S(2)}) collective-permute-start(f32[7,64,128]{2,1,0:T(8,128)S(1)} %get-tuple-element.82), channel_id=1, source_target_pairs={{0,128},{32,160},{64,192},{96,224},{128,0},{160,32},{192,64},{224,... | collective-permute-start | bytes 688136 | tf_op jit(solution)/shard_map/ppermute | solution.py:581
  44.1 0.9 collective-permute-start.13
  45.0 0.0 collective-permute-done.9.refs_1_
  45.0 3.4 %collective-permute-start.14 = (f32[7,64,128]{2,1,0:T(8,128)S(1)}, f32[7,64,128]{2,1,0:T(8,128)S(1)}, u32[]{:S(2)}, u32[]{:S(2)}) collective-permute-start(f32[7,64,128]{2,1,0:T(8,128)S(1)} %get-tuple-element.84), channel_id=1, source_target_pairs={{0,192},{32,224},{64,0},{96,32},{128,64},{160,96},{192,128},{224,1... | collective-permute-start | bytes 688136 | tf_op jit(solution)/shard_map/ppermute | solution.py:581
  48.4 0.0 collective-permute-done.10.refs_2_
  48.4 8.8 %collective-permute-start.15 = (f32[7,64,128]{2,1,0:T(8,128)S(1)}, f32[7,64,128]{2,1,0:T(8,128)S(1)}, u32[]{:S(2)}, u32[]{:S(2)}) collective-permute-start(f32[7,64,128]{2,1,0:T(8,128)S(1)} %get-tuple-element.85), channel_id=1, source_target_pairs={{0,224},{32,192},{64,32},{96,0},{128,96},{160,64},{192,160},{224,1... | collective-permute-start | bytes 688136 | tf_op jit(solution)/shard_map/ppermute | solution.py:581
  57.2 6.6 %collective-permute-done.12.refs_4_ = f32[7,64,128]{2,1,0:T(8,128)S(1)} collective-permute-done((f32[7,64,128]{2,1,0:T(8,128)S(1)}, f32[7,64,128]{2,1,0:T(8,128)S(1)}, u32[]{:S(2)}, u32[]{:S(2)}) %collective-permute-start.12) | collective-permute-done | bytes 229408 | tf_op jit(solution)/shard_map/ppermute | solution.py:581
  63.8 0.0 collective-permute-done.15.refs_7_
  63.8 0.5 shard_map.32
  64.3 2.8 %collective-permute-start.16 = (f32[14,32,128]{2,1,0:T(8,128)S(1)}, f32[14,32,128]{2,1,0:T(8,128)S(1)}, u32[]{:S(2)}, u32[]{:S(2)}) collective-permute-start(f32[14,32,128]{2,1,0:T(8,128)S(1)} %get-tuple-element.88), channel_id=1, source_target_pairs={{0,2},{2,0},{4,6},{6,4},{8,10},{10,8},{12,14},{14,12},{16,18},{18,... | collective-permute-start | bytes 688136 | tf_op jit(solution)/shard_map/ppermute | solution.py:554
  67.2 1.3 %collective-permute-start.17 = (f32[2,32,128]{2,1,0:T(8,128)S(1)}, f32[2,32,128]{2,1,0:T(8,128)S(1)}, u32[]{:S(2)}, u32[]{:S(2)}) collective-permute-start(f32[2,32,128]{2,1,0:T(8,128)S(1)} %get-tuple-element.91), channel_id=1, source_target_pairs={{4,0},{6,2},{8,4},{10,6},{12,8},{14,10},{16,12},{18,14},{20,16},{2... | collective-permute-start | bytes 98312 | tf_op jit(solution)/shard_map/ppermute | solution.py:558
  68.5 3.9 %collective-permute-done.17.ends_ref = f32[2,32,128]{2,1,0:T(8,128)S(1)} collective-permute-done((f32[2,32,128]{2,1,0:T(8,128)S(1)}, f32[2,32,128]{2,1,0:T(8,128)S(1)}, u32[]{:S(2)}, u32[]{:S(2)}) %collective-permute-start.17) | collective-permute-done | bytes 32800 | tf_op jit(solution)/shard_map/ppermute | solution.py:558
  72.4 3.5 %collective-permute-start.18 = (f32[1,32,128]{2,1,0:T(8,128)S(1)}, f32[1,32,128]{2,1,0:T(8,128)S(1)}, u32[]{:S(2)}, u32[]{:S(2)}) collective-permute-start(f32[1,32,128]{2,1,0:T(8,128)S(1)} %get-tuple-element.93), channel_id=1, source_target_pairs={{0,4},{2,6},{4,8},{6,10},{8,12},{10,14},{12,16},{14,18},{16,20},{1... | collective-permute-start | bytes 49160 | tf_op jit(solution)/shard_map/ppermute | solution.py:558
  75.9 0.9 collective-permute-done.18.edge_ref
  76.8 0.5 shard_map.33
  77.3 0.1 shard_map.36
  77.4 18.2 %all_to_all.10.rhs_ref = f32[8,16,4,128]{3,2,1,0:T(4,128)S(1)} all-to-all(f32[8,16,4,128]{3,2,1,0:T(4,128)S(1)} %get-tuple-element.94), channel_id=1, replica_groups={{0,4,8,12,16,20,24,28},{2,6,10,14,18,22,26,30},{1,5,9,13,17,21,25,29},{..., dimensions={0} | all-to-all | bytes 524288 | tf_op jit(solution)/shard_map/all_to_all | solution.py:537
  95.6 0.1 shard_map.37
  95.7 11.4 %all_to_all.11.solved_ref = f32[8,14,4,128]{3,2,1,0:T(4,128)S(1)} all-to-all(f32[8,14,4,128]{3,2,1,0:T(4,128)S(1)} %shard_map.37), channel_id=1, replica_groups={{0,4,8,12,16,20,24,28},{2,6,10,14,18,22,26,30},{1,5,9,13,17,21,25,29},{..., dimensions={0} | all-to-all | bytes 458752 | tf_op jit(solution)/shard_map/all_to_all | solution.py:537
  107.1 0.1 shard_map.38
  107.1 4.9 %collective-permute-start.19 = (f32[14,32,128]{2,1,0:T(8,128)S(1)}, f32[14,32,128]{2,1,0:T(8,128)S(1)}, u32[]{:S(2)}, u32[]{:S(2)}) collective-permute-start(f32[14,32,128]{2,1,0:T(8,128)S(1)} %get-tuple-element.96), channel_id=1, source_target_pairs={{0,2},{2,0},{4,6},{6,4},{8,10},{10,8},{12,14},{14,12},{16,18},{18,... | collective-permute-start | bytes 688136 | tf_op jit(solution)/shard_map/ppermute | solution.py:554
  112.0 1.3 %shard_map.39.refs_0_ = f32[1,7,8,64,128]{4,3,2,1,0:T(8,128)} custom-call(f32[1,7,8,64,128]{4,3,2,1,0:T(8,128)S(1)} %copy-done, f32[7,64,128]{2,1,0:T(8,128)S(1)} %get-tuple-element.53.v_ref, f32[7,64,128]{2,1,0:T(8,128)S(1)} %get-tuple-element.54.w_ref, f32[7,7,32,128]{3,2,1,0:T(8,128)S(1)} %get-tuple-element.97.y_ref, ...), custom_call_target="tpu_custom_call" | custom-call | flops 917504 | bytes 2752512 | tf_op jit(solution)/shard_map/pallas_call | solution.py:498
  113.3 1.3 %shard_map.40 = f32[1,7,8,64,128]{4,3,2,1,0:T(8,128)} custom-call(f32[1,7,8,64,128]{4,3,2,1,0:T(8,128)S(1)} %copy-done, f32[7,64,128]{2,1,0:T(8,128)S(1)} %get-tuple-element.53.v_ref, f32[7,64,128]{2,1,0:T(8,128)S(1)} %get-tuple-element.54.w_ref, f32[7,7,32,128]{3,2,1,0:T(8,128)S(1)} %get-tuple-element.86.y_ref, ...), custom_call_target="tpu_custom_call", output_to_operand_aliasing={{}: (5, {})} | custom-call | flops 917504 | bytes 2752512 | tf_op jit(solution)/shard_map/pallas_call | solution.py:498
  (13 shorter events, 0.1 us)
Async XLA Ops:
  0.0 7.3 %copy-start = (f32[1,7,8,64,128]{4,3,2,1,0:T(8,128)S(1)}, f32[1,7,8,64,128]{4,3,2,1,0:T(8,128)}, u32[]{:S(2)}) copy-start(f32[1,7,8,64,128]{4,3,2,1,0:T(8,128)} %state_ref.7) | copy-start | bytes 5505028
  0.0 7.0 %copy-start.1 = (s32[1,8,64]{2,1,0:T(8,128)S(1)}, s32[1,8,64]{2,1,0:T(8,128)}, u32[]{:S(2)}) copy-start(s32[1,8,64]{2,1,0:T(8,128)} %flag_ref.1) | copy-start | bytes 6148
  1.8 5.3 %collective-permute-start = (f32[17,8,128]{2,1,0:T(8,128)S(1)}, f32[17,8,128]{2,1,0:T(8,128)S(1)}, u32[]{:S(2)}, u32[]{:S(2)}) collective-permute-start(f32[17,8,128]{2,1,0:T(8,128)S(1)} %get-tuple-element.52), channel_id=1, source_target_pairs={{0,1},{1,0},{2,3},{3,2},{4,5},{5,4},{6,7},{7,6},{8,9},{9,8},{10,11... | collective-permute-start | bytes 208904 | tf_op jit(solution)/shard_map/ppermute | solution.py:563
  5.4 12.1 %collective-permute-start.1 = (f32[7,64,128]{2,1,0:T(8,128)S(1)}, f32[7,64,128]{2,1,0:T(8,128)S(1)}, u32[]{:S(2)}, u32[]{:S(2)}) collective-permute-start(f32[7,64,128]{2,1,0:T(8,128)S(1)} %get-tuple-element.56), channel_id=1, source_target_pairs={{0,32},{32,0},{64,96},{96,64},{128,160},{160,128},{192,224},{224,1... | collective-permute-start | bytes 688136 | tf_op jit(solution)/shard_map/ppermute | solution.py:568
  5.8 15.2 %collective-permute-start.2 = (f32[7,64,128]{2,1,0:T(8,128)S(1)}, f32[7,64,128]{2,1,0:T(8,128)S(1)}, u32[]{:S(2)}, u32[]{:S(2)}) collective-permute-start(f32[7,64,128]{2,1,0:T(8,128)S(1)} %get-tuple-element.57), channel_id=1, source_target_pairs={{0,64},{32,96},{64,128},{96,160},{128,192},{160,224},{192,0},{224,... | collective-permute-start | bytes 688136 | tf_op jit(solution)/shard_map/ppermute | solution.py:568
  9.8 7.7 %collective-permute-start.8 = (f32[5,32,128]{2,1,0:T(8,128)S(1)}, f32[5,32,128]{2,1,0:T(8,128)S(1)}, u32[]{:S(2)}, u32[]{:S(2)}) collective-permute-start(f32[5,32,128]{2,1,0:T(8,128)S(1)} %get-tuple-element.65), channel_id=1, source_target_pairs={{0,2},{2,0},{4,6},{6,4},{8,10},{10,8},{12,14},{14,12},{16,18},{18,... | collective-permute-start | bytes 245768 | tf_op jit(solution)/shard_map/ppermute | solution.py:554
  14.3 9.5 %collective-permute-start.3 = (f32[7,64,128]{2,1,0:T(8,128)S(1)}, f32[7,64,128]{2,1,0:T(8,128)S(1)}, u32[]{:S(2)}, u32[]{:S(2)}) collective-permute-start(f32[7,64,128]{2,1,0:T(8,128)S(1)} %get-tuple-element.58), channel_id=1, source_target_pairs={{0,96},{32,64},{64,160},{96,128},{128,224},{160,192},{192,32},{224... | collective-permute-start | bytes 688136 | tf_op jit(solution)/shard_map/ppermute | solution.py:568
  14.9 18.9 %collective-permute-start.4 = (f32[7,64,128]{2,1,0:T(8,128)S(1)}, f32[7,64,128]{2,1,0:T(8,128)S(1)}, u32[]{:S(2)}, u32[]{:S(2)}) collective-permute-start(f32[7,64,128]{2,1,0:T(8,128)S(1)} %get-tuple-element.59), channel_id=1, source_target_pairs={{0,128},{32,160},{64,192},{96,224},{128,0},{160,32},{192,64},{224,... | collective-permute-start | bytes 688136 | tf_op jit(solution)/shard_map/ppermute | solution.py:568
  17.5 16.3 %collective-permute-start.5 = (f32[7,64,128]{2,1,0:T(8,128)S(1)}, f32[7,64,128]{2,1,0:T(8,128)S(1)}, u32[]{:S(2)}, u32[]{:S(2)}) collective-permute-start(f32[7,64,128]{2,1,0:T(8,128)S(1)} %get-tuple-element.60), channel_id=1, source_target_pairs={{0,160},{32,128},{64,224},{96,192},{128,32},{160,0},{192,96},{224,... | collective-permute-start | bytes 688136 | tf_op jit(solution)/shard_map/ppermute | solution.py:568
  17.5 19.4 %collective-permute-start.6 = (f32[7,64,128]{2,1,0:T(8,128)S(1)}, f32[7,64,128]{2,1,0:T(8,128)S(1)}, u32[]{:S(2)}, u32[]{:S(2)}) collective-permute-start(f32[7,64,128]{2,1,0:T(8,128)S(1)} %get-tuple-element.61), channel_id=1, source_target_pairs={{0,192},{32,224},{64,0},{96,32},{128,64},{160,96},{192,128},{224,1... | collective-permute-start | bytes 688136 | tf_op jit(solution)/shard_map/ppermute | solution.py:568
  20.9 16.0 %collective-permute-start.7 = (f32[7,64,128]{2,1,0:T(8,128)S(1)}, f32[7,64,128]{2,1,0:T(8,128)S(1)}, u32[]{:S(2)}, u32[]{:S(2)}) collective-permute-start(f32[7,64,128]{2,1,0:T(8,128)S(1)} %get-tuple-element.62), channel_id=1, source_target_pairs={{0,224},{32,192},{64,32},{96,0},{128,96},{160,64},{192,160},{224,1... | collective-permute-start | bytes 688136 | tf_op jit(solution)/shard_map/ppermute | solution.py:568
  37.8 7.2 %collective-permute-start.9 = (f32[7,64,128]{2,1,0:T(8,128)S(1)}, f32[7,64,128]{2,1,0:T(8,128)S(1)}, u32[]{:S(2)}, u32[]{:S(2)}) collective-permute-start(f32[7,64,128]{2,1,0:T(8,128)S(1)} %get-tuple-element.79), channel_id=1, source_target_pairs={{0,32},{32,0},{64,96},{96,64},{128,160},{160,128},{192,224},{224,1... | collective-permute-start | bytes 688136 | tf_op jit(solution)/shard_map/ppermute | solution.py:581
  39.8 8.6 %collective-permute-start.10 = (f32[7,64,128]{2,1,0:T(8,128)S(1)}, f32[7,64,128]{2,1,0:T(8,128)S(1)}, u32[]{:S(2)}, u32[]{:S(2)}) collective-permute-start(f32[7,64,128]{2,1,0:T(8,128)S(1)} %get-tuple-element.80), channel_id=1, source_target_pairs={{0,64},{32,96},{64,128},{96,160},{128,192},{160,224},{192,0},{224,... | collective-permute-start | bytes 688136 | tf_op jit(solution)/shard_map/ppermute | solution.py:581
  41.0 16.3 %collective-permute-start.11 = (f32[7,64,128]{2,1,0:T(8,128)S(1)}, f32[7,64,128]{2,1,0:T(8,128)S(1)}, u32[]{:S(2)}, u32[]{:S(2)}) collective-permute-start(f32[7,64,128]{2,1,0:T(8,128)S(1)} %get-tuple-element.81), channel_id=1, source_target_pairs={{0,96},{32,64},{64,160},{96,128},{128,224},{160,192},{192,32},{224... | collective-permute-start | bytes 688136 | tf_op jit(solution)/shard_map/ppermute | solution.py:581
  42.0 21.7 %collective-permute-start.12 = (f32[7,64,128]{2,1,0:T(8,128)S(1)}, f32[7,64,128]{2,1,0:T(8,128)S(1)}, u32[]{:S(2)}, u32[]{:S(2)}) collective-permute-start(f32[7,64,128]{2,1,0:T(8,128)S(1)} %get-tuple-element.82), channel_id=1, source_target_pairs={{0,128},{32,160},{64,192},{96,224},{128,0},{160,32},{192,64},{224,... | collective-permute-start | bytes 688136 | tf_op jit(solution)/shard_map/ppermute | solution.py:581
  44.1 19.7 %collective-permute-start.13 = (f32[7,64,128]{2,1,0:T(8,128)S(1)}, f32[7,64,128]{2,1,0:T(8,128)S(1)}, u32[]{:S(2)}, u32[]{:S(2)}) collective-permute-start(f32[7,64,128]{2,1,0:T(8,128)S(1)} %get-tuple-element.83), channel_id=1, source_target_pairs={{0,160},{32,128},{64,224},{96,192},{128,32},{160,0},{192,96},{224,... | collective-permute-start | bytes 688136 | tf_op jit(solution)/shard_map/ppermute | solution.py:581
  45.0 18.8 %collective-permute-start.14 = (f32[7,64,128]{2,1,0:T(8,128)S(1)}, f32[7,64,128]{2,1,0:T(8,128)S(1)}, u32[]{:S(2)}, u32[]{:S(2)}) collective-permute-start(f32[7,64,128]{2,1,0:T(8,128)S(1)} %get-tuple-element.84), channel_id=1, source_target_pairs={{0,192},{32,224},{64,0},{96,32},{128,64},{160,96},{192,128},{224,1... | collective-permute-start | bytes 688136 | tf_op jit(solution)/shard_map/ppermute | solution.py:581
  48.4 15.4 %collective-permute-start.15 = (f32[7,64,128]{2,1,0:T(8,128)S(1)}, f32[7,64,128]{2,1,0:T(8,128)S(1)}, u32[]{:S(2)}, u32[]{:S(2)}) collective-permute-start(f32[7,64,128]{2,1,0:T(8,128)S(1)} %get-tuple-element.85), channel_id=1, source_target_pairs={{0,224},{32,192},{64,32},{96,0},{128,96},{160,64},{192,160},{224,1... | collective-permute-start | bytes 688136 | tf_op jit(solution)/shard_map/ppermute | solution.py:581
  64.3 12.9 %collective-permute-start.16 = (f32[14,32,128]{2,1,0:T(8,128)S(1)}, f32[14,32,128]{2,1,0:T(8,128)S(1)}, u32[]{:S(2)}, u32[]{:S(2)}) collective-permute-start(f32[14,32,128]{2,1,0:T(8,128)S(1)} %get-tuple-element.88), channel_id=1, source_target_pairs={{0,2},{2,0},{4,6},{6,4},{8,10},{10,8},{12,14},{14,12},{16,18},{18,... | collective-permute-start | bytes 688136 | tf_op jit(solution)/shard_map/ppermute | solution.py:554
  67.2 5.2 %collective-permute-start.17 = (f32[2,32,128]{2,1,0:T(8,128)S(1)}, f32[2,32,128]{2,1,0:T(8,128)S(1)}, u32[]{:S(2)}, u32[]{:S(2)}) collective-permute-start(f32[2,32,128]{2,1,0:T(8,128)S(1)} %get-tuple-element.91), channel_id=1, source_target_pairs={{4,0},{6,2},{8,4},{10,6},{12,8},{14,10},{16,12},{18,14},{20,16},{2... | collective-permute-start | bytes 98312 | tf_op jit(solution)/shard_map/ppermute | solution.py:558
  72.4 4.4 %collective-permute-start.18 = (f32[1,32,128]{2,1,0:T(8,128)S(1)}, f32[1,32,128]{2,1,0:T(8,128)S(1)}, u32[]{:S(2)}, u32[]{:S(2)}) collective-permute-start(f32[1,32,128]{2,1,0:T(8,128)S(1)} %get-tuple-element.93), channel_id=1, source_target_pairs={{0,4},{2,6},{4,8},{6,10},{8,12},{10,14},{12,16},{14,18},{16,20},{1... | collective-permute-start | bytes 49160 | tf_op jit(solution)/shard_map/ppermute | solution.py:558
  107.1 6.2 %collective-permute-start.19 = (f32[14,32,128]{2,1,0:T(8,128)S(1)}, f32[14,32,128]{2,1,0:T(8,128)S(1)}, u32[]{:S(2)}, u32[]{:S(2)}) collective-permute-start(f32[14,32,128]{2,1,0:T(8,128)S(1)} %get-tuple-element.96), channel_id=1, source_target_pairs={{0,2},{2,0},{4,6},{6,4},{8,10},{10,8},{12,14},{14,12},{16,18},{18,... | collective-permute-start | bytes 688136 | tf_op jit(solution)/shard_map/ppermute | solution.py:554

commit v2 on v1

--- a/solution.py
+++ b/solution.py
@@ -20,7 +20,7 @@
 NU_T = 0.25
 
 FIELDS = 7
-ORDER = (4, 5, 3, 7, 1, 2, 6)
+ORDER = (3, 4, 5, 7, 1, 2, 6)
 EDGES = 2 * FIELDS + 3
 COEFS = 5
 TILE = 8
@@ -74,52 +74,86 @@
     return [(i, 2 * ((i // 2 + dy) % ring) + ((i % 2) ^ dx)) for i in range(count)]
 
 
-def pick_kernel(count, state_ref, flag_ref, *refs):
-    outs = refs[:count]
-    edge_ref, held_ref, sems = refs[count:]
-    fields, _, rows = state_ref.shape[1:4]
+def places_of(count, chosen):
     index = lax.axis_index("inst")
     ring = count // 2
-    places = [
-        2 * lax.rem(index // 2 + dy, ring) + lax.rem(lax.rem(index, 2) + dx, 2)
-        for dy, dx in slots(count)
+    steps = slots(count)
+    return [
+        2 * lax.rem(index // 2 + steps[k][0], ring) + lax.rem(lax.rem(index, 2) + steps[k][1], 2)
+        for k in chosen
     ]
+
+
+def first_kernel(count, chosen, state_ref, out_ref, sem):
+    (place,) = places_of(count, (chosen,))
+    copy = pltpu.make_async_copy(state_ref.at[0, :, place], out_ref, sem)
+    copy.start()
+    copy.wait()
+
+
+def rest_kernel(count, chosen, state_ref, flag_ref, early_ref, *refs):
+    outs = refs[: len(chosen)]
+    edge_ref, held_ref, sems = refs[len(chosen) :]
+    fields, rows = state_ref.shape[1], state_ref.shape[3]
+    early = next(k for k in range(count) if k not in chosen)
+    (early_place,), places = places_of(count, (early,)), places_of(count, chosen)
     copies = [
         pltpu.make_async_copy(state_ref.at[0, :, place], out, sems.at[k])
         for k, (place, out) in enumerate(zip(places, outs))
     ]
     for copy in copies:
         copy.start()
-    flag_copy = pltpu.make_async_copy(flag_ref, held_ref, sems.at[count])
+    flag_copy = pltpu.make_async_copy(flag_ref, held_ref, sems.at[len(chosen)])
     flag_copy.start()
+
+    def edges(place, block):
+        row = pl.ds(place, 1)
+        for f in range(fields):
+            edge_ref[f, row] = block[f, 0:1]
+            edge_ref[fields + f, row] = block[f, rows - 1 : rows]
+        edge_ref[2 * fields, row] = block[fields - 1, 1:2]
+        edge_ref[2 * fields + 1, row] = block[fields - 1, rows - 2 : rows - 1]
+
+    edges(early_place, early_ref)
     flag_copy.wait()
     flags = (held_ref[0] > 0).astype(jnp.float32)
     edge_ref[EDGES - 1] = jnp.broadcast_to(flags[:, 0:1], edge_ref.shape[1:])
     for copy, place, out in zip(copies, places, outs):
         copy.wait()
-        row = pl.ds(place, 1)
-        for f in range(fields):
-            edge_ref[f, row] = out[f, 0:1]
-            edge_ref[fields + f, row] = out[f, rows - 1 : rows]
-        edge_ref[2 * fields, row] = out[fields - 1, 1:2]
-        edge_ref[2 * fields + 1, row] = out[fields - 1, rows - 2 : rows - 1]
-
-
-def pick(state, flags, count):
+        edges(place, out)
+
+
+def pick_first(state, count, chosen):
+    _, fields, _, rows, lanes = state.shape
+    return pl.pallas_call(
+        functools.partial(first_kernel, count, chosen),
+        out_shape=jax.ShapeDtypeStruct((fields, rows, lanes), jnp.float32),
+        in_specs=[pl.BlockSpec(memory_space=pltpu.HBM)],
+        out_specs=VMEM,
+        scratch_shapes=[pltpu.SemaphoreType.DMA],
+        compiler_params=pltpu.CompilerParams(vmem_limit_bytes=4 << 20),
+        cost_estimate=pl.CostEstimate(
+            flops=0, bytes_accessed=fields * rows * lanes * 8, transcendentals=0
+        ),
+    )(pltpu.with_memory_space_constraint(state, pltpu.HBM))
+
+
+def pick_rest(state, flags, early, count, chosen):
     _, fields, planes, rows, lanes = state.shape
-    shapes = [(fields, rows, lanes)] * count + [(EDGES, planes, lanes)]
+    shapes = [(fields, rows, lanes)] * len(chosen) + [(EDGES, planes, lanes)]
+    hbm = pl.BlockSpec(memory_space=pltpu.HBM)
     return pl.pallas_call(
-        functools.partial(pick_kernel, count),
+        functools.partial(rest_kernel, count, chosen),
         out_shape=[jax.ShapeDtypeStruct(x, jnp.float32) for x in shapes],
-        in_specs=[pl.BlockSpec(memory_space=pltpu.HBM)] * 2,
+        in_specs=[hbm, hbm, VMEM],
         out_specs=[VMEM] * len(shapes),
         scratch_shapes=[
             pltpu.VMEM(flags.shape, flags.dtype),
-            pltpu.SemaphoreType.DMA((count + 1,)),
+            pltpu.SemaphoreType.DMA((len(chosen) + 1,)),
         ],
         compiler_params=pltpu.CompilerParams(vmem_limit_bytes=state.size * 4 + (3 << 20)),
         cost_estimate=pl.CostEstimate(flops=0, bytes_accessed=state.size * 8, transcendentals=0),
-    )(*(pltpu.with_memory_space_constraint(x, pltpu.HBM) for x in (state, flags)))
+    )(*(pltpu.with_memory_space_constraint(x, pltpu.HBM) for x in (state, flags)), early)
 
 
 def mixing(count, parity):
@@ -477,7 +511,7 @@
             block_ref[f, last, place] = state_ref[0, f, last, span] + own
             return 0
 
-        lax.fori_loop(0, tiles, tile, 0)
+        lax.fori_loop(0, tiles, tile, 0, unroll=True)
         copy = pltpu.make_async_copy(block_ref.at[f], out_ref.at[0, f, :, lines], sems.at[f])
         copy.start()
         copies.append(copy)
@@ -558,18 +592,24 @@
         return lax.ppermute(x, "ax", moves)
 
     steps = slots(instances)
-    blocks = list(pick(flow_state, thinc_flags, instances))
-    edges = blocks.pop()
+    order = ORDER
+    rest = tuple(k for k in range(instances) if k != order[0])
+    blocks = [None] * instances
+    early = pick_first(flow_state, instances, order[0])
+    *others, edges = pick_rest(flow_state, thinc_flags, early, instances, rest)
+    blocks[order[0]] = early
+    late_state, edges = lax.optimization_barrier((flow_state, edges))
+    for k, block in zip(rest, others):
+        blocks[k] = block
     halo = lax.ppermute(
         edges, "circ", [(i, (i + 1) % circ_count) for i in range(circ_count)]
     )
-    order = ORDER
     for k in order:
         blocks[k] = lax.ppermute(blocks[k], "inst", route(*steps[k], instances))
     flags = (thinc_flags[0] > 0).astype(jnp.float32)
     flag_cells = jnp.broadcast_to(flags[:, :, None], (planes, rows, lanes))
 
-    res, coup, inv, v, w, keep, send = flux_parts(flow_state, halo, flag_cells)
+    res, coup, inv, v, w, keep, send = flux_parts(late_state, halo, flag_cells)
 
     thin = (half, lanes)
     pair, raw, ends = call(
@@ -622,8 +662,8 @@
         flops=send.size * 4,
     )
     got = partner(send)
-    out = finish(True, flow_state, v, w, y_mine, keep)
-    return finish(False, flow_state, v, w, y_other, got, out)
+    out = finish(True, late_state, v, w, y_mine, keep)
+    return finish(False, late_state, v, w, y_other, got, out)
 
 
 def solution(mesh):

time: 115 us -> 119 us (1.035)
  waiting for transfers between devices: 26.7 us -> 34.6 us
  starting transfers between devices: 49.1 us -> 45.2 us
    ppermute x1, waiting for transfers between devices: 0.08 us -> 4.84 us  [body(): lax.ppermute(edges, 'circ', [(i, (i + 1) % circ_count) for i in range(cir...]
    ppermute x7, starting transfers between devices: 19.4 us -> 16.4 us  [body(): specs[k] = lax.ppermute(specs[k], 'inst', route(*steps[k], instances))]
    ppermute x7, waiting for transfers between devices: 6.57 us -> 8.33 us  [body(): specs[k] = lax.ppermute(specs[k], 'inst', route(*steps[k], instances))]
    ppermute x7, waiting for transfers between devices: 15.3 us -> 16.6 us  [body(): blocks[k] = lax.ppermute(blocks[k], 'inst', route(*steps[k], instances))]
    pallas_call x1 -> x2, Pallas kernels: 1.78 us -> 2.66 us  [the longest x1 1.57 us: pick_rest(): pl.pallas_call(functools.partial(rest_kernel, count, chosen), out_shape=[...]
  transfers between devices with their start and end apart: 20 -> 20, of which waited for: 7 -> 9; matrix products, arithmetic and copies ran while one was open for 0% -> 0% of each run, Pallas kernels for 4% -> 5%
where the time goes in v2:
time: 119 us
  starting transfers between devices  45.2 us (38%)
  waiting for transfers between devices  34.6 us (29%)
  blocking collectives  29.5 us (25%)
  Pallas kernels  9.34 us (8%)
    all_to_all x2, blocking collectives, exchange(): return lax.all_to_all(x, axis, 0, 0, tiled=True, axis_index_groups=groups)  29.5 us
    ppermute x7, waiting for transfers between devices, body(): blocks[k] = lax.ppermute(blocks[k], 'inst', route(*steps[k], instances))  16.6 us
    ppermute x7, starting transfers between devices, body(): specs[k] = lax.ppermute(specs[k], 'inst', route(*steps[k], instances))  16.4 us
    ppermute x3, starting transfers between devices, partner(): return lax.ppermute(x, 'ax', swap)  11.5 us
    ppermute x7, starting transfers between devices, body(): blocks[k] = lax.ppermute(blocks[k], 'inst', route(*steps[k], instances))  9.9 us
    ppermute x7, waiting for transfers between devices, body(): specs[k] = lax.ppermute(specs[k], 'inst', route(*steps[k], instances))  8.33 us
    ppermute x1, waiting for transfers between devices, body(): lax.ppermute(edges, 'circ', [(i, (i + 1) % circ_count) for i in range(cir...  4.84 us
    ppermute x2, starting transfers between devices, neighbour(): return lax.ppermute(x, 'ax', moves)  4.83 us
  transfers between devices with their start and end apart: 20, of which 9 were waited for; matrix products, arithmetic and copies ran while one was open for 0% of the time, Pallas kernels for 5%

profile of v2, /device:TPU:1, one launch (start us, length us, event | category | flops | bytes accessed | tf_op | source)
XLA Modules:
  0.0 118.9 jit_solution(15791894506131674046)
XLA Ops:
  0.0 1.1 shard_map.28.early_ref
  1.1 3.1 %collective-permute-start.3 = (f32[7,64,128]{2,1,0:T(8,128)S(1)}, f32[7,64,128]{2,1,0:T(8,128)S(1)}, u32[]{:S(2)}, u32[]{:S(2)}) collective-permute-start(f32[7,64,128]{2,1,0:T(8,128)S(1)} %shard_map.28.early_ref), channel_id=1, source_target_pairs={{0,96},{32,64},{64,160},{96,128},{128,224},{160,192},{192,32},{224... | collective-permute-start | bytes 688136 | tf_op jit(solution)/shard_map/ppermute | solution.py:608
  4.2 1.6 %shard_map.29 = (f32[7,64,128]{2,1,0:T(8,128)S(1)}, f32[7,64,128]{2,1,0:T(8,128)S(1)}, f32[7,64,128]{2,1,0:T(8,128)S(1)}, f32[7,64,128]{2,1,0:T(8,128)S(1)}, f32...) custom-call(f32[1,7,8,64,128]{4,3,2,1,0:T(8,128)} %state_ref.6, ...), custom_call_target="tpu_custom_call" | custom-call | bytes 3670016 | tf_op jit(solution)/shard_map/pallas_call | solution.py:145
  5.8 2.5 %collective-permute-start = (f32[17,8,128]{2,1,0:T(8,128)S(1)}, f32[17,8,128]{2,1,0:T(8,128)S(1)}, u32[]{:S(2)}, u32[]{:S(2)}) collective-permute-start(f32[17,8,128]{2,1,0:T(8,128)S(1)} %get-tuple-element.55), channel_id=1, source_target_pairs={{0,1},{1,0},{2,3},{3,2},{4,5},{5,4},{6,7},{7,6},{8,9},{9,8},{10,11... | collective-permute-start | bytes 208904 | tf_op jit(solution)/shard_map/ppermute | solution.py:604
  8.3 0.0 collective-permute-start.1
  8.4 4.8 %collective-permute-done.halo_ref = f32[17,8,128]{2,1,0:T(8,128)S(1)} collective-permute-done((f32[17,8,128]{2,1,0:T(8,128)S(1)}, f32[17,8,128]{2,1,0:T(8,128)S(1)}, u32[]{:S(2)}, u32[]{:S(2)}) %collective-permute-start) | collective-permute-done | bytes 69664 | tf_op jit(solution)/shard_map/ppermute | solution.py:604
  13.2 0.1 broadcast_in_dim.2.flag_ref
  13.3 2.5 %shard_map.30 = (f32[8,7,64,128]{3,2,1,0:T(8,128)S(1)}, f32[8,64,128]{2,1,0:T(8,128)S(1)}, f32[7,64,128]{2,1,0:T(8,128)S(1)}, f32[7,64,128]{2,1,0:T(8,128)S(1)},...) custom-call(f32[1,7,8,64,128]{4,3,2,1,0:T(8,128)S(1)} %copy-done, ...), custom_call_target="tpu_custom_call" | custom-call | flops 27525120 | bytes 5115904 | tf_op jit(solution)/shard_map/pallas_call | solution.py:64
  15.8 2.7 %collective-permute-start.8 = (f32[5,32,128]{2,1,0:T(8,128)S(1)}, f32[5,32,128]{2,1,0:T(8,128)S(1)}, u32[]{:S(2)}, u32[]{:S(2)}) collective-permute-start(f32[5,32,128]{2,1,0:T(8,128)S(1)} %get-tuple-element.67), channel_id=1, source_target_pairs={{0,2},{2,0},{4,6},{6,4},{8,10},{10,8},{12,14},{14,12},{16,18},{18,... | collective-permute-start | bytes 245768 | tf_op jit(solution)/shard_map/ppermute | solution.py:588
  18.6 1.3 %collective-permute-start.2 = (f32[7,64,128]{2,1,0:T(8,128)S(1)}, f32[7,64,128]{2,1,0:T(8,128)S(1)}, u32[]{:S(2)}, u32[]{:S(2)}) collective-permute-start(f32[7,64,128]{2,1,0:T(8,128)S(1)} %get-tuple-element.60), channel_id=1, source_target_pairs={{0,64},{32,96},{64,128},{96,160},{128,192},{160,224},{192,0},{224,... | collective-permute-start | bytes 688136 | tf_op jit(solution)/shard_map/ppermute | solution.py:608
  19.9 1.3 %collective-permute-start.4 = (f32[7,64,128]{2,1,0:T(8,128)S(1)}, f32[7,64,128]{2,1,0:T(8,128)S(1)}, u32[]{:S(2)}, u32[]{:S(2)}) collective-permute-start(f32[7,64,128]{2,1,0:T(8,128)S(1)} %get-tuple-element.61), channel_id=1, source_target_pairs={{0,128},{32,160},{64,192},{96,224},{128,0},{160,32},{192,64},{224,... | collective-permute-start | bytes 688136 | tf_op jit(solution)/shard_map/ppermute | solution.py:608
  21.2 0.0 collective-permute-done.8.got_ref
  21.2 1.3 %collective-permute-start.5 = (f32[7,64,128]{2,1,0:T(8,128)S(1)}, f32[7,64,128]{2,1,0:T(8,128)S(1)}, u32[]{:S(2)}, u32[]{:S(2)}) collective-permute-start(f32[7,64,128]{2,1,0:T(8,128)S(1)} %get-tuple-element.62), channel_id=1, source_target_pairs={{0,160},{32,128},{64,224},{96,192},{128,32},{160,0},{192,96},{224,... | collective-permute-start | bytes 688136 | tf_op jit(solution)/shard_map/ppermute | solution.py:608
  22.5 1.4 %collective-permute-start.6 = (f32[7,64,128]{2,1,0:T(8,128)S(1)}, f32[7,64,128]{2,1,0:T(8,128)S(1)}, u32[]{:S(2)}, u32[]{:S(2)}) collective-permute-start(f32[7,64,128]{2,1,0:T(8,128)S(1)} %get-tuple-element.63), channel_id=1, source_target_pairs={{0,192},{32,224},{64,0},{96,32},{128,64},{160,96},{192,128},{224,1... | collective-permute-start | bytes 688136 | tf_op jit(solution)/shard_map/ppermute | solution.py:608
  23.9 0.0 collective-permute-done.1.refs_1_
  23.9 1.5 %collective-permute-start.7 = (f32[7,64,128]{2,1,0:T(8,128)S(1)}, f32[7,64,128]{2,1,0:T(8,128)S(1)}, u32[]{:S(2)}, u32[]{:S(2)}) collective-permute-start(f32[7,64,128]{2,1,0:T(8,128)S(1)} %get-tuple-element.64), channel_id=1, source_target_pairs={{0,224},{32,192},{64,32},{96,0},{128,96},{160,64},{192,160},{224,1... | collective-permute-start | bytes 688136 | tf_op jit(solution)/shard_map/ppermute | solution.py:608
  25.4 5.9 %collective-permute-done.2.refs_2_ = f32[7,64,128]{2,1,0:T(8,128)S(1)} collective-permute-done((f32[7,64,128]{2,1,0:T(8,128)S(1)}, f32[7,64,128]{2,1,0:T(8,128)S(1)}, u32[]{:S(2)}, u32[]{:S(2)}) %collective-permute-start.2) | collective-permute-done | bytes 229408 | tf_op jit(solution)/shard_map/ppermute | solution.py:608
  31.2 5.4 %collective-permute-done.4.refs_4_ = f32[7,64,128]{2,1,0:T(8,128)S(1)} collective-permute-done((f32[7,64,128]{2,1,0:T(8,128)S(1)}, f32[7,64,128]{2,1,0:T(8,128)S(1)}, u32[]{:S(2)}, u32[]{:S(2)}) %collective-permute-start.4) | collective-permute-done | bytes 229408 | tf_op jit(solution)/shard_map/ppermute | solution.py:608
  36.7 5.2 %collective-permute-done.6.refs_6_ = f32[7,64,128]{2,1,0:T(8,128)S(1)} collective-permute-done((f32[7,64,128]{2,1,0:T(8,128)S(1)}, f32[7,64,128]{2,1,0:T(8,128)S(1)}, u32[]{:S(2)}, u32[]{:S(2)}) %collective-permute-start.6) | collective-permute-done | bytes 229408 | tf_op jit(solution)/shard_map/ppermute | solution.py:608
  41.9 0.0 collective-permute-done.7.refs_7_
  41.9 0.8 shard_map.32
  42.8 0.1 collective-permute-start.9
  42.9 2.8 %collective-permute-start.10 = (f32[7,64,128]{2,1,0:T(8,128)S(1)}, f32[7,64,128]{2,1,0:T(8,128)S(1)}, u32[]{:S(2)}, u32[]{:S(2)}) collective-permute-start(f32[7,64,128]{2,1,0:T(8,128)S(1)} %get-tuple-element.82), channel_id=1, source_target_pairs={{0,64},{32,96},{64,128},{96,160},{128,192},{160,224},{192,0},{224,... | collective-permute-start | bytes 688136 | tf_op jit(solution)/shard_map/ppermute | solution.py:621
  45.7 1.1 collective-permute-start.11
  46.7 1.6 %collective-permute-start.12 = (f32[7,64,128]{2,1,0:T(8,128)S(1)}, f32[7,64,128]{2,1,0:T(8,128)S(1)}, u32[]{:S(2)}, u32[]{:S(2)}) collective-permute-start(f32[7,64,128]{2,1,0:T(8,128)S(1)} %get-tuple-element.84), channel_id=1, source_target_pairs={{0,128},{32,160},{64,192},{96,224},{128,0},{160,32},{192,64},{224,... | collective-permute-start | bytes 688136 | tf_op jit(solution)/shard_map/ppermute | solution.py:621
  48.3 1.4 %collective-permute-start.13 = (f32[7,64,128]{2,1,0:T(8,128)S(1)}, f32[7,64,128]{2,1,0:T(8,128)S(1)}, u32[]{:S(2)}, u32[]{:S(2)}) collective-permute-start(f32[7,64,128]{2,1,0:T(8,128)S(1)} %get-tuple-element.85), channel_id=1, source_target_pairs={{0,160},{32,128},{64,224},{96,192},{128,32},{160,0},{192,96},{224,... | collective-permute-start | bytes 688136 | tf_op jit(solution)/shard_map/ppermute | solution.py:621
  49.7 0.0 collective-permute-done.9.refs_1_
  49.7 2.9 %collective-permute-start.14 = (f32[7,64,128]{2,1,0:T(8,128)S(1)}, f32[7,64,128]{2,1,0:T(8,128)S(1)}, u32[]{:S(2)}, u32[]{:S(2)}) collective-permute-start(f32[7,64,128]{2,1,0:T(8,128)S(1)} %get-tuple-element.86), channel_id=1, source_target_pairs={{0,192},{32,224},{64,0},{96,32},{128,64},{160,96},{192,128},{224,1... | collective-permute-start | bytes 688136 | tf_op jit(solution)/shard_map/ppermute | solution.py:621
  52.6 4.2 %collective-permute-done.10.refs_2_ = f32[7,64,128]{2,1,0:T(8,128)S(1)} collective-permute-done((f32[7,64,128]{2,1,0:T(8,128)S(1)}, f32[7,64,128]{2,1,0:T(8,128)S(1)}, u32[]{:S(2)}, u32[]{:S(2)}) %collective-permute-start.10) | collective-permute-done | bytes 229408 | tf_op jit(solution)/shard_map/ppermute | solution.py:621
  56.8 6.5 %collective-permute-start.15 = (f32[7,64,128]{2,1,0:T(8,128)S(1)}, f32[7,64,128]{2,1,0:T(8,128)S(1)}, u32[]{:S(2)}, u32[]{:S(2)}) collective-permute-start(f32[7,64,128]{2,1,0:T(8,128)S(1)} %get-tuple-element.87), channel_id=1, source_target_pairs={{0,224},{32,192},{64,32},{96,0},{128,96},{160,64},{192,160},{224,1... | collective-permute-start | bytes 688136 | tf_op jit(solution)/shard_map/ppermute | solution.py:621
  63.3 0.0 collective-permute-done.11.refs_3_
  63.3 4.1 %collective-permute-done.12.refs_4_ = f32[7,64,128]{2,1,0:T(8,128)S(1)} collective-permute-done((f32[7,64,128]{2,1,0:T(8,128)S(1)}, f32[7,64,128]{2,1,0:T(8,128)S(1)}, u32[]{:S(2)}, u32[]{:S(2)}) %collective-permute-start.12) | collective-permute-done | bytes 229408 | tf_op jit(solution)/shard_map/ppermute | solution.py:621
  67.5 0.5 shard_map.33
  68.0 3.9 %collective-permute-start.16 = (f32[14,32,128]{2,1,0:T(8,128)S(1)}, f32[14,32,128]{2,1,0:T(8,128)S(1)}, u32[]{:S(2)}, u32[]{:S(2)}) collective-permute-start(f32[14,32,128]{2,1,0:T(8,128)S(1)} %get-tuple-element.90), channel_id=1, source_target_pairs={{0,2},{2,0},{4,6},{6,4},{8,10},{10,8},{12,14},{14,12},{16,18},{18,... | collective-permute-start | bytes 688136 | tf_op jit(solution)/shard_map/ppermute | solution.py:588
  71.9 1.3 %collective-permute-start.17 = (f32[2,32,128]{2,1,0:T(8,128)S(1)}, f32[2,32,128]{2,1,0:T(8,128)S(1)}, u32[]{:S(2)}, u32[]{:S(2)}) collective-permute-start(f32[2,32,128]{2,1,0:T(8,128)S(1)} %get-tuple-element.93), channel_id=1, source_target_pairs={{4,0},{6,2},{8,4},{10,6},{12,8},{14,10},{16,12},{18,14},{20,16},{2... | collective-permute-start | bytes 98312 | tf_op jit(solution)/shard_map/ppermute | solution.py:592
  73.2 3.9 %collective-permute-done.17.ends_ref = f32[2,32,128]{2,1,0:T(8,128)S(1)} collective-permute-done((f32[2,32,128]{2,1,0:T(8,128)S(1)}, f32[2,32,128]{2,1,0:T(8,128)S(1)}, u32[]{:S(2)}, u32[]{:S(2)}) %collective-permute-start.17) | collective-permute-done | bytes 32800 | tf_op jit(solution)/shard_map/ppermute | solution.py:592
  77.1 3.5 %collective-permute-start.18 = (f32[1,32,128]{2,1,0:T(8,128)S(1)}, f32[1,32,128]{2,1,0:T(8,128)S(1)}, u32[]{:S(2)}, u32[]{:S(2)}) collective-permute-start(f32[1,32,128]{2,1,0:T(8,128)S(1)} %get-tuple-element.95), channel_id=1, source_target_pairs={{0,4},{2,6},{4,8},{6,10},{8,12},{10,14},{12,16},{14,18},{16,20},{1... | collective-permute-start | bytes 49160 | tf_op jit(solution)/shard_map/ppermute | solution.py:592
  80.6 0.9 collective-permute-done.18.edge_ref
  81.5 0.5 shard_map.34
  82.0 0.1 shard_map.37
  82.1 18.2 %all_to_all.10.rhs_ref = f32[8,16,4,128]{3,2,1,0:T(4,128)S(1)} all-to-all(f32[8,16,4,128]{3,2,1,0:T(4,128)S(1)} %get-tuple-element.96), channel_id=1, replica_groups={{0,4,8,12,16,20,24,28},{2,6,10,14,18,22,26,30},{1,5,9,13,17,21,25,29},{..., dimensions={0} | all-to-all | bytes 524288 | tf_op jit(solution)/shard_map/all_to_all | solution.py:571
  100.3 0.1 shard_map.38
  100.4 11.4 %all_to_all.11.solved_ref = f32[8,14,4,128]{3,2,1,0:T(4,128)S(1)} all-to-all(f32[8,14,4,128]{3,2,1,0:T(4,128)S(1)} %shard_map.38), channel_id=1, replica_groups={{0,4,8,12,16,20,24,28},{2,6,10,14,18,22,26,30},{1,5,9,13,17,21,25,29},{..., dimensions={0} | all-to-all | bytes 458752 | tf_op jit(solution)/shard_map/all_to_all | solution.py:571
  111.8 0.1 shard_map.39
  111.8 4.9 %collective-permute-start.19 = (f32[14,32,128]{2,1,0:T(8,128)S(1)}, f32[14,32,128]{2,1,0:T(8,128)S(1)}, u32[]{:S(2)}, u32[]{:S(2)}) collective-permute-start(f32[14,32,128]{2,1,0:T(8,128)S(1)} %get-tuple-element.98), channel_id=1, source_target_pairs={{0,2},{2,0},{4,6},{6,4},{8,10},{10,8},{12,14},{14,12},{16,18},{18,... | collective-permute-start | bytes 688136 | tf_op jit(solution)/shard_map/ppermute | solution.py:588
  116.8 1.0 shard_map.40.refs_0_
  117.8 0.1 collective-permute-done.19.ends_ref
  117.9 1.0 shard_map.41
  (14 shorter events, 0.1 us)
Async XLA Ops:
  0.0 13.3 %copy-start = (f32[1,7,8,64,128]{4,3,2,1,0:T(8,128)S(1)}, f32[1,7,8,64,128]{4,3,2,1,0:T(8,128)}, u32[]{:S(2)}) copy-start(f32[1,7,8,64,128]{4,3,2,1,0:T(8,128)} %state_ref.6) | copy-start | bytes 5505028
  0.0 8.3 %copy-start.1 = (s32[1,8,64]{2,1,0:T(8,128)S(1)}, s32[1,8,64]{2,1,0:T(8,128)}, u32[]{:S(2)}) copy-start(s32[1,8,64]{2,1,0:T(8,128)} %flag_ref.1) | copy-start | bytes 6148
  1.1 21.4 %collective-permute-start.3 = (f32[7,64,128]{2,1,0:T(8,128)S(1)}, f32[7,64,128]{2,1,0:T(8,128)S(1)}, u32[]{:S(2)}, u32[]{:S(2)}) collective-permute-start(f32[7,64,128]{2,1,0:T(8,128)S(1)} %shard_map.28.early_ref), channel_id=1, source_target_pairs={{0,96},{32,64},{64,160},{96,128},{128,224},{160,192},{192,32},{224... | collective-permute-start | bytes 688136 | tf_op jit(solution)/shard_map/ppermute | solution.py:608
  5.8 7.4 %collective-permute-start = (f32[17,8,128]{2,1,0:T(8,128)S(1)}, f32[17,8,128]{2,1,0:T(8,128)S(1)}, u32[]{:S(2)}, u32[]{:S(2)}) collective-permute-start(f32[17,8,128]{2,1,0:T(8,128)S(1)} %get-tuple-element.55), channel_id=1, source_target_pairs={{0,1},{1,0},{2,3},{3,2},{4,5},{5,4},{6,7},{7,6},{8,9},{9,8},{10,11... | collective-permute-start | bytes 208904 | tf_op jit(solution)/shard_map/ppermute | solution.py:604
  8.3 15.5 %collective-permute-start.1 = (f32[7,64,128]{2,1,0:T(8,128)S(1)}, f32[7,64,128]{2,1,0:T(8,128)S(1)}, u32[]{:S(2)}, u32[]{:S(2)}) collective-permute-start(f32[7,64,128]{2,1,0:T(8,128)S(1)} %get-tuple-element.59), channel_id=1, source_target_pairs={{0,32},{32,0},{64,96},{96,64},{128,160},{160,128},{192,224},{224,1... | collective-permute-start | bytes 688136 | tf_op jit(solution)/shard_map/ppermute | solution.py:608
  15.8 5.4 %collective-permute-start.8 = (f32[5,32,128]{2,1,0:T(8,128)S(1)}, f32[5,32,128]{2,1,0:T(8,128)S(1)}, u32[]{:S(2)}, u32[]{:S(2)}) collective-permute-start(f32[5,32,128]{2,1,0:T(8,128)S(1)} %get-tuple-element.67), channel_id=1, source_target_pairs={{0,2},{2,0},{4,6},{6,4},{8,10},{10,8},{12,14},{14,12},{16,18},{18,... | collective-permute-start | bytes 245768 | tf_op jit(solution)/shard_map/ppermute | solution.py:588
  18.6 12.7 %collective-permute-start.2 = (f32[7,64,128]{2,1,0:T(8,128)S(1)}, f32[7,64,128]{2,1,0:T(8,128)S(1)}, u32[]{:S(2)}, u32[]{:S(2)}) collective-permute-start(f32[7,64,128]{2,1,0:T(8,128)S(1)} %get-tuple-element.60), channel_id=1, source_target_pairs={{0,64},{32,96},{64,128},{96,160},{128,192},{160,224},{192,0},{224,... | collective-permute-start | bytes 688136 | tf_op jit(solution)/shard_map/ppermute | solution.py:608
  19.9 16.8 %collective-permute-start.4 = (f32[7,64,128]{2,1,0:T(8,128)S(1)}, f32[7,64,128]{2,1,0:T(8,128)S(1)}, u32[]{:S(2)}, u32[]{:S(2)}) collective-permute-start(f32[7,64,128]{2,1,0:T(8,128)S(1)} %get-tuple-element.61), channel_id=1, source_target_pairs={{0,128},{32,160},{64,192},{96,224},{128,0},{160,32},{192,64},{224,... | collective-permute-start | bytes 688136 | tf_op jit(solution)/shard_map/ppermute | solution.py:608
  21.2 15.5 %collective-permute-start.5 = (f32[7,64,128]{2,1,0:T(8,128)S(1)}, f32[7,64,128]{2,1,0:T(8,128)S(1)}, u32[]{:S(2)}, u32[]{:S(2)}) collective-permute-start(f32[7,64,128]{2,1,0:T(8,128)S(1)} %get-tuple-element.62), channel_id=1, source_target_pairs={{0,160},{32,128},{64,224},{96,192},{128,32},{160,0},{192,96},{224,... | collective-permute-start | bytes 688136 | tf_op jit(solution)/shard_map/ppermute | solution.py:608
  22.5 19.4 %collective-permute-start.6 = (f32[7,64,128]{2,1,0:T(8,128)S(1)}, f32[7,64,128]{2,1,0:T(8,128)S(1)}, u32[]{:S(2)}, u32[]{:S(2)}) collective-permute-start(f32[7,64,128]{2,1,0:T(8,128)S(1)} %get-tuple-element.63), channel_id=1, source_target_pairs={{0,192},{32,224},{64,0},{96,32},{128,64},{160,96},{192,128},{224,1... | collective-permute-start | bytes 688136 | tf_op jit(solution)/shard_map/ppermute | solution.py:608
  23.9 18.1 %collective-permute-start.7 = (f32[7,64,128]{2,1,0:T(8,128)S(1)}, f32[7,64,128]{2,1,0:T(8,128)S(1)}, u32[]{:S(2)}, u32[]{:S(2)}) collective-permute-start(f32[7,64,128]{2,1,0:T(8,128)S(1)} %get-tuple-element.64), channel_id=1, source_target_pairs={{0,224},{32,192},{64,32},{96,0},{128,96},{160,64},{192,160},{224,1... | collective-permute-start | bytes 688136 | tf_op jit(solution)/shard_map/ppermute | solution.py:608
  42.8 7.0 %collective-permute-start.9 = (f32[7,64,128]{2,1,0:T(8,128)S(1)}, f32[7,64,128]{2,1,0:T(8,128)S(1)}, u32[]{:S(2)}, u32[]{:S(2)}) collective-permute-start(f32[7,64,128]{2,1,0:T(8,128)S(1)} %get-tuple-element.81), channel_id=1, source_target_pairs={{0,32},{32,0},{64,96},{96,64},{128,160},{160,128},{192,224},{224,1... | collective-permute-start | bytes 688136 | tf_op jit(solution)/shard_map/ppermute | solution.py:621
  42.9 14.0 %collective-permute-start.10 = (f32[7,64,128]{2,1,0:T(8,128)S(1)}, f32[7,64,128]{2,1,0:T(8,128)S(1)}, u32[]{:S(2)}, u32[]{:S(2)}) collective-permute-start(f32[7,64,128]{2,1,0:T(8,128)S(1)} %get-tuple-element.82), channel_id=1, source_target_pairs={{0,64},{32,96},{64,128},{96,160},{128,192},{160,224},{192,0},{224,... | collective-permute-start | bytes 688136 | tf_op jit(solution)/shard_map/ppermute | solution.py:621
  45.7 17.7 %collective-permute-start.11 = (f32[7,64,128]{2,1,0:T(8,128)S(1)}, f32[7,64,128]{2,1,0:T(8,128)S(1)}, u32[]{:S(2)}, u32[]{:S(2)}) collective-permute-start(f32[7,64,128]{2,1,0:T(8,128)S(1)} %get-tuple-element.83), channel_id=1, source_target_pairs={{0,96},{32,64},{64,160},{96,128},{128,224},{160,192},{192,32},{224... | collective-permute-start | bytes 688136 | tf_op jit(solution)/shard_map/ppermute | solution.py:621
  46.7 20.7 %collective-permute-start.12 = (f32[7,64,128]{2,1,0:T(8,128)S(1)}, f32[7,64,128]{2,1,0:T(8,128)S(1)}, u32[]{:S(2)}, u32[]{:S(2)}) collective-permute-start(f32[7,64,128]{2,1,0:T(8,128)S(1)} %get-tuple-element.84), channel_id=1, source_target_pairs={{0,128},{32,160},{64,192},{96,224},{128,0},{160,32},{192,64},{224,... | collective-permute-start | bytes 688136 | tf_op jit(solution)/shard_map/ppermute | solution.py:621
  48.3 19.1 %collective-permute-start.13 = (f32[7,64,128]{2,1,0:T(8,128)S(1)}, f32[7,64,128]{2,1,0:T(8,128)S(1)}, u32[]{:S(2)}, u32[]{:S(2)}) collective-permute-start(f32[7,64,128]{2,1,0:T(8,128)S(1)} %get-tuple-element.85), channel_id=1, source_target_pairs={{0,160},{32,128},{64,224},{96,192},{128,32},{160,0},{192,96},{224,... | collective-permute-start | bytes 688136 | tf_op jit(solution)/shard_map/ppermute | solution.py:621
  49.7 17.7 %collective-permute-start.14 = (f32[7,64,128]{2,1,0:T(8,128)S(1)}, f32[7,64,128]{2,1,0:T(8,128)S(1)}, u32[]{:S(2)}, u32[]{:S(2)}) collective-permute-start(f32[7,64,128]{2,1,0:T(8,128)S(1)} %get-tuple-element.86), channel_id=1, source_target_pairs={{0,192},{32,224},{64,0},{96,32},{128,64},{160,96},{192,128},{224,1... | collective-permute-start | bytes 688136 | tf_op jit(solution)/shard_map/ppermute | solution.py:621
  56.8 10.6 %collective-permute-start.15 = (f32[7,64,128]{2,1,0:T(8,128)S(1)}, f32[7,64,128]{2,1,0:T(8,128)S(1)}, u32[]{:S(2)}, u32[]{:S(2)}) collective-permute-start(f32[7,64,128]{2,1,0:T(8,128)S(1)} %get-tuple-element.87), channel_id=1, source_target_pairs={{0,224},{32,192},{64,32},{96,0},{128,96},{160,64},{192,160},{224,1... | collective-permute-start | bytes 688136 | tf_op jit(solution)/shard_map/ppermute | solution.py:621
  68.0 14.0 %collective-permute-start.16 = (f32[14,32,128]{2,1,0:T(8,128)S(1)}, f32[14,32,128]{2,1,0:T(8,128)S(1)}, u32[]{:S(2)}, u32[]{:S(2)}) collective-permute-start(f32[14,32,128]{2,1,0:T(8,128)S(1)} %get-tuple-element.90), channel_id=1, source_target_pairs={{0,2},{2,0},{4,6},{6,4},{8,10},{10,8},{12,14},{14,12},{16,18},{18,... | collective-permute-start | bytes 688136 | tf_op jit(solution)/shard_map/ppermute | solution.py:588
  71.9 5.2 %collective-permute-start.17 = (f32[2,32,128]{2,1,0:T(8,128)S(1)}, f32[2,32,128]{2,1,0:T(8,128)S(1)}, u32[]{:S(2)}, u32[]{:S(2)}) collective-permute-start(f32[2,32,128]{2,1,0:T(8,128)S(1)} %get-tuple-element.93), channel_id=1, source_target_pairs={{4,0},{6,2},{8,4},{10,6},{12,8},{14,10},{16,12},{18,14},{20,16},{2... | collective-permute-start | bytes 98312 | tf_op jit(solution)/shard_map/ppermute | solution.py:592
  77.1 4.4 %collective-permute-start.18 = (f32[1,32,128]{2,1,0:T(8,128)S(1)}, f32[1,32,128]{2,1,0:T(8,128)S(1)}, u32[]{:S(2)}, u32[]{:S(2)}) collective-permute-start(f32[1,32,128]{2,1,0:T(8,128)S(1)} %get-tuple-element.95), channel_id=1, source_target_pairs={{0,4},{2,6},{4,8},{6,10},{8,12},{10,14},{12,16},{14,18},{16,20},{1... | collective-permute-start | bytes 49160 | tf_op jit(solution)/shard_map/ppermute | solution.py:592
  111.8 6.0 %collective-permute-start.19 = (f32[14,32,128]{2,1,0:T(8,128)S(1)}, f32[14,32,128]{2,1,0:T(8,128)S(1)}, u32[]{:S(2)}, u32[]{:S(2)}) collective-permute-start(f32[14,32,128]{2,1,0:T(8,128)S(1)} %get-tuple-element.98), channel_id=1, source_target_pairs={{0,2},{2,0},{4,6},{6,4},{8,10},{10,8},{12,14},{14,12},{16,18},{18,... | collective-permute-start | bytes 688136 | tf_op jit(solution)/shard_map/ppermute | solution.py:588

commit v3 on v2

--- a/solution.py
+++ b/solution.py
@@ -227,13 +227,31 @@
 
 
 def flux_kernel(
-    state_ref, halo_ref, flag_ref, res_ref, coup_ref, inv_ref, v_ref, w_ref, keep_ref, send_ref
+    source_ref,
+    halo_ref,
+    flag_ref,
+    res_ref,
+    coup_ref,
+    inv_ref,
+    v_ref,
+    w_ref,
+    keep_ref,
+    send_ref,
+    state_ref,
+    sems,
 ):
+    def fetch(i):
+        return pltpu.make_async_copy(source_ref.at[0, :, i], state_ref.at[0, :, i], sems.at[i])
+
+    for i in range(state_ref.shape[2]):
+        fetch(i).start()
+
     planes = state_ref.shape[2]
     rows = state_ref.shape[3]
     last = planes - 1
 
     def plane(i, _):
+        fetch(i).wait()
         row = pl.ds(i, 1)
         quad = (TILE // 2, state_ref.shape[4])
         cells = []
@@ -549,22 +567,27 @@
 def flux_parts(state, halo, flag_cells):
     fields, planes, rows, lanes = state.shape[1:]
     grid = (rows, lanes)
-    return call(
+    shapes = [
+        (planes, fields) + grid,
+        (planes,) + grid,
+        (planes - 1,) + grid,
+        (planes - 1,) + grid,
+        (planes - 1,) + grid,
+        (COEFS, rows // 2, lanes),
+        (COEFS, rows // 2, lanes),
+        state.shape,
+    ]
+    return pl.pallas_call(
         flux_kernel,
-        [
-            (planes, fields) + grid,
-            (planes,) + grid,
-            (planes - 1,) + grid,
-            (planes - 1,) + grid,
-            (planes - 1,) + grid,
-            (COEFS, rows // 2, lanes),
-            (COEFS, rows // 2, lanes),
-        ],
-        state,
-        halo,
-        flag_cells,
-        flops=state.size * 60,
-    )
+        out_shape=[jax.ShapeDtypeStruct(x, jnp.float32) for x in shapes],
+        in_specs=[pl.BlockSpec(memory_space=pltpu.HBM), VMEM, VMEM],
+        out_specs=[VMEM] * len(shapes),
+        scratch_shapes=[pltpu.SemaphoreType.DMA((planes,))],
+        compiler_params=pltpu.CompilerParams(vmem_limit_bytes=state.size * 12),
+        cost_estimate=pl.CostEstimate(
+            flops=state.size * 60, bytes_accessed=state.size * 16, transcendentals=0
+        ),
+    )(pltpu.with_memory_space_constraint(state, pltpu.HBM), halo, flag_cells)
 
 
 def exchange(x, axis, groups=None):
@@ -598,7 +621,6 @@
     early = pick_first(flow_state, instances, order[0])
     *others, edges = pick_rest(flow_state, thinc_flags, early, instances, rest)
     blocks[order[0]] = early
-    late_state, edges = lax.optimization_barrier((flow_state, edges))
     for k, block in zip(rest, others):
         blocks[k] = block
     halo = lax.ppermute(
@@ -609,18 +631,17 @@
     flags = (thinc_flags[0] > 0).astype(jnp.float32)
     flag_cells = jnp.broadcast_to(flags[:, :, None], (planes, rows, lanes))
 
-    res, coup, inv, v, w, keep, send = flux_parts(late_state, halo, flag_cells)
+    res, coup, inv, v, w, keep, send, held_state = flux_parts(flow_state, halo, flag_cells)
 
     thin = (half, lanes)
     pair, raw, ends = call(
         pair_kernel, [(6,) + thin, (3,) + thin, (2,) + thin], keep, partner(send)
     )
-    blocks, res, ends = lax.optimization_barrier((blocks, res, ends))
+    ends = neighbour(ends, -1)
+    link, edge = call(link_kernel, [(3,) + thin, (1,) + thin], raw, ends)
     specs = call(spectral_kernel, [blocks[0].shape] * instances, *blocks, flops=own.size * 9)
     for k in order:
         specs[k] = lax.ppermute(specs[k], "inst", route(*steps[k], instances))
-    ends = neighbour(ends, -1)
-    link, edge = call(link_kernel, [(3,) + thin, (1,) + thin], raw, ends)
     edge = neighbour(edge, 1)
     (link,) = call(join_kernel, [(4,) + thin], link, edge)
     shapes = [(planes - 1, FIELDS, half, lanes), (2 * FIELDS, half, lanes)]
@@ -662,8 +683,8 @@
         flops=send.size * 4,
     )
     got = partner(send)
-    out = finish(True, late_state, v, w, y_mine, keep)
-    return finish(False, late_state, v, w, y_other, got, out)
+    out = finish(True, held_state, v, w, y_mine, keep)
+    return finish(False, held_state, v, w, y_other, got, out)
 
 
 def solution(mesh):

time: 119 us -> 111 us (0.933)
  starting transfers between devices: 45.2 us -> 38.1 us
  waiting for transfers between devices: 34.6 us -> 31.7 us
    ppermute x3, starting transfers between devices: 11.5 us -> 6.85 us  [partner(): return lax.ppermute(x, 'ax', swap)]
    ppermute x7, starting transfers between devices: 16.4 us -> 11.7 us  [body(): specs[k] = lax.ppermute(specs[k], 'inst', route(*steps[k], instances))]
    pallas_call x0 -> x1, Pallas kernels: none -> 3.51 us  [flux_parts(): pl.pallas_call(flux_kernel, out_shape=[jax.ShapeDtypeStruct(x, jnp.float3...]
    ppermute x7, waiting for transfers between devices: 16.6 us -> 13.8 us  [body(): blocks[k] = lax.ppermute(blocks[k], 'inst', route(*steps[k], instances))]
    ppermute x1, waiting for transfers between devices: 4.84 us -> 2.17 us  [body(): lax.ppermute(edges, 'circ', [(i, (i + 1) % circ_count) for i in range(cir...]
    pallas_call x10 -> x9, Pallas kernels: 4.65 us -> 2.12 us  [call(): return list(run(*operands))]
    ppermute x7, starting transfers between devices: 9.9 us -> 12.3 us  [body(): blocks[k] = lax.ppermute(blocks[k], 'inst', route(*steps[k], instances))]
    ppermute x7, waiting for transfers between devices: 8.33 us -> 10.3 us  [body(): specs[k] = lax.ppermute(specs[k], 'inst', route(*steps[k], instances))]
  transfers between devices with their start and end apart: 20 -> 20, of which waited for: 9 -> 10; matrix products, arithmetic and copies ran while one was open for 0% -> 0% of each run, Pallas kernels for 5% -> 6%
where the time goes in v3:
time: 111 us; the launch traced here: 110 us
  starting transfers between devices  38.1 us (34%)
  waiting for transfers between devices  31.7 us (29%)
  blocking collectives  29.9 us (27%)
  Pallas kernels  10.2 us (9%)
    all_to_all x2, blocking collectives, exchange(): return lax.all_to_all(x, axis, 0, 0, tiled=True, axis_index_groups=groups)  29.9 us
    ppermute x7, waiting for transfers between devices, body(): blocks[k] = lax.ppermute(blocks[k], 'inst', route(*steps[k], instances))  13.8 us
    ppermute x7, starting transfers between devices, body(): blocks[k] = lax.ppermute(blocks[k], 'inst', route(*steps[k], instances))  12.3 us
    ppermute x7, starting transfers between devices, body(): specs[k] = lax.ppermute(specs[k], 'inst', route(*steps[k], instances))  11.7 us
    ppermute x7, waiting for transfers between devices, body(): specs[k] = lax.ppermute(specs[k], 'inst', route(*steps[k], instances))  10.3 us
    ppermute x3, starting transfers between devices, partner(): return lax.ppermute(x, 'ax', swap)  6.85 us
    ppermute x2, starting transfers between devices, neighbour(): return lax.ppermute(x, 'ax', moves)  4.83 us
    ppermute x2, waiting for transfers between devices, neighbour(): return lax.ppermute(x, 'ax', moves)  4.21 us
  transfers between devices with their start and end apart: 20, of which 10 were waited for; matrix products, arithmetic and copies ran while one was open for 0% of the time, Pallas kernels for 6%

profile of v3, /device:TPU:1, one launch (start us, length us, event | category | flops | bytes accessed | tf_op | source)
XLA Modules:
  0.0 110.1 jit_solution(2561434441455199307)
XLA Ops:
  0.0 0.9 shard_map.28.early_ref
  1.0 0.0 copy-start
  1.0 3.1 %collective-permute-start.3 = (f32[7,64,128]{2,1,0:T(8,128)S(1)}, f32[7,64,128]{2,1,0:T(8,128)S(1)}, u32[]{:S(2)}, u32[]{:S(2)}) collective-permute-start(f32[7,64,128]{2,1,0:T(8,128)S(1)} %shard_map.28.early_ref), channel_id=1, source_target_pairs={{0,96},{32,64},{64,160},{96,128},{128,224},{160,192},{192,32},{224... | collective-permute-start | bytes 688136 | tf_op jit(solution)/shard_map/ppermute | solution.py:630
  4.1 1.6 %shard_map.29 = (f32[7,64,128]{2,1,0:T(8,128)S(1)}, f32[7,64,128]{2,1,0:T(8,128)S(1)}, f32[7,64,128]{2,1,0:T(8,128)S(1)}, f32[7,64,128]{2,1,0:T(8,128)S(1)}, f32...) custom-call(f32[1,7,8,64,128]{4,3,2,1,0:T(8,128)} %source_ref.1, ...), custom_call_target="tpu_custom_call" | custom-call | bytes 3670016 | tf_op jit(solution)/shard_map/pallas_call | solution.py:145
  5.7 0.3 collective-permute-start.1
  6.0 1.3 %collective-permute-start.2 = (f32[7,64,128]{2,1,0:T(8,128)S(1)}, f32[7,64,128]{2,1,0:T(8,128)S(1)}, u32[]{:S(2)}, u32[]{:S(2)}) collective-permute-start(f32[7,64,128]{2,1,0:T(8,128)S(1)} %get-tuple-element.51), channel_id=1, source_target_pairs={{0,64},{32,96},{64,128},{96,160},{128,192},{160,224},{192,0},{224,... | collective-permute-start | bytes 688136 | tf_op jit(solution)/shard_map/ppermute | solution.py:630
  7.3 1.4 %collective-permute-start.4 = (f32[7,64,128]{2,1,0:T(8,128)S(1)}, f32[7,64,128]{2,1,0:T(8,128)S(1)}, u32[]{:S(2)}, u32[]{:S(2)}) collective-permute-start(f32[7,64,128]{2,1,0:T(8,128)S(1)} %get-tuple-element.52), channel_id=1, source_target_pairs={{0,128},{32,160},{64,192},{96,224},{128,0},{160,32},{192,64},{224,... | collective-permute-start | bytes 688136 | tf_op jit(solution)/shard_map/ppermute | solution.py:630
  8.7 2.5 %collective-permute-start.5 = (f32[7,64,128]{2,1,0:T(8,128)S(1)}, f32[7,64,128]{2,1,0:T(8,128)S(1)}, u32[]{:S(2)}, u32[]{:S(2)}) collective-permute-start(f32[7,64,128]{2,1,0:T(8,128)S(1)} %get-tuple-element.53), channel_id=1, source_target_pairs={{0,160},{32,128},{64,224},{96,192},{128,32},{160,0},{192,96},{224,... | collective-permute-start | bytes 688136 | tf_op jit(solution)/shard_map/ppermute | solution.py:630
  11.2 0.0 collective-permute-done.3.refs_3_
  11.2 1.4 %collective-permute-start.6 = (f32[7,64,128]{2,1,0:T(8,128)S(1)}, f32[7,64,128]{2,1,0:T(8,128)S(1)}, u32[]{:S(2)}, u32[]{:S(2)}) collective-permute-start(f32[7,64,128]{2,1,0:T(8,128)S(1)} %get-tuple-element.54), channel_id=1, source_target_pairs={{0,192},{32,224},{64,0},{96,32},{128,64},{160,96},{192,128},{224,1... | collective-permute-start | bytes 688136 | tf_op jit(solution)/shard_map/ppermute | solution.py:630
  12.6 1.7 %collective-permute-done.1.refs_1_ = f32[7,64,128]{2,1,0:T(8,128)S(1)} collective-permute-done((f32[7,64,128]{2,1,0:T(8,128)S(1)}, f32[7,64,128]{2,1,0:T(8,128)S(1)}, u32[]{:S(2)}, u32[]{:S(2)}) %collective-permute-start.1) | collective-permute-done | bytes 229408 | tf_op jit(solution)/shard_map/ppermute | solution.py:630
  14.3 2.3 %collective-permute-start.7 = (f32[7,64,128]{2,1,0:T(8,128)S(1)}, f32[7,64,128]{2,1,0:T(8,128)S(1)}, u32[]{:S(2)}, u32[]{:S(2)}) collective-permute-start(f32[7,64,128]{2,1,0:T(8,128)S(1)} %get-tuple-element.55), channel_id=1, source_target_pairs={{0,224},{32,192},{64,32},{96,0},{128,96},{160,64},{192,160},{224,1... | collective-permute-start | bytes 688136 | tf_op jit(solution)/shard_map/ppermute | solution.py:630
  16.6 10.2 %collective-permute-done.4.refs_4_ = f32[7,64,128]{2,1,0:T(8,128)S(1)} collective-permute-done((f32[7,64,128]{2,1,0:T(8,128)S(1)}, f32[7,64,128]{2,1,0:T(8,128)S(1)}, u32[]{:S(2)}, u32[]{:S(2)}) %collective-permute-start.4) | collective-permute-done | bytes 229408 | tf_op jit(solution)/shard_map/ppermute | solution.py:630
  26.8 1.8 %collective-permute-done.6.refs_6_ = f32[7,64,128]{2,1,0:T(8,128)S(1)} collective-permute-done((f32[7,64,128]{2,1,0:T(8,128)S(1)}, f32[7,64,128]{2,1,0:T(8,128)S(1)}, u32[]{:S(2)}, u32[]{:S(2)}) %collective-permute-start.6) | collective-permute-done | bytes 229408 | tf_op jit(solution)/shard_map/ppermute | solution.py:630
  28.7 0.8 shard_map.31
  29.5 0.8 collective-permute-start.8
  30.3 3.6 %collective-permute-start.9 = (f32[7,64,128]{2,1,0:T(8,128)S(1)}, f32[7,64,128]{2,1,0:T(8,128)S(1)}, u32[]{:S(2)}, u32[]{:S(2)}) collective-permute-start(f32[7,64,128]{2,1,0:T(8,128)S(1)} %get-tuple-element.58), channel_id=1, source_target_pairs={{0,64},{32,96},{64,128},{96,160},{128,192},{160,224},{192,0},{224,... | collective-permute-start | bytes 688136 | tf_op jit(solution)/shard_map/ppermute | solution.py:644
  33.9 2.4 %collective-permute-start = (f32[17,8,128]{2,1,0:T(8,128)S(1)}, f32[17,8,128]{2,1,0:T(8,128)S(1)}, u32[]{:S(2)}, u32[]{:S(2)}) collective-permute-start(f32[17,8,128]{2,1,0:T(8,128)S(1)} %get-tuple-element.42), channel_id=1, source_target_pairs={{0,1},{1,0},{2,3},{3,2},{4,5},{5,4},{6,7},{7,6},{8,9},{9,8},{10,11... | collective-permute-start | bytes 208904 | tf_op jit(solution)/shard_map/ppermute | solution.py:626
  36.3 0.0 collective-permute-start.10
  36.3 0.9 collective-permute-start.11
  37.2 2.2 %collective-permute-done.halo_ref = f32[17,8,128]{2,1,0:T(8,128)S(1)} collective-permute-done((f32[17,8,128]{2,1,0:T(8,128)S(1)}, f32[17,8,128]{2,1,0:T(8,128)S(1)}, u32[]{:S(2)}, u32[]{:S(2)}) %collective-permute-start) | collective-permute-done | bytes 69664 | tf_op jit(solution)/shard_map/ppermute | solution.py:626
  39.3 1.1 collective-permute-start.12
  40.4 0.0 collective-permute-done.8.refs_1_
  40.4 3.8 %collective-permute-start.13 = (f32[7,64,128]{2,1,0:T(8,128)S(1)}, f32[7,64,128]{2,1,0:T(8,128)S(1)}, u32[]{:S(2)}, u32[]{:S(2)}) collective-permute-start(f32[7,64,128]{2,1,0:T(8,128)S(1)} %get-tuple-element.62), channel_id=1, source_target_pairs={{0,192},{32,224},{64,0},{96,32},{128,64},{160,96},{192,128},{224,1... | collective-permute-start | bytes 688136 | tf_op jit(solution)/shard_map/ppermute | solution.py:644
  44.2 0.0 collective-permute-done.9.refs_2_
  44.2 1.5 %collective-permute-start.14 = (f32[7,64,128]{2,1,0:T(8,128)S(1)}, f32[7,64,128]{2,1,0:T(8,128)S(1)}, u32[]{:S(2)}, u32[]{:S(2)}) collective-permute-start(f32[7,64,128]{2,1,0:T(8,128)S(1)} %get-tuple-element.63), channel_id=1, source_target_pairs={{0,224},{32,192},{64,32},{96,0},{128,96},{160,64},{192,160},{224,1... | collective-permute-start | bytes 688136 | tf_op jit(solution)/shard_map/ppermute | solution.py:644
  45.7 0.1 broadcast_in_dim.2.flag_ref
  45.9 3.5 %shard_map.30 = (f32[8,7,64,128]{3,2,1,0:T(8,128)S(1)}, f32[8,64,128]{2,1,0:T(8,128)S(1)}, f32[7,64,128]{2,1,0:T(8,128)S(1)}, f32[7,64,128]{2,1,0:T(8,128)S(1)},...) custom-call(f32[1,7,8,64,128]{4,3,2,1,0:T(8,128)} %source_ref.1, ...), custom_call_target="tpu_custom_call" | custom-call | flops 27525120 | bytes 7340032 | tf_op jit(solution)/shard_map/pallas_call | solution.py:580
  49.4 5.9 %collective-permute-done.11.refs_4_ = f32[7,64,128]{2,1,0:T(8,128)S(1)} collective-permute-done((f32[7,64,128]{2,1,0:T(8,128)S(1)}, f32[7,64,128]{2,1,0:T(8,128)S(1)}, u32[]{:S(2)}, u32[]{:S(2)}) %collective-permute-start.11) | collective-permute-done | bytes 229408 | tf_op jit(solution)/shard_map/ppermute | solution.py:644
  55.3 4.4 %collective-permute-done.13.refs_6_ = f32[7,64,128]{2,1,0:T(8,128)S(1)} collective-permute-done((f32[7,64,128]{2,1,0:T(8,128)S(1)}, f32[7,64,128]{2,1,0:T(8,128)S(1)}, u32[]{:S(2)}, u32[]{:S(2)}) %collective-permute-start.13) | collective-permute-done | bytes 229408 | tf_op jit(solution)/shard_map/ppermute | solution.py:644
  59.7 0.5 shard_map.32
  60.2 1.5 %collective-permute-start.15 = (f32[14,32,128]{2,1,0:T(8,128)S(1)}, f32[14,32,128]{2,1,0:T(8,128)S(1)}, u32[]{:S(2)}, u32[]{:S(2)}) collective-permute-start(f32[14,32,128]{2,1,0:T(8,128)S(1)} %get-tuple-element.66), channel_id=1, source_target_pairs={{0,2},{2,0},{4,6},{6,4},{8,10},{10,8},{12,14},{14,12},{16,18},{18,... | collective-permute-start | bytes 688136 | tf_op jit(solution)/shard_map/ppermute | solution.py:611
  61.7 0.1 collective-permute-start.16
  61.8 1.2 %collective-permute-done.16.got_ref = f32[5,32,128]{2,1,0:T(8,128)S(1)} collective-permute-done((f32[5,32,128]{2,1,0:T(8,128)S(1)}, f32[5,32,128]{2,1,0:T(8,128)S(1)}, u32[]{:S(2)}, u32[]{:S(2)}) %collective-permute-start.16) | collective-permute-done | bytes 81952 | tf_op jit(solution)/shard_map/ppermute | solution.py:611
  63.0 1.3 %collective-permute-start.17 = (f32[2,32,128]{2,1,0:T(8,128)S(1)}, f32[2,32,128]{2,1,0:T(8,128)S(1)}, u32[]{:S(2)}, u32[]{:S(2)}) collective-permute-start(f32[2,32,128]{2,1,0:T(8,128)S(1)} %get-tuple-element.71), channel_id=1, source_target_pairs={{4,0},{6,2},{8,4},{10,6},{12,8},{14,10},{16,12},{18,14},{20,16},{2... | collective-permute-start | bytes 98312 | tf_op jit(solution)/shard_map/ppermute | solution.py:615
  64.3 3.4 %collective-permute-done.17.ends_ref = f32[2,32,128]{2,1,0:T(8,128)S(1)} collective-permute-done((f32[2,32,128]{2,1,0:T(8,128)S(1)}, f32[2,32,128]{2,1,0:T(8,128)S(1)}, u32[]{:S(2)}, u32[]{:S(2)}) %collective-permute-start.17) | collective-permute-done | bytes 32800 | tf_op jit(solution)/shard_map/ppermute | solution.py:615
  67.7 3.5 %collective-permute-start.18 = (f32[1,32,128]{2,1,0:T(8,128)S(1)}, f32[1,32,128]{2,1,0:T(8,128)S(1)}, u32[]{:S(2)}, u32[]{:S(2)}) collective-permute-start(f32[1,32,128]{2,1,0:T(8,128)S(1)} %get-tuple-element.73), channel_id=1, source_target_pairs={{0,4},{2,6},{4,8},{6,10},{8,12},{10,14},{12,16},{14,18},{16,20},{1... | collective-permute-start | bytes 49160 | tf_op jit(solution)/shard_map/ppermute | solution.py:615
  71.2 0.9 collective-permute-done.18.edge_ref
  72.1 0.5 shard_map.33
  72.6 0.1 shard_map.37
  72.7 18.5 %all_to_all.10.rhs_ref = f32[8,16,4,128]{3,2,1,0:T(4,128)S(1)} all-to-all(f32[8,16,4,128]{3,2,1,0:T(4,128)S(1)} %get-tuple-element.74), channel_id=1, replica_groups={{0,4,8,12,16,20,24,28},{2,6,10,14,18,22,26,30},{1,5,9,13,17,21,25,29},{..., dimensions={0} | all-to-all | bytes 524288 | tf_op jit(solution)/shard_map/all_to_all | solution.py:594
  91.1 0.1 shard_map.38
  91.2 11.4 %all_to_all.11.solved_ref = f32[8,14,4,128]{3,2,1,0:T(4,128)S(1)} all-to-all(f32[8,14,4,128]{3,2,1,0:T(4,128)S(1)} %shard_map.38), channel_id=1, replica_groups={{0,4,8,12,16,20,24,28},{2,6,10,14,18,22,26,30},{1,5,9,13,17,21,25,29},{..., dimensions={0} | all-to-all | bytes 458752 | tf_op jit(solution)/shard_map/all_to_all | solution.py:594
  102.6 0.1 shard_map.39
  102.7 5.2 %collective-permute-start.19 = (f32[14,32,128]{2,1,0:T(8,128)S(1)}, f32[14,32,128]{2,1,0:T(8,128)S(1)}, u32[]{:S(2)}, u32[]{:S(2)}) collective-permute-start(f32[14,32,128]{2,1,0:T(8,128)S(1)} %get-tuple-element.76), channel_id=1, source_target_pairs={{0,2},{2,0},{4,6},{6,4},{8,10},{10,8},{12,14},{14,12},{16,18},{18,... | collective-permute-start | bytes 688136 | tf_op jit(solution)/shard_map/ppermute | solution.py:611
  108.0 1.0 shard_map.40.refs_0_
  109.0 0.1 collective-permute-done.19.ends_ref
  109.1 1.0 shard_map.41
  (12 shorter events, 0.1 us)
Async XLA Ops:
  1.0 44.8 %copy-start = (s32[1,8,64]{2,1,0:T(8,128)S(1)}, s32[1,8,64]{2,1,0:T(8,128)}, u32[]{:S(2)}) copy-start(s32[1,8,64]{2,1,0:T(8,128)} %flag_ref.1) | copy-start | bytes 6148
  1.0 10.2 %collective-permute-start.3 = (f32[7,64,128]{2,1,0:T(8,128)S(1)}, f32[7,64,128]{2,1,0:T(8,128)S(1)}, u32[]{:S(2)}, u32[]{:S(2)}) collective-permute-start(f32[7,64,128]{2,1,0:T(8,128)S(1)} %shard_map.28.early_ref), channel_id=1, source_target_pairs={{0,96},{32,64},{64,160},{96,128},{128,224},{160,192},{192,32},{224... | collective-permute-start | bytes 688136 | tf_op jit(solution)/shard_map/ppermute | solution.py:630
  5.7 8.6 %collective-permute-start.1 = (f32[7,64,128]{2,1,0:T(8,128)S(1)}, f32[7,64,128]{2,1,0:T(8,128)S(1)}, u32[]{:S(2)}, u32[]{:S(2)}) collective-permute-start(f32[7,64,128]{2,1,0:T(8,128)S(1)} %get-tuple-element.50), channel_id=1, source_target_pairs={{0,32},{32,0},{64,96},{96,64},{128,160},{160,128},{192,224},{224,1... | collective-permute-start | bytes 688136 | tf_op jit(solution)/shard_map/ppermute | solution.py:630
  6.0 10.6 %collective-permute-start.2 = (f32[7,64,128]{2,1,0:T(8,128)S(1)}, f32[7,64,128]{2,1,0:T(8,128)S(1)}, u32[]{:S(2)}, u32[]{:S(2)}) collective-permute-start(f32[7,64,128]{2,1,0:T(8,128)S(1)} %get-tuple-element.51), channel_id=1, source_target_pairs={{0,64},{32,96},{64,128},{96,160},{128,192},{160,224},{192,0},{224,... | collective-permute-start | bytes 688136 | tf_op jit(solution)/shard_map/ppermute | solution.py:630
  7.3 19.5 %collective-permute-start.4 = (f32[7,64,128]{2,1,0:T(8,128)S(1)}, f32[7,64,128]{2,1,0:T(8,128)S(1)}, u32[]{:S(2)}, u32[]{:S(2)}) collective-permute-start(f32[7,64,128]{2,1,0:T(8,128)S(1)} %get-tuple-element.52), channel_id=1, source_target_pairs={{0,128},{32,160},{64,192},{96,224},{128,0},{160,32},{192,64},{224,... | collective-permute-start | bytes 688136 | tf_op jit(solution)/shard_map/ppermute | solution.py:630
  8.7 18.1 %collective-permute-start.5 = (f32[7,64,128]{2,1,0:T(8,128)S(1)}, f32[7,64,128]{2,1,0:T(8,128)S(1)}, u32[]{:S(2)}, u32[]{:S(2)}) collective-permute-start(f32[7,64,128]{2,1,0:T(8,128)S(1)} %get-tuple-element.53), channel_id=1, source_target_pairs={{0,160},{32,128},{64,224},{96,192},{128,32},{160,0},{192,96},{224,... | collective-permute-start | bytes 688136 | tf_op jit(solution)/shard_map/ppermute | solution.py:630
  11.2 17.5 %collective-permute-start.6 = (f32[7,64,128]{2,1,0:T(8,128)S(1)}, f32[7,64,128]{2,1,0:T(8,128)S(1)}, u32[]{:S(2)}, u32[]{:S(2)}) collective-permute-start(f32[7,64,128]{2,1,0:T(8,128)S(1)} %get-tuple-element.54), channel_id=1, source_target_pairs={{0,192},{32,224},{64,0},{96,32},{128,64},{160,96},{192,128},{224,1... | collective-permute-start | bytes 688136 | tf_op jit(solution)/shard_map/ppermute | solution.py:630
  14.3 14.4 %collective-permute-start.7 = (f32[7,64,128]{2,1,0:T(8,128)S(1)}, f32[7,64,128]{2,1,0:T(8,128)S(1)}, u32[]{:S(2)}, u32[]{:S(2)}) collective-permute-start(f32[7,64,128]{2,1,0:T(8,128)S(1)} %get-tuple-element.55), channel_id=1, source_target_pairs={{0,224},{32,192},{64,32},{96,0},{128,96},{160,64},{192,160},{224,1... | collective-permute-start | bytes 688136 | tf_op jit(solution)/shard_map/ppermute | solution.py:630
  29.5 10.9 %collective-permute-start.8 = (f32[7,64,128]{2,1,0:T(8,128)S(1)}, f32[7,64,128]{2,1,0:T(8,128)S(1)}, u32[]{:S(2)}, u32[]{:S(2)}) collective-permute-start(f32[7,64,128]{2,1,0:T(8,128)S(1)} %get-tuple-element.57), channel_id=1, source_target_pairs={{0,32},{32,0},{64,96},{96,64},{128,160},{160,128},{192,224},{224,1... | collective-permute-start | bytes 688136 | tf_op jit(solution)/shard_map/ppermute | solution.py:644
  30.3 13.9 %collective-permute-start.9 = (f32[7,64,128]{2,1,0:T(8,128)S(1)}, f32[7,64,128]{2,1,0:T(8,128)S(1)}, u32[]{:S(2)}, u32[]{:S(2)}) collective-permute-start(f32[7,64,128]{2,1,0:T(8,128)S(1)} %get-tuple-element.58), channel_id=1, source_target_pairs={{0,64},{32,96},{64,128},{96,160},{128,192},{160,224},{192,0},{224,... | collective-permute-start | bytes 688136 | tf_op jit(solution)/shard_map/ppermute | solution.py:644
  33.9 5.4 %collective-permute-start = (f32[17,8,128]{2,1,0:T(8,128)S(1)}, f32[17,8,128]{2,1,0:T(8,128)S(1)}, u32[]{:S(2)}, u32[]{:S(2)}) collective-permute-start(f32[17,8,128]{2,1,0:T(8,128)S(1)} %get-tuple-element.42), channel_id=1, source_target_pairs={{0,1},{1,0},{2,3},{3,2},{4,5},{5,4},{6,7},{7,6},{8,9},{9,8},{10,11... | collective-permute-start | bytes 208904 | tf_op jit(solution)/shard_map/ppermute | solution.py:626
  36.3 13.1 %collective-permute-start.10 = (f32[7,64,128]{2,1,0:T(8,128)S(1)}, f32[7,64,128]{2,1,0:T(8,128)S(1)}, u32[]{:S(2)}, u32[]{:S(2)}) collective-permute-start(f32[7,64,128]{2,1,0:T(8,128)S(1)} %get-tuple-element.59), channel_id=1, source_target_pairs={{0,96},{32,64},{64,160},{96,128},{128,224},{160,192},{192,32},{224... | collective-permute-start | bytes 688136 | tf_op jit(solution)/shard_map/ppermute | solution.py:644
  36.3 19.0 %collective-permute-start.11 = (f32[7,64,128]{2,1,0:T(8,128)S(1)}, f32[7,64,128]{2,1,0:T(8,128)S(1)}, u32[]{:S(2)}, u32[]{:S(2)}) collective-permute-start(f32[7,64,128]{2,1,0:T(8,128)S(1)} %get-tuple-element.60), channel_id=1, source_target_pairs={{0,128},{32,160},{64,192},{96,224},{128,0},{160,32},{192,64},{224,... | collective-permute-start | bytes 688136 | tf_op jit(solution)/shard_map/ppermute | solution.py:644
  39.3 16.0 %collective-permute-start.12 = (f32[7,64,128]{2,1,0:T(8,128)S(1)}, f32[7,64,128]{2,1,0:T(8,128)S(1)}, u32[]{:S(2)}, u32[]{:S(2)}) collective-permute-start(f32[7,64,128]{2,1,0:T(8,128)S(1)} %get-tuple-element.61), channel_id=1, source_target_pairs={{0,160},{32,128},{64,224},{96,192},{128,32},{160,0},{192,96},{224,... | collective-permute-start | bytes 688136 | tf_op jit(solution)/shard_map/ppermute | solution.py:644
  40.4 19.2 %collective-permute-start.13 = (f32[7,64,128]{2,1,0:T(8,128)S(1)}, f32[7,64,128]{2,1,0:T(8,128)S(1)}, u32[]{:S(2)}, u32[]{:S(2)}) collective-permute-start(f32[7,64,128]{2,1,0:T(8,128)S(1)} %get-tuple-element.62), channel_id=1, source_target_pairs={{0,192},{32,224},{64,0},{96,32},{128,64},{160,96},{192,128},{224,1... | collective-permute-start | bytes 688136 | tf_op jit(solution)/shard_map/ppermute | solution.py:644
  44.2 15.5 %collective-permute-start.14 = (f32[7,64,128]{2,1,0:T(8,128)S(1)}, f32[7,64,128]{2,1,0:T(8,128)S(1)}, u32[]{:S(2)}, u32[]{:S(2)}) collective-permute-start(f32[7,64,128]{2,1,0:T(8,128)S(1)} %get-tuple-element.63), channel_id=1, source_target_pairs={{0,224},{32,192},{64,32},{96,0},{128,96},{160,64},{192,160},{224,1... | collective-permute-start | bytes 688136 | tf_op jit(solution)/shard_map/ppermute | solution.py:644
  60.2 12.4 %collective-permute-start.15 = (f32[14,32,128]{2,1,0:T(8,128)S(1)}, f32[14,32,128]{2,1,0:T(8,128)S(1)}, u32[]{:S(2)}, u32[]{:S(2)}) collective-permute-start(f32[14,32,128]{2,1,0:T(8,128)S(1)} %get-tuple-element.66), channel_id=1, source_target_pairs={{0,2},{2,0},{4,6},{6,4},{8,10},{10,8},{12,14},{14,12},{16,18},{18,... | collective-permute-start | bytes 688136 | tf_op jit(solution)/shard_map/ppermute | solution.py:611
  61.7 1.3 %collective-permute-start.16 = (f32[5,32,128]{2,1,0:T(8,128)S(1)}, f32[5,32,128]{2,1,0:T(8,128)S(1)}, u32[]{:S(2)}, u32[]{:S(2)}) collective-permute-start(f32[5,32,128]{2,1,0:T(8,128)S(1)} %get-tuple-element.68), channel_id=1, source_target_pairs={{0,2},{2,0},{4,6},{6,4},{8,10},{10,8},{12,14},{14,12},{16,18},{18,... | collective-permute-start | bytes 245768 | tf_op jit(solution)/shard_map/ppermute | solution.py:611
  63.0 4.7 %collective-permute-start.17 = (f32[2,32,128]{2,1,0:T(8,128)S(1)}, f32[2,32,128]{2,1,0:T(8,128)S(1)}, u32[]{:S(2)}, u32[]{:S(2)}) collective-permute-start(f32[2,32,128]{2,1,0:T(8,128)S(1)} %get-tuple-element.71), channel_id=1, source_target_pairs={{4,0},{6,2},{8,4},{10,6},{12,8},{14,10},{16,12},{18,14},{20,16},{2... | collective-permute-start | bytes 98312 | tf_op jit(solution)/shard_map/ppermute | solution.py:615
  67.7 4.4 %collective-permute-start.18 = (f32[1,32,128]{2,1,0:T(8,128)S(1)}, f32[1,32,128]{2,1,0:T(8,128)S(1)}, u32[]{:S(2)}, u32[]{:S(2)}) collective-permute-start(f32[1,32,128]{2,1,0:T(8,128)S(1)} %get-tuple-element.73), channel_id=1, source_target_pairs={{0,4},{2,6},{4,8},{6,10},{8,12},{10,14},{12,16},{14,18},{16,20},{1... | collective-permute-start | bytes 49160 | tf_op jit(solution)/shard_map/ppermute | solution.py:615
  102.7 6.4 %collective-permute-start.19 = (f32[14,32,128]{2,1,0:T(8,128)S(1)}, f32[14,32,128]{2,1,0:T(8,128)S(1)}, u32[]{:S(2)}, u32[]{:S(2)}) collective-permute-start(f32[14,32,128]{2,1,0:T(8,128)S(1)} %get-tuple-element.76), channel_id=1, source_target_pairs={{0,2},{2,0},{4,6},{6,4},{8,10},{10,8},{12,14},{14,12},{16,18},{18,... | collective-permute-start | bytes 688136 | tf_op jit(solution)/shard_map/ppermute | solution.py:611

commit v4 on v3

--- a/solution.py
+++ b/solution.py
@@ -20,7 +20,7 @@
 NU_T = 0.25
 
 FIELDS = 7
-ORDER = (3, 4, 5, 7, 1, 2, 6)
+ORDER = (5, 7, 3, 4, 1, 2, 6)
 EDGES = 2 * FIELDS + 3
 COEFS = 5
 TILE = 8
@@ -360,19 +360,32 @@
     ends_ref[1] = -(w_a * w)
 
 
-def link_kernel(raw_ref, ends_ref, link_ref, edge_ref):
+def link_kernel(raw_ref, ends_ref, link_ref, edge_ref, table_ref):
+    count, _, piece, _ = table_ref.shape
     sep = raw_ref[2]
     scale = 1.0 / (raw_ref[0] - sep * ends_ref[0])
     link_ref[0] = scale
-    link_ref[1] = raw_ref[1] * scale
-    link_ref[2] = -(sep * ends_ref[1]) * scale
     edge_ref[0] = sep * scale
+    lower, upper = raw_ref[1] * scale, -(sep * ends_ref[1]) * scale
+    for q in range(count):
+        table_ref[q, 0] = lower[q * piece : (q + 1) * piece]
+        table_ref[q, 1] = upper[q * piece : (q + 1) * piece]
+
+
+def factor_kernel(table_ref, out_ref):
+    ratio = None
+    for p in range(table_ref.shape[0]):
+        lower, upper = table_ref[p, 0], table_ref[p, 1]
+        inv = 1.0 / (1.0 - lower * ratio) if p else jnp.ones_like(lower)
+        ratio = upper * inv
+        out_ref[p, 0] = lower
+        out_ref[p, 1] = inv
+        out_ref[p, 2] = ratio
 
 
 def join_kernel(link_ref, edge_ref, out_ref):
-    for k in range(3):
-        out_ref[k] = link_ref[k]
-    out_ref[3] = edge_ref[0]
+    out_ref[0] = link_ref[0]
+    out_ref[1] = edge_ref[0]
 
 
 def half_of(mine):
@@ -432,7 +445,7 @@
     def step(t, _):
         span = pl.ds(pl.multiple_of(t * TILE, TILE), TILE)
         inv, sep_a, first_a, lower_b = (pair_ref[k, span] for k in range(4))
-        scale, lower, upper, edge = (link_ref[k, span] for k in range(4))
+        scale, edge = link_ref[0, span], link_ref[1, span]
         for f in range(fields):
             keep_y, got_y = keep_ref[f, span], got_ref[f, span]
             keep_own, got_own = keep_ref[fields + f, span], got_ref[fields + f, span]
@@ -448,28 +461,22 @@
             ):
                 out_ref[2 * t, k] = x[0:4]
                 out_ref[2 * t + 1, k] = x[4:8]
-        for k, x in ((2 * fields, lower), (2 * fields + 1, upper)):
-            out_ref[2 * t, k] = x[0:4]
-            out_ref[2 * t + 1, k] = x[4:8]
         return 0
 
     lax.fori_loop(0, rows // TILE, step, 0)
 
 
-def reduced_kernel(rhs_ref, out_ref):
+def reduced_kernel(table_ref, rhs_ref, out_ref):
     count = rhs_ref.shape[0]
     fields = out_ref.shape[1] // 2
-    ratio = []
+    ratio = [table_ref[p, 2] for p in range(count)]
     values = []
     for p in range(count):
-        lower, upper = rhs_ref[p, 2 * fields], rhs_ref[p, 2 * fields + 1]
-        more = p + 1 < count
-        inv = 1.0 / (1.0 - lower * ratio[-1]) if p else jnp.ones_like(lower)
-        ratio.append(upper * inv)
+        lower, inv = table_ref[p, 0], table_ref[p, 1]
         row = []
         for f in range(fields):
             right = rhs_ref[p, f]
-            if more:
+            if p + 1 < count:
                 right = right - rhs_ref[p + 1, fields + f]
             if p:
                 right = right - lower * values[-1][f]
@@ -638,12 +645,16 @@
         pair_kernel, [(6,) + thin, (3,) + thin, (2,) + thin], keep, partner(send)
     )
     ends = neighbour(ends, -1)
-    link, edge = call(link_kernel, [(3,) + thin, (1,) + thin], raw, ends)
+    link, edge, table = call(
+        link_kernel, [(1,) + thin, (1,) + thin, (chips, 2, piece, lanes)], raw, ends
+    )
     specs = call(spectral_kernel, [blocks[0].shape] * instances, *blocks, flops=own.size * 9)
     for k in order:
         specs[k] = lax.ppermute(specs[k], "inst", route(*steps[k], instances))
+    table = exchange(table, "ax", groups)
+    (table,) = call(factor_kernel, [(chips, 3, piece, lanes)], table)
     edge = neighbour(edge, 1)
-    (link,) = call(join_kernel, [(4,) + thin], link, edge)
+    (link,) = call(join_kernel, [(2,) + thin], link, edge)
     shapes = [(planes - 1, FIELDS, half, lanes), (2 * FIELDS, half, lanes)]
     parts = []
     for mine in (False, True):
@@ -662,7 +673,7 @@
     (y_other, send), (y_mine, keep) = parts
     inner, rhs = call(
         merge_kernel,
-        [(FIELDS, half, lanes), (chips, 2 * FIELDS + 2, piece, lanes)],
+        [(FIELDS, half, lanes), (chips, 2 * FIELDS, piece, lanes)],
         keep,
         partner(send),
         pair,
@@ -671,7 +682,7 @@
     )
     rhs = exchange(rhs, "ax", groups)
     (solved,) = call(
-        reduced_kernel, [(chips, 2 * FIELDS, piece, lanes)], rhs, flops=rhs.size * 8
+        reduced_kernel, [(chips, 2 * FIELDS, piece, lanes)], table, rhs, flops=rhs.size * 8
     )
     solved = exchange(solved, "ax", groups)
     keep, send = call(

time: 111 us -> 130 us (1.17)
  blocking collectives: 29.9 us -> 11.4 us
  starting transfers between devices: 38.1 us -> 52.1 us
  waiting for transfers between devices: 31.7 us -> 42.9 us
  local copies, waits for them, and re-layouts: 0.13 us -> 9.76 us
  Pallas kernels: 10.2 us -> 13.3 us
    all_to_all x2 -> x1, blocking collectives: 29.9 us -> 11.4 us  [exchange(): return lax.all_to_all(x, axis, 0, 0, tiled=True, axis_index_groups=groups)]
    all_to_all x0 -> x2, starting transfers between devices: none -> 16.1 us  [exchange(): return lax.all_to_all(x, axis, 0, 0, tiled=True, axis_index_groups=groups)]
    unnamed x2 -> x40, local copies, waits for them, and re-layouts: 0.01 us -> 9.64 us
    all_to_all x0 -> x2, waiting for transfers between devices: none -> 9.04 us  [exchange(): return lax.all_to_all(x, axis, 0, 0, tiled=True, axis_index_groups=groups)]
    ppermute x7, starting transfers between devices: 11.7 us -> 7.17 us  [body(): specs[k] = lax.ppermute(specs[k], 'inst', route(*steps[k], instances))]
    ppermute x3, starting transfers between devices: 6.85 us -> 10.4 us  [partner(): return lax.ppermute(x, 'ax', swap)]
    pallas_call x9 -> x10, Pallas kernels: 2.12 us -> 5.25 us  [call(): return list(run(*operands))]
  transfers between devices with their start and end apart: 20 -> 22, of which waited for: 10 -> 10; matrix products, arithmetic and copies ran while one was open for 0% -> 0% of each run, Pallas kernels for 6% -> 6%
where the time goes in v4:
time: 130 us
  starting transfers between devices  52.1 us (40%)
  waiting for transfers between devices  42.9 us (33%)
  Pallas kernels  13.3 us (10%)
  blocking collectives  11.4 us (9%)
  local copies, waits for them, and re-layouts  9.76 us (8%)
    all_to_all x2, starting transfers between devices, exchange(): return lax.all_to_all(x, axis, 0, 0, tiled=True, axis_index_groups=groups)  16.1 us
    ppermute x7, waiting for transfers between devices, body(): blocks[k] = lax.ppermute(blocks[k], 'inst', route(*steps[k], instances))  14.6 us
    all_to_all x1, blocking collectives, exchange(): return lax.all_to_all(x, axis, 0, 0, tiled=True, axis_index_groups=groups)  11.4 us
    ppermute x7, starting transfers between devices, body(): blocks[k] = lax.ppermute(blocks[k], 'inst', route(*steps[k], instances))  11.4 us
    ppermute x7, waiting for transfers between devices, body(): specs[k] = lax.ppermute(specs[k], 'inst', route(*steps[k], instances))  10.8 us
    ppermute x3, starting transfers between devices, partner(): return lax.ppermute(x, 'ax', swap)  10.4 us
    unnamed x40, local copies, waits for them, and re-layouts  9.64 us
    all_to_all x2, waiting for transfers between devices, exchange(): return lax.all_to_all(x, axis, 0, 0, tiled=True, axis_index_groups=groups)  9.04 us
  transfers between devices with their start and end apart: 22, of which 10 were waited for; matrix products, arithmetic and copies ran while one was open for 0% of the time, Pallas kernels for 6%

profile of v4, /device:TPU:1, one launch (start us, length us, event | category | flops | bytes accessed | tf_op | source)
XLA Modules:
  0.0 129.7 jit_solution(14387580520441410858)
XLA Ops:
  0.0 0.9 shard_map.28.early_ref
  1.0 1.6 %shard_map.29 = (f32[7,64,128]{2,1,0:T(8,128)S(1)}, f32[7,64,128]{2,1,0:T(8,128)S(1)}, f32[7,64,128]{2,1,0:T(8,128)S(1)}, f32[7,64,128]{2,1,0:T(8,128)S(1)}, f32...) custom-call(f32[1,7,8,64,128]{4,3,2,1,0:T(8,128)} %source_ref.1, ...), custom_call_target="tpu_custom_call" | custom-call | bytes 3670016 | tf_op jit(solution)/shard_map/pallas_call | solution.py:145
  2.6 2.1 %collective-permute-start.1 = (f32[7,64,128]{2,1,0:T(8,128)S(1)}, f32[7,64,128]{2,1,0:T(8,128)S(1)}, u32[]{:S(2)}, u32[]{:S(2)}) collective-permute-start(f32[7,64,128]{2,1,0:T(8,128)S(1)} %get-tuple-element.51), channel_id=1, source_target_pairs={{0,32},{32,0},{64,96},{96,64},{128,160},{160,128},{192,224},{224,1... | collective-permute-start | bytes 688136 | tf_op jit(solution)/shard_map/ppermute | solution.py:637
  4.7 1.3 collective-permute-start.2
  6.0 1.3 collective-permute-start.3
  7.2 1.4 %collective-permute-start.4 = (f32[7,64,128]{2,1,0:T(8,128)S(1)}, f32[7,64,128]{2,1,0:T(8,128)S(1)}, u32[]{:S(2)}, u32[]{:S(2)}) collective-permute-start(f32[7,64,128]{2,1,0:T(8,128)S(1)} %get-tuple-element.54), channel_id=1, source_target_pairs={{0,128},{32,160},{64,192},{96,224},{128,0},{160,32},{192,64},{224,... | collective-permute-start | bytes 688136 | tf_op jit(solution)/shard_map/ppermute | solution.py:637
  8.6 2.0 %collective-permute-start.6 = (f32[7,64,128]{2,1,0:T(8,128)S(1)}, f32[7,64,128]{2,1,0:T(8,128)S(1)}, u32[]{:S(2)}, u32[]{:S(2)}) collective-permute-start(f32[7,64,128]{2,1,0:T(8,128)S(1)} %get-tuple-element.55), channel_id=1, source_target_pairs={{0,192},{32,224},{64,0},{96,32},{128,64},{160,96},{192,128},{224,1... | collective-permute-start | bytes 688136 | tf_op jit(solution)/shard_map/ppermute | solution.py:637
  10.6 3.0 %collective-permute-start.7 = (f32[7,64,128]{2,1,0:T(8,128)S(1)}, f32[7,64,128]{2,1,0:T(8,128)S(1)}, u32[]{:S(2)}, u32[]{:S(2)}) collective-permute-start(f32[7,64,128]{2,1,0:T(8,128)S(1)} %get-tuple-element.56), channel_id=1, source_target_pairs={{0,224},{32,192},{64,32},{96,0},{128,96},{160,64},{192,160},{224,1... | collective-permute-start | bytes 688136 | tf_op jit(solution)/shard_map/ppermute | solution.py:637
  13.9 3.4 %collective-permute-done.3.refs_3_ = f32[7,64,128]{2,1,0:T(8,128)S(1)} collective-permute-done((f32[7,64,128]{2,1,0:T(8,128)S(1)}, f32[7,64,128]{2,1,0:T(8,128)S(1)}, u32[]{:S(2)}, u32[]{:S(2)}) %collective-permute-start.3) | collective-permute-done | bytes 229408 | tf_op jit(solution)/shard_map/ppermute | solution.py:637
  17.4 6.3 %collective-permute-done.4.refs_4_ = f32[7,64,128]{2,1,0:T(8,128)S(1)} collective-permute-done((f32[7,64,128]{2,1,0:T(8,128)S(1)}, f32[7,64,128]{2,1,0:T(8,128)S(1)}, u32[]{:S(2)}, u32[]{:S(2)}) %collective-permute-start.4) | collective-permute-done | bytes 229408 | tf_op jit(solution)/shard_map/ppermute | solution.py:637
  23.7 4.8 %collective-permute-done.6.refs_6_ = f32[7,64,128]{2,1,0:T(8,128)S(1)} collective-permute-done((f32[7,64,128]{2,1,0:T(8,128)S(1)}, f32[7,64,128]{2,1,0:T(8,128)S(1)}, u32[]{:S(2)}, u32[]{:S(2)}) %collective-permute-start.6) | collective-permute-done | bytes 229408 | tf_op jit(solution)/shard_map/ppermute | solution.py:637
  28.5 0.8 shard_map.31
  29.3 3.4 %collective-permute-start.10 = (f32[7,64,128]{2,1,0:T(8,128)S(1)}, f32[7,64,128]{2,1,0:T(8,128)S(1)}, u32[]{:S(2)}, u32[]{:S(2)}) collective-permute-start(f32[7,64,128]{2,1,0:T(8,128)S(1)} %get-tuple-element.60), channel_id=1, source_target_pairs={{0,96},{32,64},{64,160},{96,128},{128,224},{160,192},{192,32},{224... | collective-permute-start | bytes 688136 | tf_op jit(solution)/shard_map/ppermute | solution.py:653
  32.8 2.2 %collective-permute-start.11 = (f32[7,64,128]{2,1,0:T(8,128)S(1)}, f32[7,64,128]{2,1,0:T(8,128)S(1)}, u32[]{:S(2)}, u32[]{:S(2)}) collective-permute-start(f32[7,64,128]{2,1,0:T(8,128)S(1)} %get-tuple-element.61), channel_id=1, source_target_pairs={{0,128},{32,160},{64,192},{96,224},{128,0},{160,32},{192,64},{224,... | collective-permute-start | bytes 688136 | tf_op jit(solution)/shard_map/ppermute | solution.py:653
  35.0 2.5 %collective-permute-start = (f32[17,8,128]{2,1,0:T(8,128)S(1)}, f32[17,8,128]{2,1,0:T(8,128)S(1)}, u32[]{:S(2)}, u32[]{:S(2)}) collective-permute-start(f32[17,8,128]{2,1,0:T(8,128)S(1)} %get-tuple-element.43), channel_id=1, source_target_pairs={{0,1},{1,0},{2,3},{3,2},{4,5},{5,4},{6,7},{7,6},{8,9},{9,8},{10,11... | collective-permute-start | bytes 208904 | tf_op jit(solution)/shard_map/ppermute | solution.py:633
  37.8 0.9 collective-permute-start.13
  38.7 2.7 %collective-permute-done.halo_ref = f32[17,8,128]{2,1,0:T(8,128)S(1)} collective-permute-done((f32[17,8,128]{2,1,0:T(8,128)S(1)}, f32[17,8,128]{2,1,0:T(8,128)S(1)}, u32[]{:S(2)}, u32[]{:S(2)}) %collective-permute-start) | collective-permute-done | bytes 69664 | tf_op jit(solution)/shard_map/ppermute | solution.py:633
  41.6 9.3 %collective-permute-done.11.refs_4_ = f32[7,64,128]{2,1,0:T(8,128)S(1)} collective-permute-done((f32[7,64,128]{2,1,0:T(8,128)S(1)}, f32[7,64,128]{2,1,0:T(8,128)S(1)}, u32[]{:S(2)}, u32[]{:S(2)}) %collective-permute-start.11) | collective-permute-done | bytes 229408 | tf_op jit(solution)/shard_map/ppermute | solution.py:653
  51.0 3.5 %shard_map.30 = (f32[8,7,64,128]{3,2,1,0:T(8,128)S(1)}, f32[8,64,128]{2,1,0:T(8,128)S(1)}, f32[7,64,128]{2,1,0:T(8,128)S(1)}, f32[7,64,128]{2,1,0:T(8,128)S(1)},...) custom-call(f32[1,7,8,64,128]{4,3,2,1,0:T(8,128)} %source_ref.1, ...), custom_call_target="tpu_custom_call" | custom-call | flops 27525120 | bytes 7340032 | tf_op jit(solution)/shard_map/pallas_call | solution.py:587
  54.6 1.2 copy-done
  55.8 0.7 copy-done.8
  56.5 1.5 %collective-permute-done.9.refs_2_ = f32[7,64,128]{2,1,0:T(8,128)S(1)} collective-permute-done((f32[7,64,128]{2,1,0:T(8,128)S(1)}, f32[7,64,128]{2,1,0:T(8,128)S(1)}, u32[]{:S(2)}, u32[]{:S(2)}) %collective-permute-start.9) | collective-permute-done | bytes 229408 | tf_op jit(solution)/shard_map/ppermute | solution.py:653
  58.0 1.2 shard_map.32
  59.2 0.9 copy-done.14
  60.1 4.6 %collective-permute-start.17 = (f32[14,32,128]{2,1,0:T(8,128)}, f32[14,32,128]{2,1,0:T(8,128)}, u32[]{:S(2)}, u32[]{:S(2)}) collective-permute-start(f32[14,32,128]{2,1,0:T(8,128)} %get-tuple-element.72), channel_id=1, source_target_pairs={{0,2},{2,0},{4,6},{6,4},{8,10},{10,8},{12,14},{14,12},{16,18},{18,... | collective-permute-start | bytes 688136 | tf_op jit(solution)/shard_map/ppermute | solution.py:618
  64.7 1.5 %collective-permute-done.15.got_ref = f32[5,32,128]{2,1,0:T(8,128)S(1)} collective-permute-done((f32[5,32,128]{2,1,0:T(8,128)S(1)}, f32[5,32,128]{2,1,0:T(8,128)S(1)}, u32[]{:S(2)}, u32[]{:S(2)}) %collective-permute-start.15) | collective-permute-done | bytes 81952 | tf_op jit(solution)/shard_map/ppermute | solution.py:618
  66.2 0.6 copy-done.16
  66.8 1.3 collective-permute-start.16
  68.1 3.5 %collective-permute-done.16.ends_ref = f32[2,32,128]{2,1,0:T(8,128)S(1)} collective-permute-done((f32[2,32,128]{2,1,0:T(8,128)S(1)}, f32[2,32,128]{2,1,0:T(8,128)S(1)}, u32[]{:S(2)}, u32[]{:S(2)}) %collective-permute-start.16) | collective-permute-done | bytes 32800 | tf_op jit(solution)/shard_map/ppermute | solution.py:622
  71.6 0.6 shard_map.34
  72.3 8.0 %all-to-all-start = ((f32[8,2,4,128]{3,2,1,0:T(4,128)}), f32[8,2,4,128]{3,2,1,0:T(4,128)S(1)}, u32[]{:S(2)}, u32[]{:S(2)}) async-start(f32[8,2,4,128]{3,2,1,0:T(4,128)} %get-tuple-element.70), calls=%async_computation | async-start | bytes 65536 | tf_op jit(solution)/shard_map/all_to_all | solution.py:601
  80.3 3.4 %collective-permute-start.18 = (f32[1,32,128]{2,1,0:T(8,128)S(1)}, f32[1,32,128]{2,1,0:T(8,128)S(1)}, u32[]{:S(2)}, u32[]{:S(2)}) collective-permute-start(f32[1,32,128]{2,1,0:T(8,128)S(1)} %get-tuple-element.75), channel_id=1, source_target_pairs={{0,4},{2,6},{4,8},{6,10},{8,12},{10,14},{12,16},{14,18},{16,20},{1... | collective-permute-start | bytes 49160 | tf_op jit(solution)/shard_map/ppermute | solution.py:622
  83.6 0.9 collective-permute-done.18.edge_ref
  84.5 0.9 copy-done.3
  85.4 0.9 copy-done.5
  86.4 0.9 copy-done.7
  87.3 0.5 shard_map.36
  87.8 0.9 copy-done.12
  88.7 1.9 %shard_map.38 = (f32[7,32,128]{2,1,0:T(8,128)S(1)}, f32[8,14,4,128]{3,2,1,0:T(4,128)}) custom-call(f32[14,32,128]{2,1,0:T(8,128)S(1)} %get-tuple-element.71.keep_ref, f32[14,32,128]{2,1,0:T(8,128)} %collective-permute-done.17.got_ref, f32[6,32,128]{2,1,0:T(8,128)S(1)} %copy-done.17, f32[2,32,128]{2,1,0:T(8,128)S(1)} %shard_map.37.link_ref), custom_call_target="tpu_custom_call" | custom-call | flops 229376 | bytes 933888 | tf_op jit(solution)/shard_map/pallas_call | solution.py:64
  90.6 8.1 %all-to-all-start.1 = ((f32[8,14,4,128]{3,2,1,0:T(4,128)}), f32[8,14,4,128]{3,2,1,0:T(4,128)S(1)}, u32[]{:S(2)}, u32[]{:S(2)}) async-start(f32[8,14,4,128]{3,2,1,0:T(4,128)} %get-tuple-element.76), calls=%async_computation.1 | async-start | bytes 458752 | tf_op jit(solution)/shard_map/all_to_all | solution.py:601
  98.8 9.0 %all-to-all-done.1.rhs_ref = f32[8,14,4,128]{3,2,1,0:T(4,128)S(1)} async-done(((f32[8,14,4,128]{3,2,1,0:T(4,128)}), f32[8,14,4,128]{3,2,1,0:T(4,128)S(1)}, u32[]{:S(2)}, u32[]{:S(2)}) %all-to-all-start.1) | async-done | bytes 229408 | tf_op jit(solution)/shard_map/all_to_all | solution.py:601
  107.9 11.4 %all_to_all.15.solved_ref = f32[8,14,4,128]{3,2,1,0:T(4,128)S(1)} all-to-all(f32[8,14,4,128]{3,2,1,0:T(4,128)S(1)} %shard_map.39), channel_id=1, replica_groups={{0,4,8,12,16,20,24,28},{2,6,10,14,18,22,26,30},{1,5,9,13,17,21,25,29},{..., dimensions={0} | all-to-all | bytes 458752 | tf_op jit(solution)/shard_map/all_to_all | solution.py:601
  119.3 0.9 copy-done.18
  120.3 5.8 %collective-permute-start.19 = (f32[14,32,128]{2,1,0:T(8,128)S(1)}, f32[14,32,128]{2,1,0:T(8,128)S(1)}, u32[]{:S(2)}, u32[]{:S(2)}) collective-permute-start(f32[14,32,128]{2,1,0:T(8,128)S(1)} %get-tuple-element.78), channel_id=1, source_target_pairs={{0,2},{2,0},{4,6},{6,4},{8,10},{10,8},{12,14},{14,12},{16,18},{18,... | collective-permute-start | bytes 688136 | tf_op jit(solution)/shard_map/ppermute | solution.py:618
  126.1 1.1 copy-done.13
  127.2 1.0 shard_map.41.refs_0_
  128.2 0.4 copy-done.15
  128.7 1.0 shard_map.42
  (54 shorter events, 1.4 us)
Async XLA Ops:
  1.0 50.0 %copy-start.19 = (s32[1,8,64]{2,1,0:T(8,128)S(1)}, s32[1,8,64]{2,1,0:T(8,128)}, u32[]{:S(2)}) copy-start(s32[1,8,64]{2,1,0:T(8,128)} %flag_ref.1) | copy-start | bytes 6148
  2.6 8.1 %collective-permute-start.1 = (f32[7,64,128]{2,1,0:T(8,128)S(1)}, f32[7,64,128]{2,1,0:T(8,128)S(1)}, u32[]{:S(2)}, u32[]{:S(2)}) collective-permute-start(f32[7,64,128]{2,1,0:T(8,128)S(1)} %get-tuple-element.51), channel_id=1, source_target_pairs={{0,32},{32,0},{64,96},{96,64},{128,160},{160,128},{192,224},{224,1... | collective-permute-start | bytes 688136 | tf_op jit(solution)/shard_map/ppermute | solution.py:637
  4.7 8.9 %collective-permute-start.2 = (f32[7,64,128]{2,1,0:T(8,128)S(1)}, f32[7,64,128]{2,1,0:T(8,128)S(1)}, u32[]{:S(2)}, u32[]{:S(2)}) collective-permute-start(f32[7,64,128]{2,1,0:T(8,128)S(1)} %get-tuple-element.52), channel_id=1, source_target_pairs={{0,64},{32,96},{64,128},{96,160},{128,192},{160,224},{192,0},{224,... | collective-permute-start | bytes 688136 | tf_op jit(solution)/shard_map/ppermute | solution.py:637
  6.0 11.4 %collective-permute-start.3 = (f32[7,64,128]{2,1,0:T(8,128)S(1)}, f32[7,64,128]{2,1,0:T(8,128)S(1)}, u32[]{:S(2)}, u32[]{:S(2)}) collective-permute-start(f32[7,64,128]{2,1,0:T(8,128)S(1)} %get-tuple-element.53), channel_id=1, source_target_pairs={{0,96},{32,64},{64,160},{96,128},{128,224},{160,192},{192,32},{224... | collective-permute-start | bytes 688136 | tf_op jit(solution)/shard_map/ppermute | solution.py:637
  7.2 16.4 %collective-permute-start.4 = (f32[7,64,128]{2,1,0:T(8,128)S(1)}, f32[7,64,128]{2,1,0:T(8,128)S(1)}, u32[]{:S(2)}, u32[]{:S(2)}) collective-permute-start(f32[7,64,128]{2,1,0:T(8,128)S(1)} %get-tuple-element.54), channel_id=1, source_target_pairs={{0,128},{32,160},{64,192},{96,224},{128,0},{160,32},{192,64},{224,... | collective-permute-start | bytes 688136 | tf_op jit(solution)/shard_map/ppermute | solution.py:637
  8.6 19.9 %collective-permute-start.6 = (f32[7,64,128]{2,1,0:T(8,128)S(1)}, f32[7,64,128]{2,1,0:T(8,128)S(1)}, u32[]{:S(2)}, u32[]{:S(2)}) collective-permute-start(f32[7,64,128]{2,1,0:T(8,128)S(1)} %get-tuple-element.55), channel_id=1, source_target_pairs={{0,192},{32,224},{64,0},{96,32},{128,64},{160,96},{192,128},{224,1... | collective-permute-start | bytes 688136 | tf_op jit(solution)/shard_map/ppermute | solution.py:637
  10.6 17.9 %collective-permute-start.7 = (f32[7,64,128]{2,1,0:T(8,128)S(1)}, f32[7,64,128]{2,1,0:T(8,128)S(1)}, u32[]{:S(2)}, u32[]{:S(2)}) collective-permute-start(f32[7,64,128]{2,1,0:T(8,128)S(1)} %get-tuple-element.56), channel_id=1, source_target_pairs={{0,224},{32,192},{64,32},{96,0},{128,96},{160,64},{192,160},{224,1... | collective-permute-start | bytes 688136 | tf_op jit(solution)/shard_map/ppermute | solution.py:637
  13.6 14.9 %collective-permute-start.5 = (f32[7,64,128]{2,1,0:T(8,128)S(1)}, f32[7,64,128]{2,1,0:T(8,128)S(1)}, u32[]{:S(2)}, u32[]{:S(2)}) collective-permute-start(f32[7,64,128]{2,1,0:T(8,128)S(1)} %shard_map.28.early_ref), channel_id=1, source_target_pairs={{0,160},{32,128},{64,224},{96,192},{128,32},{160,0},{192,96},{224,... | collective-permute-start | bytes 688136 | tf_op jit(solution)/shard_map/ppermute | solution.py:637
  29.3 12.3 %collective-permute-start.10 = (f32[7,64,128]{2,1,0:T(8,128)S(1)}, f32[7,64,128]{2,1,0:T(8,128)S(1)}, u32[]{:S(2)}, u32[]{:S(2)}) collective-permute-start(f32[7,64,128]{2,1,0:T(8,128)S(1)} %get-tuple-element.60), channel_id=1, source_target_pairs={{0,96},{32,64},{64,160},{96,128},{128,224},{160,192},{192,32},{224... | collective-permute-start | bytes 688136 | tf_op jit(solution)/shard_map/ppermute | solution.py:653
  32.8 18.1 %collective-permute-start.11 = (f32[7,64,128]{2,1,0:T(8,128)S(1)}, f32[7,64,128]{2,1,0:T(8,128)S(1)}, u32[]{:S(2)}, u32[]{:S(2)}) collective-permute-start(f32[7,64,128]{2,1,0:T(8,128)S(1)} %get-tuple-element.61), channel_id=1, source_target_pairs={{0,128},{32,160},{64,192},{96,224},{128,0},{160,32},{192,64},{224,... | collective-permute-start | bytes 688136 | tf_op jit(solution)/shard_map/ppermute | solution.py:653
  35.0 6.4 %collective-permute-start = (f32[17,8,128]{2,1,0:T(8,128)S(1)}, f32[17,8,128]{2,1,0:T(8,128)S(1)}, u32[]{:S(2)}, u32[]{:S(2)}) collective-permute-start(f32[17,8,128]{2,1,0:T(8,128)S(1)} %get-tuple-element.43), channel_id=1, source_target_pairs={{0,1},{1,0},{2,3},{3,2},{4,5},{5,4},{6,7},{7,6},{8,9},{9,8},{10,11... | collective-permute-start | bytes 208904 | tf_op jit(solution)/shard_map/ppermute | solution.py:633
  37.5 19.0 %collective-permute-start.12 = (f32[7,64,128]{2,1,0:T(8,128)S(1)}, f32[7,64,128]{2,1,0:T(8,128)S(1)}, u32[]{:S(2)}, u32[]{:S(2)}) collective-permute-start(f32[7,64,128]{2,1,0:T(8,128)S(1)} %get-tuple-element.62), channel_id=1, source_target_pairs={{0,160},{32,128},{64,224},{96,192},{128,32},{160,0},{192,96},{224,... | collective-permute-start | bytes 688136 | tf_op jit(solution)/shard_map/ppermute | solution.py:653
  37.8 18.6 %collective-permute-start.13 = (f32[7,64,128]{2,1,0:T(8,128)S(1)}, f32[7,64,128]{2,1,0:T(8,128)S(1)}, u32[]{:S(2)}, u32[]{:S(2)}) collective-permute-start(f32[7,64,128]{2,1,0:T(8,128)S(1)} %get-tuple-element.63), channel_id=1, source_target_pairs={{0,192},{32,224},{64,0},{96,32},{128,64},{160,96},{192,128},{224,1... | collective-permute-start | bytes 688136 | tf_op jit(solution)/shard_map/ppermute | solution.py:653
  41.4 15.1 %collective-permute-start.14 = (f32[7,64,128]{2,1,0:T(8,128)S(1)}, f32[7,64,128]{2,1,0:T(8,128)S(1)}, u32[]{:S(2)}, u32[]{:S(2)}) collective-permute-start(f32[7,64,128]{2,1,0:T(8,128)S(1)} %get-tuple-element.64), channel_id=1, source_target_pairs={{0,224},{32,192},{64,32},{96,0},{128,96},{160,64},{192,160},{224,1... | collective-permute-start | bytes 688136 | tf_op jit(solution)/shard_map/ppermute | solution.py:653
  41.6 14.9 %collective-permute-start.8 = (f32[7,64,128]{2,1,0:T(8,128)S(1)}, f32[7,64,128]{2,1,0:T(8,128)S(1)}, u32[]{:S(2)}, u32[]{:S(2)}) collective-permute-start(f32[7,64,128]{2,1,0:T(8,128)S(1)} %get-tuple-element.58), channel_id=1, source_target_pairs={{0,32},{32,0},{64,96},{96,64},{128,160},{160,128},{192,224},{224,1... | collective-permute-start | bytes 688136 | tf_op jit(solution)/shard_map/ppermute | solution.py:653
  50.9 7.1 %collective-permute-start.9 = (f32[7,64,128]{2,1,0:T(8,128)S(1)}, f32[7,64,128]{2,1,0:T(8,128)S(1)}, u32[]{:S(2)}, u32[]{:S(2)}) collective-permute-start(f32[7,64,128]{2,1,0:T(8,128)S(1)} %get-tuple-element.59), channel_id=1, source_target_pairs={{0,64},{32,96},{64,128},{96,160},{128,192},{160,224},{192,0},{224,... | collective-permute-start | bytes 688136 | tf_op jit(solution)/shard_map/ppermute | solution.py:653
  54.6 1.2 copy-start
  55.8 0.7 copy-start.8
  56.5 2.7 %copy-start.6 = (f32[7,64,128]{2,1,0:T(8,128)}, f32[7,64,128]{2,1,0:T(8,128)S(1)}, u32[]{:S(2)}) copy-start(f32[7,64,128]{2,1,0:T(8,128)S(1)} %get-tuple-element.49.inv_ref) | copy-start | bytes 688132
  56.5 2.7 %copy-start.10 = (f32[7,64,128]{2,1,0:T(8,128)}, f32[7,64,128]{2,1,0:T(8,128)S(1)}, u32[]{:S(2)}) copy-start(f32[7,64,128]{2,1,0:T(8,128)S(1)} %get-tuple-element.46.w_ref) | copy-start | bytes 688132
  56.5 2.7 %copy-start.2 = (f32[7,64,128]{2,1,0:T(8,128)}, f32[7,64,128]{2,1,0:T(8,128)S(1)}, u32[]{:S(2)}) copy-start(f32[7,64,128]{2,1,0:T(8,128)S(1)} %collective-permute-done.8.refs_1_) | copy-start | bytes 688132
  58.0 1.2 copy-start.4
  59.2 0.9 copy-start.14
  60.1 28.6 %collective-permute-start.17 = (f32[14,32,128]{2,1,0:T(8,128)}, f32[14,32,128]{2,1,0:T(8,128)}, u32[]{:S(2)}, u32[]{:S(2)}) collective-permute-start(f32[14,32,128]{2,1,0:T(8,128)} %get-tuple-element.72), channel_id=1, source_target_pairs={{0,2},{2,0},{4,6},{6,4},{8,10},{10,8},{12,14},{14,12},{16,18},{18,... | collective-permute-start | bytes 688136 | tf_op jit(solution)/shard_map/ppermute | solution.py:618
  64.7 1.5 %collective-permute-start.15 = (f32[5,32,128]{2,1,0:T(8,128)S(1)}, f32[5,32,128]{2,1,0:T(8,128)S(1)}, u32[]{:S(2)}, u32[]{:S(2)}) collective-permute-start(f32[5,32,128]{2,1,0:T(8,128)S(1)} %get-tuple-element.67), channel_id=1, source_target_pairs={{0,2},{2,0},{4,6},{6,4},{8,10},{10,8},{12,14},{14,12},{16,18},{18,... | collective-permute-start | bytes 245768 | tf_op jit(solution)/shard_map/ppermute | solution.py:618
  66.2 0.6 copy-start.16
  66.8 4.8 %collective-permute-start.16 = (f32[2,32,128]{2,1,0:T(8,128)S(1)}, f32[2,32,128]{2,1,0:T(8,128)S(1)}, u32[]{:S(2)}, u32[]{:S(2)}) collective-permute-start(f32[2,32,128]{2,1,0:T(8,128)S(1)} %get-tuple-element.69), channel_id=1, source_target_pairs={{4,0},{6,2},{8,4},{10,6},{12,8},{14,10},{16,12},{18,14},{20,16},{2... | collective-permute-start | bytes 98312 | tf_op jit(solution)/shard_map/ppermute | solution.py:622
  72.3 18.4 %all-to-all-start = ((f32[8,2,4,128]{3,2,1,0:T(4,128)}), f32[8,2,4,128]{3,2,1,0:T(4,128)S(1)}, u32[]{:S(2)}, u32[]{:S(2)}) async-start(f32[8,2,4,128]{3,2,1,0:T(4,128)} %get-tuple-element.70), calls=%async_computation | async-start | bytes 65536 | tf_op jit(solution)/shard_map/all_to_all | solution.py:601
  80.3 4.2 %collective-permute-start.18 = (f32[1,32,128]{2,1,0:T(8,128)S(1)}, f32[1,32,128]{2,1,0:T(8,128)S(1)}, u32[]{:S(2)}, u32[]{:S(2)}) collective-permute-start(f32[1,32,128]{2,1,0:T(8,128)S(1)} %get-tuple-element.75), channel_id=1, source_target_pairs={{0,4},{2,6},{4,8},{6,10},{8,12},{10,14},{12,16},{14,18},{16,20},{1... | collective-permute-start | bytes 49160 | tf_op jit(solution)/shard_map/ppermute | solution.py:622
  84.5 0.9 copy-start.3
  85.4 0.9 copy-start.5
  86.4 0.9 copy-start.7
  87.3 1.4 %copy-start.17 = (f32[6,32,128]{2,1,0:T(8,128)S(1)}, f32[6,32,128]{2,1,0:T(8,128)}, u32[]{:S(2)}) copy-start(f32[6,32,128]{2,1,0:T(8,128)} %copy-done.16) | copy-start | bytes 294916
  87.8 0.9 copy-start.12
  88.7 37.4 %copy-start.1 = (f32[1,7,8,64,128]{4,3,2,1,0:T(8,128)S(1)}, f32[1,7,8,64,128]{4,3,2,1,0:T(8,128)}, u32[]{:S(2)}) copy-start(f32[1,7,8,64,128]{4,3,2,1,0:T(8,128)} %copy-done) | copy-start | bytes 5505028
  88.7 37.4 %copy-start.9 = (f32[7,64,128]{2,1,0:T(8,128)S(1)}, f32[7,64,128]{2,1,0:T(8,128)}, u32[]{:S(2)}) copy-start(f32[7,64,128]{2,1,0:T(8,128)} %copy-done.8) | copy-start | bytes 688132
  88.7 37.4 %copy-start.11 = (f32[7,64,128]{2,1,0:T(8,128)S(1)}, f32[7,64,128]{2,1,0:T(8,128)}, u32[]{:S(2)}) copy-start(f32[7,64,128]{2,1,0:T(8,128)} %copy-done.10) | copy-start | bytes 688132
  90.6 17.2 %all-to-all-start.1 = ((f32[8,14,4,128]{3,2,1,0:T(4,128)}), f32[8,14,4,128]{3,2,1,0:T(4,128)S(1)}, u32[]{:S(2)}, u32[]{:S(2)}) async-start(f32[8,14,4,128]{3,2,1,0:T(4,128)} %get-tuple-element.76), calls=%async_computation.1 | async-start | bytes 458752 | tf_op jit(solution)/shard_map/all_to_all | solution.py:601
  119.3 0.9 copy-start.18
  120.3 8.0 %collective-permute-start.19 = (f32[14,32,128]{2,1,0:T(8,128)S(1)}, f32[14,32,128]{2,1,0:T(8,128)S(1)}, u32[]{:S(2)}, u32[]{:S(2)}) collective-permute-start(f32[14,32,128]{2,1,0:T(8,128)S(1)} %get-tuple-element.78), channel_id=1, source_target_pairs={{0,2},{2,0},{4,6},{6,4},{8,10},{10,8},{12,14},{14,12},{16,18},{18,... | collective-permute-start | bytes 688136 | tf_op jit(solution)/shard_map/ppermute | solution.py:618
  126.1 1.1 copy-start.13
  127.2 1.5 %copy-start.15 = (f32[7,7,32,128]{3,2,1,0:T(8,128)S(1)}, f32[7,7,32,128]{3,2,1,0:T(8,128)}, u32[]{:S(2)}) copy-start(f32[7,7,32,128]{3,2,1,0:T(8,128)} %copy-done.14) | copy-start | bytes 2408452

commit v5 on v3

--- a/solution.py
+++ b/solution.py
@@ -20,7 +20,8 @@
 NU_T = 0.25
 
 FIELDS = 7
-ORDER = (3, 4, 5, 7, 1, 2, 6)
+ORDER = (5, 7, 3, 4, 1, 2, 6)
+RETURN = (3, 4, 5, 7, 1, 2, 6)
 EDGES = 2 * FIELDS + 3
 COEFS = 5
 TILE = 8
@@ -640,7 +641,7 @@
     ends = neighbour(ends, -1)
     link, edge = call(link_kernel, [(3,) + thin, (1,) + thin], raw, ends)
     specs = call(spectral_kernel, [blocks[0].shape] * instances, *blocks, flops=own.size * 9)
-    for k in order:
+    for k in RETURN:
         specs[k] = lax.ppermute(specs[k], "inst", route(*steps[k], instances))
     edge = neighbour(edge, 1)
     (link,) = call(join_kernel, [(4,) + thin], link, edge)

time: 111 us -> 107 us (0.964)
  waiting for transfers between devices: 31.7 us -> 28.2 us
    ppermute x7, waiting for transfers between devices: 13.8 us -> 11.5 us  [body(): blocks[k] = lax.ppermute(blocks[k], 'inst', route(*steps[k], instances))]
    ppermute x1, waiting for transfers between devices: 2.17 us -> 0.93 us  [body(): lax.ppermute(edges, 'circ', [(i, (i + 1) % circ_count) for i in range(cir...]
  transfers between devices with their start and end apart: 20 -> 20, of which waited for: 10 -> 11; matrix products, arithmetic and copies ran while one was open for 0% -> 0% of each run, Pallas kernels for 6% -> 6%
where the time goes in v5:
time: 107 us
  starting transfers between devices  38.2 us (36%)
  blocking collectives  29.9 us (28%)
  waiting for transfers between devices  28.2 us (26%)
  Pallas kernels  10.2 us (10%)
    all_to_all x2, blocking collectives, exchange(): return lax.all_to_all(x, axis, 0, 0, tiled=True, axis_index_groups=groups)  29.9 us
    ppermute x7, starting transfers between devices, body(): blocks[k] = lax.ppermute(blocks[k], 'inst', route(*steps[k], instances))  12.7 us
    ppermute x7, waiting for transfers between devices, body(): blocks[k] = lax.ppermute(blocks[k], 'inst', route(*steps[k], instances))  11.5 us
    ppermute x7, starting transfers between devices, body(): specs[k] = lax.ppermute(specs[k], 'inst', route(*steps[k], instances))  11.3 us
    ppermute x7, waiting for transfers between devices, body(): specs[k] = lax.ppermute(specs[k], 'inst', route(*steps[k], instances))  10.1 us
    ppermute x3, starting transfers between devices, partner(): return lax.ppermute(x, 'ax', swap)  6.92 us
    ppermute x2, starting transfers between devices, neighbour(): return lax.ppermute(x, 'ax', moves)  4.83 us
    ppermute x2, waiting for transfers between devices, neighbour(): return lax.ppermute(x, 'ax', moves)  4.39 us
  transfers between devices with their start and end apart: 20, of which 11 were waited for; matrix products, arithmetic and copies ran while one was open for 0% of the time, Pallas kernels for 6%

profile of v5, /device:TPU:1, one launch (start us, length us, event | category | flops | bytes accessed | tf_op | source)
XLA Modules:
  0.0 106.8 jit_solution(10613194945708697308)
XLA Ops:
  0.0 0.9 shard_map.28.early_ref
  1.0 0.0 copy-start
  1.0 4.7 %collective-permute-start.5 = (f32[7,64,128]{2,1,0:T(8,128)S(1)}, f32[7,64,128]{2,1,0:T(8,128)S(1)}, u32[]{:S(2)}, u32[]{:S(2)}) collective-permute-start(f32[7,64,128]{2,1,0:T(8,128)S(1)} %shard_map.28.early_ref), channel_id=1, source_target_pairs={{0,160},{32,128},{64,224},{96,192},{128,32},{160,0},{192,96},{224,... | collective-permute-start | bytes 688136 | tf_op jit(solution)/shard_map/ppermute | solution.py:631
  5.7 1.6 %shard_map.29 = (f32[7,64,128]{2,1,0:T(8,128)S(1)}, f32[7,64,128]{2,1,0:T(8,128)S(1)}, f32[7,64,128]{2,1,0:T(8,128)S(1)}, f32[7,64,128]{2,1,0:T(8,128)S(1)}, f32...) custom-call(f32[1,7,8,64,128]{4,3,2,1,0:T(8,128)} %source_ref.1, ...), custom_call_target="tpu_custom_call" | custom-call | bytes 3670016 | tf_op jit(solution)/shard_map/pallas_call | solution.py:146
  7.3 0.3 collective-permute-start.1
  7.6 0.4 collective-permute-start.2
  8.0 0.9 collective-permute-start.3
  9.0 3.5 %collective-permute-start.4 = (f32[7,64,128]{2,1,0:T(8,128)S(1)}, f32[7,64,128]{2,1,0:T(8,128)S(1)}, u32[]{:S(2)}, u32[]{:S(2)}) collective-permute-start(f32[7,64,128]{2,1,0:T(8,128)S(1)} %get-tuple-element.53), channel_id=1, source_target_pairs={{0,128},{32,160},{64,192},{96,224},{128,0},{160,32},{192,64},{224,... | collective-permute-start | bytes 688136 | tf_op jit(solution)/shard_map/ppermute | solution.py:631
  12.4 0.0 collective-permute-done.5.refs_5_
  12.4 1.1 %collective-permute-start.6 = (f32[7,64,128]{2,1,0:T(8,128)S(1)}, f32[7,64,128]{2,1,0:T(8,128)S(1)}, u32[]{:S(2)}, u32[]{:S(2)}) collective-permute-start(f32[7,64,128]{2,1,0:T(8,128)S(1)} %get-tuple-element.54), channel_id=1, source_target_pairs={{0,192},{32,224},{64,0},{96,32},{128,64},{160,96},{192,128},{224,1... | collective-permute-start | bytes 688136 | tf_op jit(solution)/shard_map/ppermute | solution.py:631
  13.5 2.4 %collective-permute-done.1.refs_1_ = f32[7,64,128]{2,1,0:T(8,128)S(1)} collective-permute-done((f32[7,64,128]{2,1,0:T(8,128)S(1)}, f32[7,64,128]{2,1,0:T(8,128)S(1)}, u32[]{:S(2)}, u32[]{:S(2)}) %collective-permute-start.1) | collective-permute-done | bytes 229408 | tf_op jit(solution)/shard_map/ppermute | solution.py:631
  15.9 1.7 %collective-permute-start.7 = (f32[7,64,128]{2,1,0:T(8,128)S(1)}, f32[7,64,128]{2,1,0:T(8,128)S(1)}, u32[]{:S(2)}, u32[]{:S(2)}) collective-permute-start(f32[7,64,128]{2,1,0:T(8,128)S(1)} %get-tuple-element.55), channel_id=1, source_target_pairs={{0,224},{32,192},{64,32},{96,0},{128,96},{160,64},{192,160},{224,1... | collective-permute-start | bytes 688136 | tf_op jit(solution)/shard_map/ppermute | solution.py:631
  17.6 0.4 collective-permute-done.2.refs_2_
  18.0 3.7 %collective-permute-done.3.refs_3_ = f32[7,64,128]{2,1,0:T(8,128)S(1)} collective-permute-done((f32[7,64,128]{2,1,0:T(8,128)S(1)}, f32[7,64,128]{2,1,0:T(8,128)S(1)}, u32[]{:S(2)}, u32[]{:S(2)}) %collective-permute-start.3) | collective-permute-done | bytes 229408 | tf_op jit(solution)/shard_map/ppermute | solution.py:631
  21.6 5.0 %collective-permute-done.4.refs_4_ = f32[7,64,128]{2,1,0:T(8,128)S(1)} collective-permute-done((f32[7,64,128]{2,1,0:T(8,128)S(1)}, f32[7,64,128]{2,1,0:T(8,128)S(1)}, u32[]{:S(2)}, u32[]{:S(2)}) %collective-permute-start.4) | collective-permute-done | bytes 229408 | tf_op jit(solution)/shard_map/ppermute | solution.py:631
  26.7 0.0 collective-permute-done.6.refs_6_
  26.7 0.8 shard_map.31
  27.5 0.7 collective-permute-start.8
  28.3 2.0 %collective-permute-start.9 = (f32[7,64,128]{2,1,0:T(8,128)S(1)}, f32[7,64,128]{2,1,0:T(8,128)S(1)}, u32[]{:S(2)}, u32[]{:S(2)}) collective-permute-start(f32[7,64,128]{2,1,0:T(8,128)S(1)} %get-tuple-element.58), channel_id=1, source_target_pairs={{0,64},{32,96},{64,128},{96,160},{128,192},{160,224},{192,0},{224,... | collective-permute-start | bytes 688136 | tf_op jit(solution)/shard_map/ppermute | solution.py:645
  30.3 2.6 %collective-permute-start = (f32[17,8,128]{2,1,0:T(8,128)S(1)}, f32[17,8,128]{2,1,0:T(8,128)S(1)}, u32[]{:S(2)}, u32[]{:S(2)}) collective-permute-start(f32[17,8,128]{2,1,0:T(8,128)S(1)} %get-tuple-element.42), channel_id=1, source_target_pairs={{0,1},{1,0},{2,3},{3,2},{4,5},{5,4},{6,7},{7,6},{8,9},{9,8},{10,11... | collective-permute-start | bytes 208904 | tf_op jit(solution)/shard_map/ppermute | solution.py:627
  32.9 0.5 collective-permute-start.10
  33.4 1.4 %collective-permute-start.11 = (f32[7,64,128]{2,1,0:T(8,128)S(1)}, f32[7,64,128]{2,1,0:T(8,128)S(1)}, u32[]{:S(2)}, u32[]{:S(2)}) collective-permute-start(f32[7,64,128]{2,1,0:T(8,128)S(1)} %get-tuple-element.60), channel_id=1, source_target_pairs={{0,128},{32,160},{64,192},{96,224},{128,0},{160,32},{192,64},{224,... | collective-permute-start | bytes 688136 | tf_op jit(solution)/shard_map/ppermute | solution.py:645
  34.8 0.9 collective-permute-done.halo_ref
  35.7 4.3 %collective-permute-start.12 = (f32[7,64,128]{2,1,0:T(8,128)S(1)}, f32[7,64,128]{2,1,0:T(8,128)S(1)}, u32[]{:S(2)}, u32[]{:S(2)}) collective-permute-start(f32[7,64,128]{2,1,0:T(8,128)S(1)} %get-tuple-element.61), channel_id=1, source_target_pairs={{0,160},{32,128},{64,224},{96,192},{128,32},{160,0},{192,96},{224,... | collective-permute-start | bytes 688136 | tf_op jit(solution)/shard_map/ppermute | solution.py:645
  40.0 1.2 %collective-permute-start.13 = (f32[7,64,128]{2,1,0:T(8,128)S(1)}, f32[7,64,128]{2,1,0:T(8,128)S(1)}, u32[]{:S(2)}, u32[]{:S(2)}) collective-permute-start(f32[7,64,128]{2,1,0:T(8,128)S(1)} %get-tuple-element.62), channel_id=1, source_target_pairs={{0,192},{32,224},{64,0},{96,32},{128,64},{160,96},{192,128},{224,1... | collective-permute-start | bytes 688136 | tf_op jit(solution)/shard_map/ppermute | solution.py:645
  41.2 1.1 %collective-permute-start.14 = (f32[7,64,128]{2,1,0:T(8,128)S(1)}, f32[7,64,128]{2,1,0:T(8,128)S(1)}, u32[]{:S(2)}, u32[]{:S(2)}) collective-permute-start(f32[7,64,128]{2,1,0:T(8,128)S(1)} %get-tuple-element.63), channel_id=1, source_target_pairs={{0,224},{32,192},{64,32},{96,0},{128,96},{160,64},{192,160},{224,1... | collective-permute-start | bytes 688136 | tf_op jit(solution)/shard_map/ppermute | solution.py:645
  42.3 0.1 broadcast_in_dim.2.flag_ref
  42.4 3.5 %shard_map.30 = (f32[8,7,64,128]{3,2,1,0:T(8,128)S(1)}, f32[8,64,128]{2,1,0:T(8,128)S(1)}, f32[7,64,128]{2,1,0:T(8,128)S(1)}, f32[7,64,128]{2,1,0:T(8,128)S(1)},...) custom-call(f32[1,7,8,64,128]{4,3,2,1,0:T(8,128)} %source_ref.1, ...), custom_call_target="tpu_custom_call" | custom-call | flops 27525120 | bytes 7340032 | tf_op jit(solution)/shard_map/pallas_call | solution.py:581
  46.0 6.3 %collective-permute-done.11.refs_4_ = f32[7,64,128]{2,1,0:T(8,128)S(1)} collective-permute-done((f32[7,64,128]{2,1,0:T(8,128)S(1)}, f32[7,64,128]{2,1,0:T(8,128)S(1)}, u32[]{:S(2)}, u32[]{:S(2)}) %collective-permute-start.11) | collective-permute-done | bytes 229408 | tf_op jit(solution)/shard_map/ppermute | solution.py:645
  52.3 3.8 %collective-permute-done.13.refs_6_ = f32[7,64,128]{2,1,0:T(8,128)S(1)} collective-permute-done((f32[7,64,128]{2,1,0:T(8,128)S(1)}, f32[7,64,128]{2,1,0:T(8,128)S(1)}, u32[]{:S(2)}, u32[]{:S(2)}) %collective-permute-start.13) | collective-permute-done | bytes 229408 | tf_op jit(solution)/shard_map/ppermute | solution.py:645
  56.1 0.5 shard_map.32
  56.6 1.6 %collective-permute-start.15 = (f32[14,32,128]{2,1,0:T(8,128)S(1)}, f32[14,32,128]{2,1,0:T(8,128)S(1)}, u32[]{:S(2)}, u32[]{:S(2)}) collective-permute-start(f32[14,32,128]{2,1,0:T(8,128)S(1)} %get-tuple-element.66), channel_id=1, source_target_pairs={{0,2},{2,0},{4,6},{6,4},{8,10},{10,8},{12,14},{14,12},{16,18},{18,... | collective-permute-start | bytes 688136 | tf_op jit(solution)/shard_map/ppermute | solution.py:612
  58.1 0.1 collective-permute-start.16
  58.2 1.2 %collective-permute-done.16.got_ref = f32[5,32,128]{2,1,0:T(8,128)S(1)} collective-permute-done((f32[5,32,128]{2,1,0:T(8,128)S(1)}, f32[5,32,128]{2,1,0:T(8,128)S(1)}, u32[]{:S(2)}, u32[]{:S(2)}) %collective-permute-start.16) | collective-permute-done | bytes 81952 | tf_op jit(solution)/shard_map/ppermute | solution.py:612
  59.5 1.3 %collective-permute-start.17 = (f32[2,32,128]{2,1,0:T(8,128)S(1)}, f32[2,32,128]{2,1,0:T(8,128)S(1)}, u32[]{:S(2)}, u32[]{:S(2)}) collective-permute-start(f32[2,32,128]{2,1,0:T(8,128)S(1)} %get-tuple-element.71), channel_id=1, source_target_pairs={{4,0},{6,2},{8,4},{10,6},{12,8},{14,10},{16,12},{18,14},{20,16},{2... | collective-permute-start | bytes 98312 | tf_op jit(solution)/shard_map/ppermute | solution.py:616
  60.8 3.5 %collective-permute-done.17.ends_ref = f32[2,32,128]{2,1,0:T(8,128)S(1)} collective-permute-done((f32[2,32,128]{2,1,0:T(8,128)S(1)}, f32[2,32,128]{2,1,0:T(8,128)S(1)}, u32[]{:S(2)}, u32[]{:S(2)}) %collective-permute-start.17) | collective-permute-done | bytes 32800 | tf_op jit(solution)/shard_map/ppermute | solution.py:616
  64.3 3.5 %collective-permute-start.18 = (f32[1,32,128]{2,1,0:T(8,128)S(1)}, f32[1,32,128]{2,1,0:T(8,128)S(1)}, u32[]{:S(2)}, u32[]{:S(2)}) collective-permute-start(f32[1,32,128]{2,1,0:T(8,128)S(1)} %get-tuple-element.73), channel_id=1, source_target_pairs={{0,4},{2,6},{4,8},{6,10},{8,12},{10,14},{12,16},{14,18},{16,20},{1... | collective-permute-start | bytes 49160 | tf_op jit(solution)/shard_map/ppermute | solution.py:616
  67.9 0.9 collective-permute-done.18.edge_ref
  68.7 0.5 shard_map.33
  69.2 0.1 shard_map.37
  69.4 18.5 %all_to_all.10.rhs_ref = f32[8,16,4,128]{3,2,1,0:T(4,128)S(1)} all-to-all(f32[8,16,4,128]{3,2,1,0:T(4,128)S(1)} %get-tuple-element.74), channel_id=1, replica_groups={{0,4,8,12,16,20,24,28},{2,6,10,14,18,22,26,30},{1,5,9,13,17,21,25,29},{..., dimensions={0} | all-to-all | bytes 524288 | tf_op jit(solution)/shard_map/all_to_all | solution.py:595
  87.8 0.1 shard_map.38
  87.9 11.4 %all_to_all.11.solved_ref = f32[8,14,4,128]{3,2,1,0:T(4,128)S(1)} all-to-all(f32[8,14,4,128]{3,2,1,0:T(4,128)S(1)} %shard_map.38), channel_id=1, replica_groups={{0,4,8,12,16,20,24,28},{2,6,10,14,18,22,26,30},{1,5,9,13,17,21,25,29},{..., dimensions={0} | all-to-all | bytes 458752 | tf_op jit(solution)/shard_map/all_to_all | solution.py:595
  99.3 0.1 shard_map.39
  99.4 5.2 %collective-permute-start.19 = (f32[14,32,128]{2,1,0:T(8,128)S(1)}, f32[14,32,128]{2,1,0:T(8,128)S(1)}, u32[]{:S(2)}, u32[]{:S(2)}) collective-permute-start(f32[14,32,128]{2,1,0:T(8,128)S(1)} %get-tuple-element.76), channel_id=1, source_target_pairs={{0,2},{2,0},{4,6},{6,4},{8,10},{10,8},{12,14},{14,12},{16,18},{18,... | collective-permute-start | bytes 688136 | tf_op jit(solution)/shard_map/ppermute | solution.py:612
  104.6 1.0 shard_map.40.refs_0_
  105.7 0.1 collective-permute-done.19.ends_ref
  105.7 1.0 shard_map.41
  (12 shorter events, 0.1 us)
Async XLA Ops:
  1.0 41.3 %copy-start = (s32[1,8,64]{2,1,0:T(8,128)S(1)}, s32[1,8,64]{2,1,0:T(8,128)}, u32[]{:S(2)}) copy-start(s32[1,8,64]{2,1,0:T(8,128)} %flag_ref.1) | copy-start | bytes 6148
  1.0 11.5 %collective-permute-start.5 = (f32[7,64,128]{2,1,0:T(8,128)S(1)}, f32[7,64,128]{2,1,0:T(8,128)S(1)}, u32[]{:S(2)}, u32[]{:S(2)}) collective-permute-start(f32[7,64,128]{2,1,0:T(8,128)S(1)} %shard_map.28.early_ref), channel_id=1, source_target_pairs={{0,160},{32,128},{64,224},{96,192},{128,32},{160,0},{192,96},{224,... | collective-permute-start | bytes 688136 | tf_op jit(solution)/shard_map/ppermute | solution.py:631
  7.3 8.6 %collective-permute-start.1 = (f32[7,64,128]{2,1,0:T(8,128)S(1)}, f32[7,64,128]{2,1,0:T(8,128)S(1)}, u32[]{:S(2)}, u32[]{:S(2)}) collective-permute-start(f32[7,64,128]{2,1,0:T(8,128)S(1)} %get-tuple-element.50), channel_id=1, source_target_pairs={{0,32},{32,0},{64,96},{96,64},{128,160},{160,128},{192,224},{224,1... | collective-permute-start | bytes 688136 | tf_op jit(solution)/shard_map/ppermute | solution.py:631
  7.6 10.4 %collective-permute-start.2 = (f32[7,64,128]{2,1,0:T(8,128)S(1)}, f32[7,64,128]{2,1,0:T(8,128)S(1)}, u32[]{:S(2)}, u32[]{:S(2)}) collective-permute-start(f32[7,64,128]{2,1,0:T(8,128)S(1)} %get-tuple-element.51), channel_id=1, source_target_pairs={{0,64},{32,96},{64,128},{96,160},{128,192},{160,224},{192,0},{224,... | collective-permute-start | bytes 688136 | tf_op jit(solution)/shard_map/ppermute | solution.py:631
  8.0 13.6 %collective-permute-start.3 = (f32[7,64,128]{2,1,0:T(8,128)S(1)}, f32[7,64,128]{2,1,0:T(8,128)S(1)}, u32[]{:S(2)}, u32[]{:S(2)}) collective-permute-start(f32[7,64,128]{2,1,0:T(8,128)S(1)} %get-tuple-element.52), channel_id=1, source_target_pairs={{0,96},{32,64},{64,160},{96,128},{128,224},{160,192},{192,32},{224... | collective-permute-start | bytes 688136 | tf_op jit(solution)/shard_map/ppermute | solution.py:631
  9.0 17.7 %collective-permute-start.4 = (f32[7,64,128]{2,1,0:T(8,128)S(1)}, f32[7,64,128]{2,1,0:T(8,128)S(1)}, u32[]{:S(2)}, u32[]{:S(2)}) collective-permute-start(f32[7,64,128]{2,1,0:T(8,128)S(1)} %get-tuple-element.53), channel_id=1, source_target_pairs={{0,128},{32,160},{64,192},{96,224},{128,0},{160,32},{192,64},{224,... | collective-permute-start | bytes 688136 | tf_op jit(solution)/shard_map/ppermute | solution.py:631
  12.4 14.2 %collective-permute-start.6 = (f32[7,64,128]{2,1,0:T(8,128)S(1)}, f32[7,64,128]{2,1,0:T(8,128)S(1)}, u32[]{:S(2)}, u32[]{:S(2)}) collective-permute-start(f32[7,64,128]{2,1,0:T(8,128)S(1)} %get-tuple-element.54), channel_id=1, source_target_pairs={{0,192},{32,224},{64,0},{96,32},{128,64},{160,96},{192,128},{224,1... | collective-permute-start | bytes 688136 | tf_op jit(solution)/shard_map/ppermute | solution.py:631
  15.9 10.8 %collective-permute-start.7 = (f32[7,64,128]{2,1,0:T(8,128)S(1)}, f32[7,64,128]{2,1,0:T(8,128)S(1)}, u32[]{:S(2)}, u32[]{:S(2)}) collective-permute-start(f32[7,64,128]{2,1,0:T(8,128)S(1)} %get-tuple-element.55), channel_id=1, source_target_pairs={{0,224},{32,192},{64,32},{96,0},{128,96},{160,64},{192,160},{224,1... | collective-permute-start | bytes 688136 | tf_op jit(solution)/shard_map/ppermute | solution.py:631
  27.5 12.5 %collective-permute-start.8 = (f32[7,64,128]{2,1,0:T(8,128)S(1)}, f32[7,64,128]{2,1,0:T(8,128)S(1)}, u32[]{:S(2)}, u32[]{:S(2)}) collective-permute-start(f32[7,64,128]{2,1,0:T(8,128)S(1)} %get-tuple-element.57), channel_id=1, source_target_pairs={{0,32},{32,0},{64,96},{96,64},{128,160},{160,128},{192,224},{224,1... | collective-permute-start | bytes 688136 | tf_op jit(solution)/shard_map/ppermute | solution.py:645
  28.3 12.9 %collective-permute-start.9 = (f32[7,64,128]{2,1,0:T(8,128)S(1)}, f32[7,64,128]{2,1,0:T(8,128)S(1)}, u32[]{:S(2)}, u32[]{:S(2)}) collective-permute-start(f32[7,64,128]{2,1,0:T(8,128)S(1)} %get-tuple-element.58), channel_id=1, source_target_pairs={{0,64},{32,96},{64,128},{96,160},{128,192},{160,224},{192,0},{224,... | collective-permute-start | bytes 688136 | tf_op jit(solution)/shard_map/ppermute | solution.py:645
  30.3 5.4 %collective-permute-start = (f32[17,8,128]{2,1,0:T(8,128)S(1)}, f32[17,8,128]{2,1,0:T(8,128)S(1)}, u32[]{:S(2)}, u32[]{:S(2)}) collective-permute-start(f32[17,8,128]{2,1,0:T(8,128)S(1)} %get-tuple-element.42), channel_id=1, source_target_pairs={{0,1},{1,0},{2,3},{3,2},{4,5},{5,4},{6,7},{7,6},{8,9},{9,8},{10,11... | collective-permute-start | bytes 208904 | tf_op jit(solution)/shard_map/ppermute | solution.py:627
  32.9 13.1 %collective-permute-start.10 = (f32[7,64,128]{2,1,0:T(8,128)S(1)}, f32[7,64,128]{2,1,0:T(8,128)S(1)}, u32[]{:S(2)}, u32[]{:S(2)}) collective-permute-start(f32[7,64,128]{2,1,0:T(8,128)S(1)} %get-tuple-element.59), channel_id=1, source_target_pairs={{0,96},{32,64},{64,160},{96,128},{128,224},{160,192},{192,32},{224... | collective-permute-start | bytes 688136 | tf_op jit(solution)/shard_map/ppermute | solution.py:645
  33.4 19.0 %collective-permute-start.11 = (f32[7,64,128]{2,1,0:T(8,128)S(1)}, f32[7,64,128]{2,1,0:T(8,128)S(1)}, u32[]{:S(2)}, u32[]{:S(2)}) collective-permute-start(f32[7,64,128]{2,1,0:T(8,128)S(1)} %get-tuple-element.60), channel_id=1, source_target_pairs={{0,128},{32,160},{64,192},{96,224},{128,0},{160,32},{192,64},{224,... | collective-permute-start | bytes 688136 | tf_op jit(solution)/shard_map/ppermute | solution.py:645
  35.7 16.6 %collective-permute-start.12 = (f32[7,64,128]{2,1,0:T(8,128)S(1)}, f32[7,64,128]{2,1,0:T(8,128)S(1)}, u32[]{:S(2)}, u32[]{:S(2)}) collective-permute-start(f32[7,64,128]{2,1,0:T(8,128)S(1)} %get-tuple-element.61), channel_id=1, source_target_pairs={{0,160},{32,128},{64,224},{96,192},{128,32},{160,0},{192,96},{224,... | collective-permute-start | bytes 688136 | tf_op jit(solution)/shard_map/ppermute | solution.py:645
  40.0 16.1 %collective-permute-start.13 = (f32[7,64,128]{2,1,0:T(8,128)S(1)}, f32[7,64,128]{2,1,0:T(8,128)S(1)}, u32[]{:S(2)}, u32[]{:S(2)}) collective-permute-start(f32[7,64,128]{2,1,0:T(8,128)S(1)} %get-tuple-element.62), channel_id=1, source_target_pairs={{0,192},{32,224},{64,0},{96,32},{128,64},{160,96},{192,128},{224,1... | collective-permute-start | bytes 688136 | tf_op jit(solution)/shard_map/ppermute | solution.py:645
  41.2 14.9 %collective-permute-start.14 = (f32[7,64,128]{2,1,0:T(8,128)S(1)}, f32[7,64,128]{2,1,0:T(8,128)S(1)}, u32[]{:S(2)}, u32[]{:S(2)}) collective-permute-start(f32[7,64,128]{2,1,0:T(8,128)S(1)} %get-tuple-element.63), channel_id=1, source_target_pairs={{0,224},{32,192},{64,32},{96,0},{128,96},{160,64},{192,160},{224,1... | collective-permute-start | bytes 688136 | tf_op jit(solution)/shard_map/ppermute | solution.py:645
  56.6 12.6 %collective-permute-start.15 = (f32[14,32,128]{2,1,0:T(8,128)S(1)}, f32[14,32,128]{2,1,0:T(8,128)S(1)}, u32[]{:S(2)}, u32[]{:S(2)}) collective-permute-start(f32[14,32,128]{2,1,0:T(8,128)S(1)} %get-tuple-element.66), channel_id=1, source_target_pairs={{0,2},{2,0},{4,6},{6,4},{8,10},{10,8},{12,14},{14,12},{16,18},{18,... | collective-permute-start | bytes 688136 | tf_op jit(solution)/shard_map/ppermute | solution.py:612
  58.1 1.3 %collective-permute-start.16 = (f32[5,32,128]{2,1,0:T(8,128)S(1)}, f32[5,32,128]{2,1,0:T(8,128)S(1)}, u32[]{:S(2)}, u32[]{:S(2)}) collective-permute-start(f32[5,32,128]{2,1,0:T(8,128)S(1)} %get-tuple-element.68), channel_id=1, source_target_pairs={{0,2},{2,0},{4,6},{6,4},{8,10},{10,8},{12,14},{14,12},{16,18},{18,... | collective-permute-start | bytes 245768 | tf_op jit(solution)/shard_map/ppermute | solution.py:612
  59.5 4.8 %collective-permute-start.17 = (f32[2,32,128]{2,1,0:T(8,128)S(1)}, f32[2,32,128]{2,1,0:T(8,128)S(1)}, u32[]{:S(2)}, u32[]{:S(2)}) collective-permute-start(f32[2,32,128]{2,1,0:T(8,128)S(1)} %get-tuple-element.71), channel_id=1, source_target_pairs={{4,0},{6,2},{8,4},{10,6},{12,8},{14,10},{16,12},{18,14},{20,16},{2... | collective-permute-start | bytes 98312 | tf_op jit(solution)/shard_map/ppermute | solution.py:616
  64.3 4.4 %collective-permute-start.18 = (f32[1,32,128]{2,1,0:T(8,128)S(1)}, f32[1,32,128]{2,1,0:T(8,128)S(1)}, u32[]{:S(2)}, u32[]{:S(2)}) collective-permute-start(f32[1,32,128]{2,1,0:T(8,128)S(1)} %get-tuple-element.73), channel_id=1, source_target_pairs={{0,4},{2,6},{4,8},{6,10},{8,12},{10,14},{12,16},{14,18},{16,20},{1... | collective-permute-start | bytes 49160 | tf_op jit(solution)/shard_map/ppermute | solution.py:616
  99.4 6.4 %collective-permute-start.19 = (f32[14,32,128]{2,1,0:T(8,128)S(1)}, f32[14,32,128]{2,1,0:T(8,128)S(1)}, u32[]{:S(2)}, u32[]{:S(2)}) collective-permute-start(f32[14,32,128]{2,1,0:T(8,128)S(1)} %get-tuple-element.76), channel_id=1, source_target_pairs={{0,2},{2,0},{4,6},{6,4},{8,10},{10,8},{12,14},{14,12},{16,18},{18,... | collective-permute-start | bytes 688136 | tf_op jit(solution)/shard_map/ppermute | solution.py:612

commit v6 on v5

--- a/solution.py
+++ b/solution.py
@@ -167,9 +167,8 @@
     return table
 
 
-def spectral_kernel(*refs):
-    count = len(refs) // 2
-    ins, outs = refs[:count], refs[count:]
+def spectral_kernel(count, chosen, *refs):
+    ins, outs = refs[:count], dict(zip(chosen, refs[count:]))
     fields, rows, _ = ins[0].shape
     tiles = rows // TILE
     first = lax.rem(lax.axis_index("inst"), 2) == 0
@@ -195,10 +194,14 @@
                 odd = odd + (o0 * d0 + o1 * d1)
                 even_next = even_next + (e1 * s0 + e0 * s1)
                 odd_next = odd_next + (o1 * d0 - o0 * d1)
-            outs[ex][f, span] = even + odd
-            outs[4 + ex][f, span] = even - odd
-            outs[2 + ex][f, span] = even_next + odd_next
-            outs[6 + ex][f, span] = even_next - odd_next
+            for k, value in (
+                (ex, even + odd),
+                (4 + ex, even - odd),
+                (2 + ex, even_next + odd_next),
+                (6 + ex, even_next - odd_next),
+            ):
+                if k in outs:
+                    outs[k][f, span] = value
         return 0
 
     lax.fori_loop(0, fields * tiles, step, 0, unroll=4)
@@ -640,7 +643,18 @@
     )
     ends = neighbour(ends, -1)
     link, edge = call(link_kernel, [(3,) + thin, (1,) + thin], raw, ends)
-    specs = call(spectral_kernel, [blocks[0].shape] * instances, *blocks, flops=own.size * 9)
+    head = RETURN[0]
+    others = tuple(k for k in range(instances) if k != head)
+    specs = [None] * instances
+    for chosen in ((head,), others):
+        parts = call(
+            functools.partial(spectral_kernel, instances, chosen),
+            [blocks[0].shape] * len(chosen),
+            *blocks,
+            flops=own.size * len(chosen),
+        )
+        for k, part in zip(chosen, parts):
+            specs[k] = part
     for k in RETURN:
         specs[k] = lax.ppermute(specs[k], "inst", route(*steps[k], instances))
     edge = neighbour(edge, 1)

time: 107 us -> 106 us (level)
    ppermute x7, starting transfers between devices: 11.3 us -> 9.61 us  [body(): specs[k] = lax.ppermute(specs[k], 'inst', route(*steps[k], instances))]
    pallas_call x9 -> x10, Pallas kernels: 2.12 us -> 2.7 us  [call(): return list(run(*operands))]
  transfers between devices with their start and end apart: 20 -> 20, of which waited for: 11 -> 10; matrix products, arithmetic and copies ran while one was open for 0% -> 0% of each run, Pallas kernels for 6% -> 7%
where the time goes in v6:
time: 106 us; the launch traced here: 105 us
  starting transfers between devices  37.3 us (35%)
  blocking collectives  29.8 us (28%)
  waiting for transfers between devices  27.2 us (26%)
  Pallas kernels  10.8 us (10%)
    all_to_all x2, blocking collectives, exchange(): return lax.all_to_all(x, axis, 0, 0, tiled=True, axis_index_groups=groups)  29.8 us
    ppermute x7, starting transfers between devices, body(): blocks[k] = lax.ppermute(blocks[k], 'inst', route(*steps[k], instances))  12.7 us
    ppermute x7, waiting for transfers between devices, body(): blocks[k] = lax.ppermute(blocks[k], 'inst', route(*steps[k], instances))  11.5 us
    ppermute x7, waiting for transfers between devices, body(): specs[k] = lax.ppermute(specs[k], 'inst', route(*steps[k], instances))  10.1 us
    ppermute x7, starting transfers between devices, body(): specs[k] = lax.ppermute(specs[k], 'inst', route(*steps[k], instances))  9.61 us
    ppermute x3, starting transfers between devices, partner(): return lax.ppermute(x, 'ax', swap)  7.58 us
    ppermute x2, starting transfers between devices, neighbour(): return lax.ppermute(x, 'ax', moves)  4.83 us
    ppermute x2, waiting for transfers between devices, neighbour(): return lax.ppermute(x, 'ax', moves)  4.39 us
  transfers between devices with their start and end apart: 20, of which 10 were waited for; matrix products, arithmetic and copies ran while one was open for 0% of the time, Pallas kernels for 7%

profile of v6, /device:TPU:1, one launch (start us, length us, event | category | flops | bytes accessed | tf_op | source)
XLA Modules:
  0.0 105.4 jit_solution(6985582785586804486)
XLA Ops:
  0.0 0.9 shard_map.28.early_ref
  1.0 4.7 %collective-permute-start.5 = (f32[7,64,128]{2,1,0:T(8,128)S(1)}, f32[7,64,128]{2,1,0:T(8,128)S(1)}, u32[]{:S(2)}, u32[]{:S(2)}) collective-permute-start(f32[7,64,128]{2,1,0:T(8,128)S(1)} %shard_map.28.early_ref), channel_id=1, source_target_pairs={{0,160},{32,128},{64,224},{96,192},{128,32},{160,0},{192,96},{224,... | collective-permute-start | bytes 688136 | tf_op jit(solution)/shard_map/ppermute | solution.py:634
  5.7 1.6 %shard_map.29 = (f32[7,64,128]{2,1,0:T(8,128)S(1)}, f32[7,64,128]{2,1,0:T(8,128)S(1)}, f32[7,64,128]{2,1,0:T(8,128)S(1)}, f32[7,64,128]{2,1,0:T(8,128)S(1)}, f32...) custom-call(f32[1,7,8,64,128]{4,3,2,1,0:T(8,128)} %source_ref.1, ...), custom_call_target="tpu_custom_call" | custom-call | bytes 3670016 | tf_op jit(solution)/shard_map/pallas_call | solution.py:146
  7.3 0.3 collective-permute-start.1
  7.6 0.4 collective-permute-start.2
  8.0 0.9 collective-permute-start.3
  8.9 3.5 %collective-permute-start.4 = (f32[7,64,128]{2,1,0:T(8,128)S(1)}, f32[7,64,128]{2,1,0:T(8,128)S(1)}, u32[]{:S(2)}, u32[]{:S(2)}) collective-permute-start(f32[7,64,128]{2,1,0:T(8,128)S(1)} %get-tuple-element.52), channel_id=1, source_target_pairs={{0,128},{32,160},{64,192},{96,224},{128,0},{160,32},{192,64},{224,... | collective-permute-start | bytes 688136 | tf_op jit(solution)/shard_map/ppermute | solution.py:634
  12.4 1.1 %collective-permute-start.6 = (f32[7,64,128]{2,1,0:T(8,128)S(1)}, f32[7,64,128]{2,1,0:T(8,128)S(1)}, u32[]{:S(2)}, u32[]{:S(2)}) collective-permute-start(f32[7,64,128]{2,1,0:T(8,128)S(1)} %get-tuple-element.53), channel_id=1, source_target_pairs={{0,192},{32,224},{64,0},{96,32},{128,64},{160,96},{192,128},{224,1... | collective-permute-start | bytes 688136 | tf_op jit(solution)/shard_map/ppermute | solution.py:634
  13.5 2.4 %collective-permute-done.1.refs_1_ = f32[7,64,128]{2,1,0:T(8,128)S(1)} collective-permute-done((f32[7,64,128]{2,1,0:T(8,128)S(1)}, f32[7,64,128]{2,1,0:T(8,128)S(1)}, u32[]{:S(2)}, u32[]{:S(2)}) %collective-permute-start.1) | collective-permute-done | bytes 229408 | tf_op jit(solution)/shard_map/ppermute | solution.py:634
  15.9 1.7 %collective-permute-start.7 = (f32[7,64,128]{2,1,0:T(8,128)S(1)}, f32[7,64,128]{2,1,0:T(8,128)S(1)}, u32[]{:S(2)}, u32[]{:S(2)}) collective-permute-start(f32[7,64,128]{2,1,0:T(8,128)S(1)} %get-tuple-element.54), channel_id=1, source_target_pairs={{0,224},{32,192},{64,32},{96,0},{128,96},{160,64},{192,160},{224,1... | collective-permute-start | bytes 688136 | tf_op jit(solution)/shard_map/ppermute | solution.py:634
  17.6 0.4 collective-permute-done.2.refs_2_
  18.0 3.7 %collective-permute-done.3.refs_3_ = f32[7,64,128]{2,1,0:T(8,128)S(1)} collective-permute-done((f32[7,64,128]{2,1,0:T(8,128)S(1)}, f32[7,64,128]{2,1,0:T(8,128)S(1)}, u32[]{:S(2)}, u32[]{:S(2)}) %collective-permute-start.3) | collective-permute-done | bytes 229408 | tf_op jit(solution)/shard_map/ppermute | solution.py:634
  21.6 5.0 %collective-permute-done.4.refs_4_ = f32[7,64,128]{2,1,0:T(8,128)S(1)} collective-permute-done((f32[7,64,128]{2,1,0:T(8,128)S(1)}, f32[7,64,128]{2,1,0:T(8,128)S(1)}, u32[]{:S(2)}, u32[]{:S(2)}) %collective-permute-start.4) | collective-permute-done | bytes 229408 | tf_op jit(solution)/shard_map/ppermute | solution.py:634
  26.7 0.0 collective-permute-done.6.refs_6_
  26.7 0.0 collective-permute-done.7.refs_7_
  26.7 0.9 shard_map.31
  27.5 0.7 collective-permute-start.8
  28.3 2.0 %collective-permute-start.9 = (f32[7,64,128]{2,1,0:T(8,128)S(1)}, f32[7,64,128]{2,1,0:T(8,128)S(1)}, u32[]{:S(2)}, u32[]{:S(2)}) collective-permute-start(f32[7,64,128]{2,1,0:T(8,128)S(1)} %get-tuple-element.57), channel_id=1, source_target_pairs={{0,64},{32,96},{64,128},{96,160},{128,192},{160,224},{192,0},{224,... | collective-permute-start | bytes 688136 | tf_op jit(solution)/shard_map/ppermute | solution.py:659
  30.3 2.6 %collective-permute-start = (f32[17,8,128]{2,1,0:T(8,128)S(1)}, f32[17,8,128]{2,1,0:T(8,128)S(1)}, u32[]{:S(2)}, u32[]{:S(2)}) collective-permute-start(f32[17,8,128]{2,1,0:T(8,128)S(1)} %get-tuple-element.41), channel_id=1, source_target_pairs={{0,1},{1,0},{2,3},{3,2},{4,5},{5,4},{6,7},{7,6},{8,9},{9,8},{10,11... | collective-permute-start | bytes 208904 | tf_op jit(solution)/shard_map/ppermute | solution.py:630
  32.9 1.4 %collective-permute-start.11 = (f32[7,64,128]{2,1,0:T(8,128)S(1)}, f32[7,64,128]{2,1,0:T(8,128)S(1)}, u32[]{:S(2)}, u32[]{:S(2)}) collective-permute-start(f32[7,64,128]{2,1,0:T(8,128)S(1)} %get-tuple-element.58), channel_id=1, source_target_pairs={{0,128},{32,160},{64,192},{96,224},{128,0},{160,32},{192,64},{224,... | collective-permute-start | bytes 688136 | tf_op jit(solution)/shard_map/ppermute | solution.py:659
  34.3 1.4 %collective-permute-start.12 = (f32[7,64,128]{2,1,0:T(8,128)S(1)}, f32[7,64,128]{2,1,0:T(8,128)S(1)}, u32[]{:S(2)}, u32[]{:S(2)}) collective-permute-start(f32[7,64,128]{2,1,0:T(8,128)S(1)} %get-tuple-element.59), channel_id=1, source_target_pairs={{0,160},{32,128},{64,224},{96,192},{128,32},{160,0},{192,96},{224,... | collective-permute-start | bytes 688136 | tf_op jit(solution)/shard_map/ppermute | solution.py:659
  35.7 0.6 shard_map.32
  36.3 1.4 %collective-permute-start.13 = (f32[7,64,128]{2,1,0:T(8,128)S(1)}, f32[7,64,128]{2,1,0:T(8,128)S(1)}, u32[]{:S(2)}, u32[]{:S(2)}) collective-permute-start(f32[7,64,128]{2,1,0:T(8,128)S(1)} %get-tuple-element.60), channel_id=1, source_target_pairs={{0,192},{32,224},{64,0},{96,32},{128,64},{160,96},{192,128},{224,1... | collective-permute-start | bytes 688136 | tf_op jit(solution)/shard_map/ppermute | solution.py:659
  37.7 0.0 collective-permute-done.8.refs_1_
  37.7 2.6 %collective-permute-start.14 = (f32[7,64,128]{2,1,0:T(8,128)S(1)}, f32[7,64,128]{2,1,0:T(8,128)S(1)}, u32[]{:S(2)}, u32[]{:S(2)}) collective-permute-start(f32[7,64,128]{2,1,0:T(8,128)S(1)} %get-tuple-element.61), channel_id=1, source_target_pairs={{0,224},{32,192},{64,32},{96,0},{128,96},{160,64},{192,160},{224,1... | collective-permute-start | bytes 688136 | tf_op jit(solution)/shard_map/ppermute | solution.py:659
  40.4 0.0 collective-permute-done.9.refs_2_
  40.4 0.1 broadcast_in_dim.2.flag_ref
  40.5 3.5 %shard_map.30 = (f32[8,7,64,128]{3,2,1,0:T(8,128)S(1)}, f32[8,64,128]{2,1,0:T(8,128)S(1)}, f32[7,64,128]{2,1,0:T(8,128)S(1)}, f32[7,64,128]{2,1,0:T(8,128)S(1)},...) custom-call(f32[1,7,8,64,128]{4,3,2,1,0:T(8,128)} %source_ref.1, ...), custom_call_target="tpu_custom_call" | custom-call | flops 27525120 | bytes 7340032 | tf_op jit(solution)/shard_map/pallas_call | solution.py:584
  44.0 1.8 %collective-permute-done.11.refs_4_ = f32[7,64,128]{2,1,0:T(8,128)S(1)} collective-permute-done((f32[7,64,128]{2,1,0:T(8,128)S(1)}, f32[7,64,128]{2,1,0:T(8,128)S(1)}, u32[]{:S(2)}, u32[]{:S(2)}) %collective-permute-start.11) | collective-permute-done | bytes 229408 | tf_op jit(solution)/shard_map/ppermute | solution.py:659
  45.9 8.2 %collective-permute-done.13.refs_6_ = f32[7,64,128]{2,1,0:T(8,128)S(1)} collective-permute-done((f32[7,64,128]{2,1,0:T(8,128)S(1)}, f32[7,64,128]{2,1,0:T(8,128)S(1)}, u32[]{:S(2)}, u32[]{:S(2)}) %collective-permute-start.13) | collective-permute-done | bytes 229408 | tf_op jit(solution)/shard_map/ppermute | solution.py:659
  54.1 0.5 shard_map.33
  54.6 2.2 %collective-permute-start.15 = (f32[14,32,128]{2,1,0:T(8,128)S(1)}, f32[14,32,128]{2,1,0:T(8,128)S(1)}, u32[]{:S(2)}, u32[]{:S(2)}) collective-permute-start(f32[14,32,128]{2,1,0:T(8,128)S(1)} %get-tuple-element.64), channel_id=1, source_target_pairs={{0,2},{2,0},{4,6},{6,4},{8,10},{10,8},{12,14},{14,12},{16,18},{18,... | collective-permute-start | bytes 688136 | tf_op jit(solution)/shard_map/ppermute | solution.py:615
  56.8 0.1 collective-permute-start.16
  56.9 1.2 %collective-permute-done.16.got_ref = f32[5,32,128]{2,1,0:T(8,128)S(1)} collective-permute-done((f32[5,32,128]{2,1,0:T(8,128)S(1)}, f32[5,32,128]{2,1,0:T(8,128)S(1)}, u32[]{:S(2)}, u32[]{:S(2)}) %collective-permute-start.16) | collective-permute-done | bytes 81952 | tf_op jit(solution)/shard_map/ppermute | solution.py:615
  58.1 1.3 %collective-permute-start.17 = (f32[2,32,128]{2,1,0:T(8,128)S(1)}, f32[2,32,128]{2,1,0:T(8,128)S(1)}, u32[]{:S(2)}, u32[]{:S(2)}) collective-permute-start(f32[2,32,128]{2,1,0:T(8,128)S(1)} %get-tuple-element.69), channel_id=1, source_target_pairs={{4,0},{6,2},{8,4},{10,6},{12,8},{14,10},{16,12},{18,14},{20,16},{2... | collective-permute-start | bytes 98312 | tf_op jit(solution)/shard_map/ppermute | solution.py:619
  59.4 3.5 %collective-permute-done.17.ends_ref = f32[2,32,128]{2,1,0:T(8,128)S(1)} collective-permute-done((f32[2,32,128]{2,1,0:T(8,128)S(1)}, f32[2,32,128]{2,1,0:T(8,128)S(1)}, u32[]{:S(2)}, u32[]{:S(2)}) %collective-permute-start.17) | collective-permute-done | bytes 32800 | tf_op jit(solution)/shard_map/ppermute | solution.py:619
  63.0 3.5 %collective-permute-start.18 = (f32[1,32,128]{2,1,0:T(8,128)S(1)}, f32[1,32,128]{2,1,0:T(8,128)S(1)}, u32[]{:S(2)}, u32[]{:S(2)}) collective-permute-start(f32[1,32,128]{2,1,0:T(8,128)S(1)} %get-tuple-element.71), channel_id=1, source_target_pairs={{0,4},{2,6},{4,8},{6,10},{8,12},{10,14},{12,16},{14,18},{16,20},{1... | collective-permute-start | bytes 49160 | tf_op jit(solution)/shard_map/ppermute | solution.py:619
  66.5 0.9 collective-permute-done.18.edge_ref
  67.4 0.5 shard_map.34
  67.9 0.1 shard_map.38
  68.0 18.5 %all_to_all.10.rhs_ref = f32[8,16,4,128]{3,2,1,0:T(4,128)S(1)} all-to-all(f32[8,16,4,128]{3,2,1,0:T(4,128)S(1)} %get-tuple-element.72), channel_id=1, replica_groups={{0,4,8,12,16,20,24,28},{2,6,10,14,18,22,26,30},{1,5,9,13,17,21,25,29},{..., dimensions={0} | all-to-all | bytes 524288 | tf_op jit(solution)/shard_map/all_to_all | solution.py:598
  86.5 0.1 shard_map.39
  86.6 11.4 %all_to_all.11.solved_ref = f32[8,14,4,128]{3,2,1,0:T(4,128)S(1)} all-to-all(f32[8,14,4,128]{3,2,1,0:T(4,128)S(1)} %shard_map.39), channel_id=1, replica_groups={{0,4,8,12,16,20,24,28},{2,6,10,14,18,22,26,30},{1,5,9,13,17,21,25,29},{..., dimensions={0} | all-to-all | bytes 458752 | tf_op jit(solution)/shard_map/all_to_all | solution.py:598
  97.9 0.1 shard_map.40
  98.0 5.2 %collective-permute-start.19 = (f32[14,32,128]{2,1,0:T(8,128)S(1)}, f32[14,32,128]{2,1,0:T(8,128)S(1)}, u32[]{:S(2)}, u32[]{:S(2)}) collective-permute-start(f32[14,32,128]{2,1,0:T(8,128)S(1)} %get-tuple-element.74), channel_id=1, source_target_pairs={{0,2},{2,0},{4,6},{6,4},{8,10},{10,8},{12,14},{14,12},{16,18},{18,... | collective-permute-start | bytes 688136 | tf_op jit(solution)/shard_map/ppermute | solution.py:615
  103.3 1.0 shard_map.41.refs_0_
  104.3 0.1 collective-permute-done.19.ends_ref
  104.4 1.0 shard_map.42
  (13 shorter events, 0.1 us)
Async XLA Ops:
  1.0 11.5 %collective-permute-start.5 = (f32[7,64,128]{2,1,0:T(8,128)S(1)}, f32[7,64,128]{2,1,0:T(8,128)S(1)}, u32[]{:S(2)}, u32[]{:S(2)}) collective-permute-start(f32[7,64,128]{2,1,0:T(8,128)S(1)} %shard_map.28.early_ref), channel_id=1, source_target_pairs={{0,160},{32,128},{64,224},{96,192},{128,32},{160,0},{192,96},{224,... | collective-permute-start | bytes 688136 | tf_op jit(solution)/shard_map/ppermute | solution.py:634
  7.3 8.6 %collective-permute-start.1 = (f32[7,64,128]{2,1,0:T(8,128)S(1)}, f32[7,64,128]{2,1,0:T(8,128)S(1)}, u32[]{:S(2)}, u32[]{:S(2)}) collective-permute-start(f32[7,64,128]{2,1,0:T(8,128)S(1)} %get-tuple-element.49), channel_id=1, source_target_pairs={{0,32},{32,0},{64,96},{96,64},{128,160},{160,128},{192,224},{224,1... | collective-permute-start | bytes 688136 | tf_op jit(solution)/shard_map/ppermute | solution.py:634
  7.6 10.4 %collective-permute-start.2 = (f32[7,64,128]{2,1,0:T(8,128)S(1)}, f32[7,64,128]{2,1,0:T(8,128)S(1)}, u32[]{:S(2)}, u32[]{:S(2)}) collective-permute-start(f32[7,64,128]{2,1,0:T(8,128)S(1)} %get-tuple-element.50), channel_id=1, source_target_pairs={{0,64},{32,96},{64,128},{96,160},{128,192},{160,224},{192,0},{224,... | collective-permute-start | bytes 688136 | tf_op jit(solution)/shard_map/ppermute | solution.py:634
  8.0 13.6 %collective-permute-start.3 = (f32[7,64,128]{2,1,0:T(8,128)S(1)}, f32[7,64,128]{2,1,0:T(8,128)S(1)}, u32[]{:S(2)}, u32[]{:S(2)}) collective-permute-start(f32[7,64,128]{2,1,0:T(8,128)S(1)} %get-tuple-element.51), channel_id=1, source_target_pairs={{0,96},{32,64},{64,160},{96,128},{128,224},{160,192},{192,32},{224... | collective-permute-start | bytes 688136 | tf_op jit(solution)/shard_map/ppermute | solution.py:634
  8.9 17.7 %collective-permute-start.4 = (f32[7,64,128]{2,1,0:T(8,128)S(1)}, f32[7,64,128]{2,1,0:T(8,128)S(1)}, u32[]{:S(2)}, u32[]{:S(2)}) collective-permute-start(f32[7,64,128]{2,1,0:T(8,128)S(1)} %get-tuple-element.52), channel_id=1, source_target_pairs={{0,128},{32,160},{64,192},{96,224},{128,0},{160,32},{192,64},{224,... | collective-permute-start | bytes 688136 | tf_op jit(solution)/shard_map/ppermute | solution.py:634
  12.4 14.2 %collective-permute-start.6 = (f32[7,64,128]{2,1,0:T(8,128)S(1)}, f32[7,64,128]{2,1,0:T(8,128)S(1)}, u32[]{:S(2)}, u32[]{:S(2)}) collective-permute-start(f32[7,64,128]{2,1,0:T(8,128)S(1)} %get-tuple-element.53), channel_id=1, source_target_pairs={{0,192},{32,224},{64,0},{96,32},{128,64},{160,96},{192,128},{224,1... | collective-permute-start | bytes 688136 | tf_op jit(solution)/shard_map/ppermute | solution.py:634
  15.9 10.8 %collective-permute-start.7 = (f32[7,64,128]{2,1,0:T(8,128)S(1)}, f32[7,64,128]{2,1,0:T(8,128)S(1)}, u32[]{:S(2)}, u32[]{:S(2)}) collective-permute-start(f32[7,64,128]{2,1,0:T(8,128)S(1)} %get-tuple-element.54), channel_id=1, source_target_pairs={{0,224},{32,192},{64,32},{96,0},{128,96},{160,64},{192,160},{224,1... | collective-permute-start | bytes 688136 | tf_op jit(solution)/shard_map/ppermute | solution.py:634
  26.7 13.7 %copy-start = (s32[1,8,64]{2,1,0:T(8,128)S(1)}, s32[1,8,64]{2,1,0:T(8,128)}, u32[]{:S(2)}) copy-start(s32[1,8,64]{2,1,0:T(8,128)} %flag_ref.1) | copy-start | bytes 6148
  27.5 10.2 %collective-permute-start.8 = (f32[7,64,128]{2,1,0:T(8,128)S(1)}, f32[7,64,128]{2,1,0:T(8,128)S(1)}, u32[]{:S(2)}, u32[]{:S(2)}) collective-permute-start(f32[7,64,128]{2,1,0:T(8,128)S(1)} %get-tuple-element.56), channel_id=1, source_target_pairs={{0,32},{32,0},{64,96},{96,64},{128,160},{160,128},{192,224},{224,1... | collective-permute-start | bytes 688136 | tf_op jit(solution)/shard_map/ppermute | solution.py:659
  28.3 12.1 %collective-permute-start.9 = (f32[7,64,128]{2,1,0:T(8,128)S(1)}, f32[7,64,128]{2,1,0:T(8,128)S(1)}, u32[]{:S(2)}, u32[]{:S(2)}) collective-permute-start(f32[7,64,128]{2,1,0:T(8,128)S(1)} %get-tuple-element.57), channel_id=1, source_target_pairs={{0,64},{32,96},{64,128},{96,160},{128,192},{160,224},{192,0},{224,... | collective-permute-start | bytes 688136 | tf_op jit(solution)/shard_map/ppermute | solution.py:659
  30.3 6.0 %collective-permute-start = (f32[17,8,128]{2,1,0:T(8,128)S(1)}, f32[17,8,128]{2,1,0:T(8,128)S(1)}, u32[]{:S(2)}, u32[]{:S(2)}) collective-permute-start(f32[17,8,128]{2,1,0:T(8,128)S(1)} %get-tuple-element.41), channel_id=1, source_target_pairs={{0,1},{1,0},{2,3},{3,2},{4,5},{5,4},{6,7},{7,6},{8,9},{9,8},{10,11... | collective-permute-start | bytes 208904 | tf_op jit(solution)/shard_map/ppermute | solution.py:630
  32.9 13.0 %collective-permute-start.11 = (f32[7,64,128]{2,1,0:T(8,128)S(1)}, f32[7,64,128]{2,1,0:T(8,128)S(1)}, u32[]{:S(2)}, u32[]{:S(2)}) collective-permute-start(f32[7,64,128]{2,1,0:T(8,128)S(1)} %get-tuple-element.58), channel_id=1, source_target_pairs={{0,128},{32,160},{64,192},{96,224},{128,0},{160,32},{192,64},{224,... | collective-permute-start | bytes 688136 | tf_op jit(solution)/shard_map/ppermute | solution.py:659
  34.3 11.6 %collective-permute-start.12 = (f32[7,64,128]{2,1,0:T(8,128)S(1)}, f32[7,64,128]{2,1,0:T(8,128)S(1)}, u32[]{:S(2)}, u32[]{:S(2)}) collective-permute-start(f32[7,64,128]{2,1,0:T(8,128)S(1)} %get-tuple-element.59), channel_id=1, source_target_pairs={{0,160},{32,128},{64,224},{96,192},{128,32},{160,0},{192,96},{224,... | collective-permute-start | bytes 688136 | tf_op jit(solution)/shard_map/ppermute | solution.py:659
  36.3 17.8 %collective-permute-start.13 = (f32[7,64,128]{2,1,0:T(8,128)S(1)}, f32[7,64,128]{2,1,0:T(8,128)S(1)}, u32[]{:S(2)}, u32[]{:S(2)}) collective-permute-start(f32[7,64,128]{2,1,0:T(8,128)S(1)} %get-tuple-element.60), channel_id=1, source_target_pairs={{0,192},{32,224},{64,0},{96,32},{128,64},{160,96},{192,128},{224,1... | collective-permute-start | bytes 688136 | tf_op jit(solution)/shard_map/ppermute | solution.py:659
  37.7 16.4 %collective-permute-start.14 = (f32[7,64,128]{2,1,0:T(8,128)S(1)}, f32[7,64,128]{2,1,0:T(8,128)S(1)}, u32[]{:S(2)}, u32[]{:S(2)}) collective-permute-start(f32[7,64,128]{2,1,0:T(8,128)S(1)} %get-tuple-element.61), channel_id=1, source_target_pairs={{0,224},{32,192},{64,32},{96,0},{128,96},{160,64},{192,160},{224,1... | collective-permute-start | bytes 688136 | tf_op jit(solution)/shard_map/ppermute | solution.py:659
  40.4 13.8 %collective-permute-start.10 = (f32[7,64,128]{2,1,0:T(8,128)S(1)}, f32[7,64,128]{2,1,0:T(8,128)S(1)}, u32[]{:S(2)}, u32[]{:S(2)}) collective-permute-start(f32[7,64,128]{2,1,0:T(8,128)S(1)} %shard_map.32), channel_id=1, source_target_pairs={{0,96},{32,64},{64,160},{96,128},{128,224},{160,192},{192,32},{224... | collective-permute-start | bytes 688136 | tf_op jit(solution)/shard_map/ppermute | solution.py:659
  54.6 13.3 %collective-permute-start.15 = (f32[14,32,128]{2,1,0:T(8,128)S(1)}, f32[14,32,128]{2,1,0:T(8,128)S(1)}, u32[]{:S(2)}, u32[]{:S(2)}) collective-permute-start(f32[14,32,128]{2,1,0:T(8,128)S(1)} %get-tuple-element.64), channel_id=1, source_target_pairs={{0,2},{2,0},{4,6},{6,4},{8,10},{10,8},{12,14},{14,12},{16,18},{18,... | collective-permute-start | bytes 688136 | tf_op jit(solution)/shard_map/ppermute | solution.py:615
  56.8 1.3 %collective-permute-start.16 = (f32[5,32,128]{2,1,0:T(8,128)S(1)}, f32[5,32,128]{2,1,0:T(8,128)S(1)}, u32[]{:S(2)}, u32[]{:S(2)}) collective-permute-start(f32[5,32,128]{2,1,0:T(8,128)S(1)} %get-tuple-element.66), channel_id=1, source_target_pairs={{0,2},{2,0},{4,6},{6,4},{8,10},{10,8},{12,14},{14,12},{16,18},{18,... | collective-permute-start | bytes 245768 | tf_op jit(solution)/shard_map/ppermute | solution.py:615
  58.1 4.8 %collective-permute-start.17 = (f32[2,32,128]{2,1,0:T(8,128)S(1)}, f32[2,32,128]{2,1,0:T(8,128)S(1)}, u32[]{:S(2)}, u32[]{:S(2)}) collective-permute-start(f32[2,32,128]{2,1,0:T(8,128)S(1)} %get-tuple-element.69), channel_id=1, source_target_pairs={{4,0},{6,2},{8,4},{10,6},{12,8},{14,10},{16,12},{18,14},{20,16},{2... | collective-permute-start | bytes 98312 | tf_op jit(solution)/shard_map/ppermute | solution.py:619
  63.0 4.4 %collective-permute-start.18 = (f32[1,32,128]{2,1,0:T(8,128)S(1)}, f32[1,32,128]{2,1,0:T(8,128)S(1)}, u32[]{:S(2)}, u32[]{:S(2)}) collective-permute-start(f32[1,32,128]{2,1,0:T(8,128)S(1)} %get-tuple-element.71), channel_id=1, source_target_pairs={{0,4},{2,6},{4,8},{6,10},{8,12},{10,14},{12,16},{14,18},{16,20},{1... | collective-permute-start | bytes 49160 | tf_op jit(solution)/shard_map/ppermute | solution.py:619
  98.0 6.4 %collective-permute-start.19 = (f32[14,32,128]{2,1,0:T(8,128)S(1)}, f32[14,32,128]{2,1,0:T(8,128)S(1)}, u32[]{:S(2)}, u32[]{:S(2)}) collective-permute-start(f32[14,32,128]{2,1,0:T(8,128)S(1)} %get-tuple-element.74), channel_id=1, source_target_pairs={{0,2},{2,0},{4,6},{6,4},{8,10},{10,8},{12,14},{14,12},{16,18},{18,... | collective-permute-start | bytes 688136 | tf_op jit(solution)/shard_map/ppermute | solution.py:615

commit v7 on v6

--- a/solution.py
+++ b/solution.py
@@ -21,7 +21,7 @@
 
 FIELDS = 7
 ORDER = (5, 7, 3, 4, 1, 2, 6)
-RETURN = (3, 4, 5, 7, 1, 2, 6)
+RETURN = (3, 7, 4, 5, 1, 2, 6)
 EDGES = 2 * FIELDS + 3
 COEFS = 5
 TILE = 8
@@ -85,11 +85,16 @@
     ]
 
 
-def first_kernel(count, chosen, state_ref, out_ref, sem):
+def first_kernel(count, chosen, state_ref, out_ref, sems):
     (place,) = places_of(count, (chosen,))
-    copy = pltpu.make_async_copy(state_ref.at[0, :, place], out_ref, sem)
-    copy.start()
-    copy.wait()
+    copies = [
+        pltpu.make_async_copy(state_ref.at[0, f, place], out_ref.at[f], sems.at[f])
+        for f in range(out_ref.shape[0])
+    ]
+    for copy in copies:
+        copy.start()
+    for copy in copies:
+        copy.wait()
 
 
 def rest_kernel(count, chosen, state_ref, flag_ref, early_ref, *refs):
@@ -131,7 +136,7 @@
         out_shape=jax.ShapeDtypeStruct((fields, rows, lanes), jnp.float32),
         in_specs=[pl.BlockSpec(memory_space=pltpu.HBM)],
         out_specs=VMEM,
-        scratch_shapes=[pltpu.SemaphoreType.DMA],
+        scratch_shapes=[pltpu.SemaphoreType.DMA((fields,))],
         compiler_params=pltpu.CompilerParams(vmem_limit_bytes=4 << 20),
         cost_estimate=pl.CostEstimate(
             flops=0, bytes_accessed=fields * rows * lanes * 8, transcendentals=0

time: 106 us -> 106 us (level)
  no operation moved by 1% of the time
where the time goes in v7:
time: 106 us; the launch traced here: 105 us
  starting transfers between devices  37.3 us (35%)
  blocking collectives  29.8 us (28%)
  waiting for transfers between devices  27.2 us (26%)
  Pallas kernels  10.7 us (10%)
    all_to_all x2, blocking collectives, exchange(): return lax.all_to_all(x, axis, 0, 0, tiled=True, axis_index_groups=groups)  29.8 us
    ppermute x7, starting transfers between devices, body(): blocks[k] = lax.ppermute(blocks[k], 'inst', route(*steps[k], instances))  12.7 us
    ppermute x7, waiting for transfers between devices, body(): blocks[k] = lax.ppermute(blocks[k], 'inst', route(*steps[k], instances))  11.5 us
    ppermute x7, waiting for transfers between devices, body(): specs[k] = lax.ppermute(specs[k], 'inst', route(*steps[k], instances))  10.1 us
    ppermute x7, starting transfers between devices, body(): specs[k] = lax.ppermute(specs[k], 'inst', route(*steps[k], instances))  9.61 us
    ppermute x3, starting transfers between devices, partner(): return lax.ppermute(x, 'ax', swap)  7.58 us
    ppermute x2, starting transfers between devices, neighbour(): return lax.ppermute(x, 'ax', moves)  4.83 us
    ppermute x2, waiting for transfers between devices, neighbour(): return lax.ppermute(x, 'ax', moves)  4.39 us
  transfers between devices with their start and end apart: 20, of which 10 were waited for; matrix products, arithmetic and copies ran while one was open for 0% of the time, Pallas kernels for 7%

profile of v7, /device:TPU:1, one launch (start us, length us, event | category | flops | bytes accessed | tf_op | source)
XLA Modules:
  0.0 105.4 jit_solution(12617049920739997670)
XLA Ops:
  0.0 0.9 shard_map.28.early_ref
  0.9 4.7 %collective-permute-start.5 = (f32[7,64,128]{2,1,0:T(8,128)S(1)}, f32[7,64,128]{2,1,0:T(8,128)S(1)}, u32[]{:S(2)}, u32[]{:S(2)}) collective-permute-start(f32[7,64,128]{2,1,0:T(8,128)S(1)} %shard_map.28.early_ref), channel_id=1, source_target_pairs={{0,160},{32,128},{64,224},{96,192},{128,32},{160,0},{192,96},{224,... | collective-permute-start | bytes 688136 | tf_op jit(solution)/shard_map/ppermute | solution.py:639
  5.7 1.6 %shard_map.29 = (f32[7,64,128]{2,1,0:T(8,128)S(1)}, f32[7,64,128]{2,1,0:T(8,128)S(1)}, f32[7,64,128]{2,1,0:T(8,128)S(1)}, f32[7,64,128]{2,1,0:T(8,128)S(1)}, f32...) custom-call(f32[1,7,8,64,128]{4,3,2,1,0:T(8,128)} %source_ref.1, ...), custom_call_target="tpu_custom_call" | custom-call | bytes 3670016 | tf_op jit(solution)/shard_map/pallas_call | solution.py:151
  7.2 0.3 collective-permute-start.1
  7.6 0.4 collective-permute-start.2
  8.0 0.9 collective-permute-start.3
  8.9 3.5 %collective-permute-start.4 = (f32[7,64,128]{2,1,0:T(8,128)S(1)}, f32[7,64,128]{2,1,0:T(8,128)S(1)}, u32[]{:S(2)}, u32[]{:S(2)}) collective-permute-start(f32[7,64,128]{2,1,0:T(8,128)S(1)} %get-tuple-element.52), channel_id=1, source_target_pairs={{0,128},{32,160},{64,192},{96,224},{128,0},{160,32},{192,64},{224,... | collective-permute-start | bytes 688136 | tf_op jit(solution)/shard_map/ppermute | solution.py:639
  12.4 1.1 %collective-permute-start.6 = (f32[7,64,128]{2,1,0:T(8,128)S(1)}, f32[7,64,128]{2,1,0:T(8,128)S(1)}, u32[]{:S(2)}, u32[]{:S(2)}) collective-permute-start(f32[7,64,128]{2,1,0:T(8,128)S(1)} %get-tuple-element.53), channel_id=1, source_target_pairs={{0,192},{32,224},{64,0},{96,32},{128,64},{160,96},{192,128},{224,1... | collective-permute-start | bytes 688136 | tf_op jit(solution)/shard_map/ppermute | solution.py:639
  13.5 2.4 %collective-permute-done.1.refs_1_ = f32[7,64,128]{2,1,0:T(8,128)S(1)} collective-permute-done((f32[7,64,128]{2,1,0:T(8,128)S(1)}, f32[7,64,128]{2,1,0:T(8,128)S(1)}, u32[]{:S(2)}, u32[]{:S(2)}) %collective-permute-start.1) | collective-permute-done | bytes 229408 | tf_op jit(solution)/shard_map/ppermute | solution.py:639
  15.9 1.7 %collective-permute-start.7 = (f32[7,64,128]{2,1,0:T(8,128)S(1)}, f32[7,64,128]{2,1,0:T(8,128)S(1)}, u32[]{:S(2)}, u32[]{:S(2)}) collective-permute-start(f32[7,64,128]{2,1,0:T(8,128)S(1)} %get-tuple-element.54), channel_id=1, source_target_pairs={{0,224},{32,192},{64,32},{96,0},{128,96},{160,64},{192,160},{224,1... | collective-permute-start | bytes 688136 | tf_op jit(solution)/shard_map/ppermute | solution.py:639
  17.6 0.4 collective-permute-done.2.refs_2_
  17.9 3.7 %collective-permute-done.3.refs_3_ = f32[7,64,128]{2,1,0:T(8,128)S(1)} collective-permute-done((f32[7,64,128]{2,1,0:T(8,128)S(1)}, f32[7,64,128]{2,1,0:T(8,128)S(1)}, u32[]{:S(2)}, u32[]{:S(2)}) %collective-permute-start.3) | collective-permute-done | bytes 229408 | tf_op jit(solution)/shard_map/ppermute | solution.py:639
  21.6 5.0 %collective-permute-done.4.refs_4_ = f32[7,64,128]{2,1,0:T(8,128)S(1)} collective-permute-done((f32[7,64,128]{2,1,0:T(8,128)S(1)}, f32[7,64,128]{2,1,0:T(8,128)S(1)}, u32[]{:S(2)}, u32[]{:S(2)}) %collective-permute-start.4) | collective-permute-done | bytes 229408 | tf_op jit(solution)/shard_map/ppermute | solution.py:639
  26.6 0.9 shard_map.31
  27.5 0.7 collective-permute-start.8
  28.3 2.0 %collective-permute-start.9 = (f32[7,64,128]{2,1,0:T(8,128)S(1)}, f32[7,64,128]{2,1,0:T(8,128)S(1)}, u32[]{:S(2)}, u32[]{:S(2)}) collective-permute-start(f32[7,64,128]{2,1,0:T(8,128)S(1)} %get-tuple-element.57), channel_id=1, source_target_pairs={{0,64},{32,96},{64,128},{96,160},{128,192},{160,224},{192,0},{224,... | collective-permute-start | bytes 688136 | tf_op jit(solution)/shard_map/ppermute | solution.py:664
  30.3 2.6 %collective-permute-start = (f32[17,8,128]{2,1,0:T(8,128)S(1)}, f32[17,8,128]{2,1,0:T(8,128)S(1)}, u32[]{:S(2)}, u32[]{:S(2)}) collective-permute-start(f32[17,8,128]{2,1,0:T(8,128)S(1)} %get-tuple-element.41), channel_id=1, source_target_pairs={{0,1},{1,0},{2,3},{3,2},{4,5},{5,4},{6,7},{7,6},{8,9},{9,8},{10,11... | collective-permute-start | bytes 208904 | tf_op jit(solution)/shard_map/ppermute | solution.py:635
  32.9 1.4 %collective-permute-start.11 = (f32[7,64,128]{2,1,0:T(8,128)S(1)}, f32[7,64,128]{2,1,0:T(8,128)S(1)}, u32[]{:S(2)}, u32[]{:S(2)}) collective-permute-start(f32[7,64,128]{2,1,0:T(8,128)S(1)} %get-tuple-element.58), channel_id=1, source_target_pairs={{0,128},{32,160},{64,192},{96,224},{128,0},{160,32},{192,64},{224,... | collective-permute-start | bytes 688136 | tf_op jit(solution)/shard_map/ppermute | solution.py:664
  34.3 1.4 %collective-permute-start.12 = (f32[7,64,128]{2,1,0:T(8,128)S(1)}, f32[7,64,128]{2,1,0:T(8,128)S(1)}, u32[]{:S(2)}, u32[]{:S(2)}) collective-permute-start(f32[7,64,128]{2,1,0:T(8,128)S(1)} %get-tuple-element.59), channel_id=1, source_target_pairs={{0,160},{32,128},{64,224},{96,192},{128,32},{160,0},{192,96},{224,... | collective-permute-start | bytes 688136 | tf_op jit(solution)/shard_map/ppermute | solution.py:664
  35.7 0.6 shard_map.32
  36.3 1.4 %collective-permute-start.13 = (f32[7,64,128]{2,1,0:T(8,128)S(1)}, f32[7,64,128]{2,1,0:T(8,128)S(1)}, u32[]{:S(2)}, u32[]{:S(2)}) collective-permute-start(f32[7,64,128]{2,1,0:T(8,128)S(1)} %get-tuple-element.60), channel_id=1, source_target_pairs={{0,192},{32,224},{64,0},{96,32},{128,64},{160,96},{192,128},{224,1... | collective-permute-start | bytes 688136 | tf_op jit(solution)/shard_map/ppermute | solution.py:664
  37.7 0.0 collective-permute-done.8.refs_1_
  37.7 2.6 %collective-permute-start.14 = (f32[7,64,128]{2,1,0:T(8,128)S(1)}, f32[7,64,128]{2,1,0:T(8,128)S(1)}, u32[]{:S(2)}, u32[]{:S(2)}) collective-permute-start(f32[7,64,128]{2,1,0:T(8,128)S(1)} %get-tuple-element.61), channel_id=1, source_target_pairs={{0,224},{32,192},{64,32},{96,0},{128,96},{160,64},{192,160},{224,1... | collective-permute-start | bytes 688136 | tf_op jit(solution)/shard_map/ppermute | solution.py:664
  40.3 0.0 collective-permute-done.9.refs_2_
  40.3 0.0 collective-permute-start.10
  40.3 0.1 broadcast_in_dim.2.flag_ref
  40.5 3.5 %shard_map.30 = (f32[8,7,64,128]{3,2,1,0:T(8,128)S(1)}, f32[8,64,128]{2,1,0:T(8,128)S(1)}, f32[7,64,128]{2,1,0:T(8,128)S(1)}, f32[7,64,128]{2,1,0:T(8,128)S(1)},...) custom-call(f32[1,7,8,64,128]{4,3,2,1,0:T(8,128)} %source_ref.1, ...), custom_call_target="tpu_custom_call" | custom-call | flops 27525120 | bytes 7340032 | tf_op jit(solution)/shard_map/pallas_call | solution.py:589
  44.0 1.8 %collective-permute-done.11.refs_4_ = f32[7,64,128]{2,1,0:T(8,128)S(1)} collective-permute-done((f32[7,64,128]{2,1,0:T(8,128)S(1)}, f32[7,64,128]{2,1,0:T(8,128)S(1)}, u32[]{:S(2)}, u32[]{:S(2)}) %collective-permute-start.11) | collective-permute-done | bytes 229408 | tf_op jit(solution)/shard_map/ppermute | solution.py:664
  45.8 8.2 %collective-permute-done.13.refs_6_ = f32[7,64,128]{2,1,0:T(8,128)S(1)} collective-permute-done((f32[7,64,128]{2,1,0:T(8,128)S(1)}, f32[7,64,128]{2,1,0:T(8,128)S(1)}, u32[]{:S(2)}, u32[]{:S(2)}) %collective-permute-start.13) | collective-permute-done | bytes 229408 | tf_op jit(solution)/shard_map/ppermute | solution.py:664
  54.1 0.0 collective-permute-done.14.refs_7_
  54.1 0.5 shard_map.33
  54.5 2.2 %collective-permute-start.15 = (f32[14,32,128]{2,1,0:T(8,128)S(1)}, f32[14,32,128]{2,1,0:T(8,128)S(1)}, u32[]{:S(2)}, u32[]{:S(2)}) collective-permute-start(f32[14,32,128]{2,1,0:T(8,128)S(1)} %get-tuple-element.64), channel_id=1, source_target_pairs={{0,2},{2,0},{4,6},{6,4},{8,10},{10,8},{12,14},{14,12},{16,18},{18,... | collective-permute-start | bytes 688136 | tf_op jit(solution)/shard_map/ppermute | solution.py:620
  56.8 0.1 collective-permute-start.16
  56.9 1.2 %collective-permute-done.16.got_ref = f32[5,32,128]{2,1,0:T(8,128)S(1)} collective-permute-done((f32[5,32,128]{2,1,0:T(8,128)S(1)}, f32[5,32,128]{2,1,0:T(8,128)S(1)}, u32[]{:S(2)}, u32[]{:S(2)}) %collective-permute-start.16) | collective-permute-done | bytes 81952 | tf_op jit(solution)/shard_map/ppermute | solution.py:620
  58.1 1.3 %collective-permute-start.17 = (f32[2,32,128]{2,1,0:T(8,128)S(1)}, f32[2,32,128]{2,1,0:T(8,128)S(1)}, u32[]{:S(2)}, u32[]{:S(2)}) collective-permute-start(f32[2,32,128]{2,1,0:T(8,128)S(1)} %get-tuple-element.69), channel_id=1, source_target_pairs={{4,0},{6,2},{8,4},{10,6},{12,8},{14,10},{16,12},{18,14},{20,16},{2... | collective-permute-start | bytes 98312 | tf_op jit(solution)/shard_map/ppermute | solution.py:624
  59.4 3.5 %collective-permute-done.17.ends_ref = f32[2,32,128]{2,1,0:T(8,128)S(1)} collective-permute-done((f32[2,32,128]{2,1,0:T(8,128)S(1)}, f32[2,32,128]{2,1,0:T(8,128)S(1)}, u32[]{:S(2)}, u32[]{:S(2)}) %collective-permute-start.17) | collective-permute-done | bytes 32800 | tf_op jit(solution)/shard_map/ppermute | solution.py:624
  62.9 3.5 %collective-permute-start.18 = (f32[1,32,128]{2,1,0:T(8,128)S(1)}, f32[1,32,128]{2,1,0:T(8,128)S(1)}, u32[]{:S(2)}, u32[]{:S(2)}) collective-permute-start(f32[1,32,128]{2,1,0:T(8,128)S(1)} %get-tuple-element.71), channel_id=1, source_target_pairs={{0,4},{2,6},{4,8},{6,10},{8,12},{10,14},{12,16},{14,18},{16,20},{1... | collective-permute-start | bytes 49160 | tf_op jit(solution)/shard_map/ppermute | solution.py:624
  66.5 0.9 collective-permute-done.18.edge_ref
  67.4 0.5 shard_map.34
  67.8 0.1 shard_map.38
  68.0 18.5 %all_to_all.10.rhs_ref = f32[8,16,4,128]{3,2,1,0:T(4,128)S(1)} all-to-all(f32[8,16,4,128]{3,2,1,0:T(4,128)S(1)} %get-tuple-element.72), channel_id=1, replica_groups={{0,4,8,12,16,20,24,28},{2,6,10,14,18,22,26,30},{1,5,9,13,17,21,25,29},{..., dimensions={0} | all-to-all | bytes 524288 | tf_op jit(solution)/shard_map/all_to_all | solution.py:603
  86.4 0.1 shard_map.39
  86.5 11.4 %all_to_all.11.solved_ref = f32[8,14,4,128]{3,2,1,0:T(4,128)S(1)} all-to-all(f32[8,14,4,128]{3,2,1,0:T(4,128)S(1)} %shard_map.39), channel_id=1, replica_groups={{0,4,8,12,16,20,24,28},{2,6,10,14,18,22,26,30},{1,5,9,13,17,21,25,29},{..., dimensions={0} | all-to-all | bytes 458752 | tf_op jit(solution)/shard_map/all_to_all | solution.py:603
  97.9 0.1 shard_map.40
  98.0 5.2 %collective-permute-start.19 = (f32[14,32,128]{2,1,0:T(8,128)S(1)}, f32[14,32,128]{2,1,0:T(8,128)S(1)}, u32[]{:S(2)}, u32[]{:S(2)}) collective-permute-start(f32[14,32,128]{2,1,0:T(8,128)S(1)} %get-tuple-element.74), channel_id=1, source_target_pairs={{0,2},{2,0},{4,6},{6,4},{8,10},{10,8},{12,14},{14,12},{16,18},{18,... | collective-permute-start | bytes 688136 | tf_op jit(solution)/shard_map/ppermute | solution.py:620
  103.2 1.0 shard_map.41.refs_0_
  104.3 0.1 collective-permute-done.19.ends_ref
  104.4 1.0 shard_map.42
  (13 shorter events, 0.1 us)
Async XLA Ops:
  0.9 11.5 %collective-permute-start.5 = (f32[7,64,128]{2,1,0:T(8,128)S(1)}, f32[7,64,128]{2,1,0:T(8,128)S(1)}, u32[]{:S(2)}, u32[]{:S(2)}) collective-permute-start(f32[7,64,128]{2,1,0:T(8,128)S(1)} %shard_map.28.early_ref), channel_id=1, source_target_pairs={{0,160},{32,128},{64,224},{96,192},{128,32},{160,0},{192,96},{224,... | collective-permute-start | bytes 688136 | tf_op jit(solution)/shard_map/ppermute | solution.py:639
  7.2 8.6 %collective-permute-start.1 = (f32[7,64,128]{2,1,0:T(8,128)S(1)}, f32[7,64,128]{2,1,0:T(8,128)S(1)}, u32[]{:S(2)}, u32[]{:S(2)}) collective-permute-start(f32[7,64,128]{2,1,0:T(8,128)S(1)} %get-tuple-element.49), channel_id=1, source_target_pairs={{0,32},{32,0},{64,96},{96,64},{128,160},{160,128},{192,224},{224,1... | collective-permute-start | bytes 688136 | tf_op jit(solution)/shard_map/ppermute | solution.py:639
  7.6 10.4 %collective-permute-start.2 = (f32[7,64,128]{2,1,0:T(8,128)S(1)}, f32[7,64,128]{2,1,0:T(8,128)S(1)}, u32[]{:S(2)}, u32[]{:S(2)}) collective-permute-start(f32[7,64,128]{2,1,0:T(8,128)S(1)} %get-tuple-element.50), channel_id=1, source_target_pairs={{0,64},{32,96},{64,128},{96,160},{128,192},{160,224},{192,0},{224,... | collective-permute-start | bytes 688136 | tf_op jit(solution)/shard_map/ppermute | solution.py:639
  8.0 13.6 %collective-permute-start.3 = (f32[7,64,128]{2,1,0:T(8,128)S(1)}, f32[7,64,128]{2,1,0:T(8,128)S(1)}, u32[]{:S(2)}, u32[]{:S(2)}) collective-permute-start(f32[7,64,128]{2,1,0:T(8,128)S(1)} %get-tuple-element.51), channel_id=1, source_target_pairs={{0,96},{32,64},{64,160},{96,128},{128,224},{160,192},{192,32},{224... | collective-permute-start | bytes 688136 | tf_op jit(solution)/shard_map/ppermute | solution.py:639
  8.9 17.7 %collective-permute-start.4 = (f32[7,64,128]{2,1,0:T(8,128)S(1)}, f32[7,64,128]{2,1,0:T(8,128)S(1)}, u32[]{:S(2)}, u32[]{:S(2)}) collective-permute-start(f32[7,64,128]{2,1,0:T(8,128)S(1)} %get-tuple-element.52), channel_id=1, source_target_pairs={{0,128},{32,160},{64,192},{96,224},{128,0},{160,32},{192,64},{224,... | collective-permute-start | bytes 688136 | tf_op jit(solution)/shard_map/ppermute | solution.py:639
  12.4 14.2 %collective-permute-start.6 = (f32[7,64,128]{2,1,0:T(8,128)S(1)}, f32[7,64,128]{2,1,0:T(8,128)S(1)}, u32[]{:S(2)}, u32[]{:S(2)}) collective-permute-start(f32[7,64,128]{2,1,0:T(8,128)S(1)} %get-tuple-element.53), channel_id=1, source_target_pairs={{0,192},{32,224},{64,0},{96,32},{128,64},{160,96},{192,128},{224,1... | collective-permute-start | bytes 688136 | tf_op jit(solution)/shard_map/ppermute | solution.py:639
  15.9 10.8 %collective-permute-start.7 = (f32[7,64,128]{2,1,0:T(8,128)S(1)}, f32[7,64,128]{2,1,0:T(8,128)S(1)}, u32[]{:S(2)}, u32[]{:S(2)}) collective-permute-start(f32[7,64,128]{2,1,0:T(8,128)S(1)} %get-tuple-element.54), channel_id=1, source_target_pairs={{0,224},{32,192},{64,32},{96,0},{128,96},{160,64},{192,160},{224,1... | collective-permute-start | bytes 688136 | tf_op jit(solution)/shard_map/ppermute | solution.py:639
  26.6 13.7 %copy-start = (s32[1,8,64]{2,1,0:T(8,128)S(1)}, s32[1,8,64]{2,1,0:T(8,128)}, u32[]{:S(2)}) copy-start(s32[1,8,64]{2,1,0:T(8,128)} %flag_ref.1) | copy-start | bytes 6148
  27.5 10.2 %collective-permute-start.8 = (f32[7,64,128]{2,1,0:T(8,128)S(1)}, f32[7,64,128]{2,1,0:T(8,128)S(1)}, u32[]{:S(2)}, u32[]{:S(2)}) collective-permute-start(f32[7,64,128]{2,1,0:T(8,128)S(1)} %get-tuple-element.56), channel_id=1, source_target_pairs={{0,32},{32,0},{64,96},{96,64},{128,160},{160,128},{192,224},{224,1... | collective-permute-start | bytes 688136 | tf_op jit(solution)/shard_map/ppermute | solution.py:664
  28.3 12.1 %collective-permute-start.9 = (f32[7,64,128]{2,1,0:T(8,128)S(1)}, f32[7,64,128]{2,1,0:T(8,128)S(1)}, u32[]{:S(2)}, u32[]{:S(2)}) collective-permute-start(f32[7,64,128]{2,1,0:T(8,128)S(1)} %get-tuple-element.57), channel_id=1, source_target_pairs={{0,64},{32,96},{64,128},{96,160},{128,192},{160,224},{192,0},{224,... | collective-permute-start | bytes 688136 | tf_op jit(solution)/shard_map/ppermute | solution.py:664
  30.3 6.0 %collective-permute-start = (f32[17,8,128]{2,1,0:T(8,128)S(1)}, f32[17,8,128]{2,1,0:T(8,128)S(1)}, u32[]{:S(2)}, u32[]{:S(2)}) collective-permute-start(f32[17,8,128]{2,1,0:T(8,128)S(1)} %get-tuple-element.41), channel_id=1, source_target_pairs={{0,1},{1,0},{2,3},{3,2},{4,5},{5,4},{6,7},{7,6},{8,9},{9,8},{10,11... | collective-permute-start | bytes 208904 | tf_op jit(solution)/shard_map/ppermute | solution.py:635
  32.9 13.0 %collective-permute-start.11 = (f32[7,64,128]{2,1,0:T(8,128)S(1)}, f32[7,64,128]{2,1,0:T(8,128)S(1)}, u32[]{:S(2)}, u32[]{:S(2)}) collective-permute-start(f32[7,64,128]{2,1,0:T(8,128)S(1)} %get-tuple-element.58), channel_id=1, source_target_pairs={{0,128},{32,160},{64,192},{96,224},{128,0},{160,32},{192,64},{224,... | collective-permute-start | bytes 688136 | tf_op jit(solution)/shard_map/ppermute | solution.py:664
  34.3 11.6 %collective-permute-start.12 = (f32[7,64,128]{2,1,0:T(8,128)S(1)}, f32[7,64,128]{2,1,0:T(8,128)S(1)}, u32[]{:S(2)}, u32[]{:S(2)}) collective-permute-start(f32[7,64,128]{2,1,0:T(8,128)S(1)} %get-tuple-element.59), channel_id=1, source_target_pairs={{0,160},{32,128},{64,224},{96,192},{128,32},{160,0},{192,96},{224,... | collective-permute-start | bytes 688136 | tf_op jit(solution)/shard_map/ppermute | solution.py:664
  36.3 17.8 %collective-permute-start.13 = (f32[7,64,128]{2,1,0:T(8,128)S(1)}, f32[7,64,128]{2,1,0:T(8,128)S(1)}, u32[]{:S(2)}, u32[]{:S(2)}) collective-permute-start(f32[7,64,128]{2,1,0:T(8,128)S(1)} %get-tuple-element.60), channel_id=1, source_target_pairs={{0,192},{32,224},{64,0},{96,32},{128,64},{160,96},{192,128},{224,1... | collective-permute-start | bytes 688136 | tf_op jit(solution)/shard_map/ppermute | solution.py:664
  37.7 16.4 %collective-permute-start.14 = (f32[7,64,128]{2,1,0:T(8,128)S(1)}, f32[7,64,128]{2,1,0:T(8,128)S(1)}, u32[]{:S(2)}, u32[]{:S(2)}) collective-permute-start(f32[7,64,128]{2,1,0:T(8,128)S(1)} %get-tuple-element.61), channel_id=1, source_target_pairs={{0,224},{32,192},{64,32},{96,0},{128,96},{160,64},{192,160},{224,1... | collective-permute-start | bytes 688136 | tf_op jit(solution)/shard_map/ppermute | solution.py:664
  40.3 13.8 %collective-permute-start.10 = (f32[7,64,128]{2,1,0:T(8,128)S(1)}, f32[7,64,128]{2,1,0:T(8,128)S(1)}, u32[]{:S(2)}, u32[]{:S(2)}) collective-permute-start(f32[7,64,128]{2,1,0:T(8,128)S(1)} %shard_map.32), channel_id=1, source_target_pairs={{0,96},{32,64},{64,160},{96,128},{128,224},{160,192},{192,32},{224... | collective-permute-start | bytes 688136 | tf_op jit(solution)/shard_map/ppermute | solution.py:664
  54.5 13.3 %collective-permute-start.15 = (f32[14,32,128]{2,1,0:T(8,128)S(1)}, f32[14,32,128]{2,1,0:T(8,128)S(1)}, u32[]{:S(2)}, u32[]{:S(2)}) collective-permute-start(f32[14,32,128]{2,1,0:T(8,128)S(1)} %get-tuple-element.64), channel_id=1, source_target_pairs={{0,2},{2,0},{4,6},{6,4},{8,10},{10,8},{12,14},{14,12},{16,18},{18,... | collective-permute-start | bytes 688136 | tf_op jit(solution)/shard_map/ppermute | solution.py:620
  56.8 1.3 %collective-permute-start.16 = (f32[5,32,128]{2,1,0:T(8,128)S(1)}, f32[5,32,128]{2,1,0:T(8,128)S(1)}, u32[]{:S(2)}, u32[]{:S(2)}) collective-permute-start(f32[5,32,128]{2,1,0:T(8,128)S(1)} %get-tuple-element.66), channel_id=1, source_target_pairs={{0,2},{2,0},{4,6},{6,4},{8,10},{10,8},{12,14},{14,12},{16,18},{18,... | collective-permute-start | bytes 245768 | tf_op jit(solution)/shard_map/ppermute | solution.py:620
  58.1 4.8 %collective-permute-start.17 = (f32[2,32,128]{2,1,0:T(8,128)S(1)}, f32[2,32,128]{2,1,0:T(8,128)S(1)}, u32[]{:S(2)}, u32[]{:S(2)}) collective-permute-start(f32[2,32,128]{2,1,0:T(8,128)S(1)} %get-tuple-element.69), channel_id=1, source_target_pairs={{4,0},{6,2},{8,4},{10,6},{12,8},{14,10},{16,12},{18,14},{20,16},{2... | collective-permute-start | bytes 98312 | tf_op jit(solution)/shard_map/ppermute | solution.py:624
  62.9 4.4 %collective-permute-start.18 = (f32[1,32,128]{2,1,0:T(8,128)S(1)}, f32[1,32,128]{2,1,0:T(8,128)S(1)}, u32[]{:S(2)}, u32[]{:S(2)}) collective-permute-start(f32[1,32,128]{2,1,0:T(8,128)S(1)} %get-tuple-element.71), channel_id=1, source_target_pairs={{0,4},{2,6},{4,8},{6,10},{8,12},{10,14},{12,16},{14,18},{16,20},{1... | collective-permute-start | bytes 49160 | tf_op jit(solution)/shard_map/ppermute | solution.py:624
  98.0 6.4 %collective-permute-start.19 = (f32[14,32,128]{2,1,0:T(8,128)S(1)}, f32[14,32,128]{2,1,0:T(8,128)S(1)}, u32[]{:S(2)}, u32[]{:S(2)}) collective-permute-start(f32[14,32,128]{2,1,0:T(8,128)S(1)} %get-tuple-element.74), channel_id=1, source_target_pairs={{0,2},{2,0},{4,6},{6,4},{8,10},{10,8},{12,14},{14,12},{16,18},{18,... | collective-permute-start | bytes 688136 | tf_op jit(solution)/shard_map/ppermute | solution.py:620
